TPU v7x, 256 devices: a whole 4x4x8 slice. The times are simulated.
256 devices in a mesh: tm: 8 (over z_hi, core), space: 32 (over z_lo, x, y).
Axes of the slice: x: 4, y: 4, z: 8 (z_hi: 4, z_lo: 2; z = z_hi * 2 + z_lo), core: 2. Of those that a mesh axis runs over, the one named last changes fastest.
Arguments:
- nodes: float32 [8, 3, 256, 128, 128], P('tm', None, 'space'), may hold values from -1 to 1
- mobility: float32 [256, 128, 128], P('space'), may hold values from 0.03 to 0.15
- reaction: float32 [256, 128, 128], P('space'), may hold values from 0.2 to 1.5
Outputs:
- updated: float32 [8, 3, 256, 128, 128], P('tm', None, 'space')
All inputs are finite; a program needn't handle non-finite values.
Results may differ from a plain program's by a relative error of at most 0.00002.
Values sent between devices are 32-bit elements; how exact they have to be, the bound alone decides.
No kernel may reach another device: no remote copies, remote signals or barrier semaphores. Data moves between devices by JAX's collectives and lax.ppermute only.
A program may use at most 64 MiB of HBM per device.

v0:
```python
import jax
import jax.numpy as jnp
from jax import lax
from jax.sharding import PartitionSpec as P

substep = 0.5
edge_weight = 5.0 / 24.0
middle_weight = 1.0 / 3.0
far_weight = -1.0 / 24.0


def padded_2(block, sides, width):
    for axis, dim in sides:
        count = lax.axis_size(axis)
        forward = [(i, i + 1) for i in range(count - 1)]
        forward.append((count - 1, 0))
        backward = [(target, source) for source, target in forward]
        low = lax.ppermute(
            lax.slice_in_dim(block, block.shape[dim] - width, None, axis=dim), axis, forward
        )
        high = lax.ppermute(lax.slice_in_dim(block, 0, width, axis=dim), axis, backward)
        block = jnp.concatenate([low, block, high], axis=dim)
    return block


def shifted(block, axis, distance):
    devices = range(lax.axis_size(axis))
    route = [((i - distance) % len(devices), i) for i in devices]
    return lax.ppermute(block, axis, route)


def shifted_2(block, axis, distance):
    devices = range(lax.axis_size(axis))
    route = [(i - distance, i) for i in devices if i - distance in devices]
    return lax.ppermute(block, axis, route)


def fine_force(field, mobility, reaction):
    padded = padded_2(field, (("space", 1),), 1)
    middle = padded[:, 1:-1]
    neighbours = padded[:, 2:] + padded[:, :-2]
    neighbours = neighbours + jnp.roll(middle, -1, 2) + jnp.roll(middle, 1, 2)
    neighbours = neighbours + jnp.roll(middle, -1, 3) + jnp.roll(middle, 1, 3)
    return mobility * (neighbours - 6.0 * middle) + reaction * (middle - middle * middle * middle)


def coarse_force(field, mob_coarse, rea_coarse):
    padded = padded_2(field, (("space", 1),), 1)
    middle = padded[:, 1:-1]
    planar = padded[:, 2:] + padded[:, :-2] + jnp.roll(middle, -1, 2) + jnp.roll(middle, 1, 2)
    vertical = jnp.roll(middle, -1, 3) + jnp.roll(middle, 1, 3)
    diffusion = 0.25 * (planar - 4.0 * middle) + (vertical - 2.0 * middle)
    return mob_coarse * diffusion + rea_coarse * (middle - middle * middle * middle)


def inner_force(padded, mob_part, rea_part):
    middle = padded[1:-1]
    planar = padded[2:] + padded[:-2] + jnp.roll(middle, -1, 1) + jnp.roll(middle, 1, 1)
    vertical = jnp.roll(middle, -1, 2) + jnp.roll(middle, 1, 2)
    diffusion = 0.25 * (planar - 4.0 * middle) + (vertical - 2.0 * middle)
    return mob_part * diffusion + rea_part * (middle - middle * middle * middle)


def wide_sweep(initial, margins):
    padded = padded_2(initial[None], (("space", 1),), 2)[0]
    first_force = inner_force(padded, margins[0][1:-1], margins[1][1:-1])
    level_wide = padded[1:-1] + substep * first_force + margins[2][1:-1]
    second_force = inner_force(level_wide, margins[0][2:-2], margins[1][2:-2])
    level_one = level_wide[1:-1]
    level_two = level_one + substep * second_force + margins[3][2:-2]
    return (level_one, level_two)


def integrals(first_force, second_force, third_force):
    leading = edge_weight * first_force + middle_weight * second_force + far_weight * third_force
    trailing = far_weight * first_force + middle_weight * second_force + edge_weight * third_force
    return (leading, trailing)


def restrict_second(values):
    evens = values[:, :, 0::2]
    odds = values[:, :, 1::2]
    return 0.5 * evens + 0.25 * (odds + jnp.roll(odds, 1, 2))


def restrict_first(values, left_plane):
    evens = values[:, 0::2]
    odds = values[:, 1::2]
    behind = jnp.concatenate([left_plane, odds[:, :-1]], 1)
    return 0.5 * evens + 0.25 * (odds + behind)


def prolong_second(values):
    upper = 0.5 * (values + jnp.roll(values, -1, 2))
    stacked = jnp.stack([values, upper], 3)
    return stacked.reshape((values.shape[0], values.shape[1], values.shape[2] * 2, values.shape[3]))


def body(nodes, mobility, reaction):
    states = nodes[0]
    mob_coarse = mobility[::2, ::2, :]
    rea_coarse = reaction[::2, ::2, :]
    old = fine_force(states, mobility, reaction)
    first, second = integrals(old[0], old[1], old[2])
    start = states[0]
    node_one = start + first
    force_one = fine_force(node_one[None], mobility, reaction)[0]
    node_two = node_one + substep * (force_one - old[1]) + second
    force_two = fine_force(node_two[None], mobility, reaction)[0]
    new_first, new_second = integrals(old[0], force_one, force_two)
    stacked = jnp.stack([start, node_one, node_two, new_first, new_second])
    last_plane = stacked[:, -1:]
    left_reduced = shifted(restrict_second(last_plane), "space", 1)
    restricted = restrict_first(restrict_second(stacked), left_reduced)
    coarse = restricted[:3]
    coarse_old = coarse_force(coarse, mob_coarse, rea_coarse)
    terms = restricted[3:] - substep * coarse_old[:2]
    slice_index = lax.axis_index("tm")
    slices = lax.axis_size("tm")
    own_start = coarse[0]
    bundle = jnp.stack([mob_coarse, rea_coarse, terms[0], terms[1]])
    margins = padded_2(bundle, (("space", 1),), 2)

    def sweep_once(initial):
        return wide_sweep(initial, margins)

    def wide_turn(turn_index, initial):
        level_one, level_two = sweep_once(initial)
        arrived = shifted_2(level_two, "tm", 1)
        return jnp.where(slice_index == 0, own_start, arrived)

    initial = lax.fori_loop(0, slices - 1, wide_turn, own_start)
    level_one, level_two = sweep_once(initial)
    difference = jnp.stack([level_one, level_two]) - coarse[1:]
    widened = prolong_second(difference)
    right_plane = shifted(widened[:, :1], "space", -1)
    following = jnp.concatenate([widened[:, 1:], right_plane], 1)
    upper = 0.5 * (widened + following)
    alternated = jnp.stack([widened, upper], 2)
    correction = alternated.reshape(
        (widened.shape[0], widened.shape[1] * 2, widened.shape[2], widened.shape[3])
    )
    corrected = jnp.stack([node_one, node_two]) + correction
    arrived_end = shifted_2(corrected[1], "tm", 1)
    head = jnp.where(slice_index == 0, start, arrived_end)
    return jnp.stack([head, corrected[0], corrected[1]])[None]


def solution(mesh):
    return jax.shard_map(
        body,
        mesh=mesh,
        in_specs=(
            P("tm", None, "space", None, None),
            P("space", None, None),
            P("space", None, None),
        ),
        out_specs=P("tm", None, "space", None, None),
        check_vma=False,
    )
```

profile of v0, /device:TPU:190, one launch (start us, length us, event | category | flops | bytes accessed | tf_op | source)
XLA Modules:
  0.0 297.4 jit_solution(18386203026374967826)
XLA Ops:
  22.9 6.2 %collective-permute-start.6 = (f32[1,1,128,128]{3,2,1,0:T(8,128)S(1)}, f32[1,1,128,128]{3,2,1,0:T(8,128)S(1)}, u32[]{:S(2)}, u32[]{:S(2)}) collective-permute-start(f32[1,1,128,128]{3,2,1,0:T(8,128)S(1)} %get-tuple-element.136), channel_id=1, source_target_pairs={{0,1},{1,2},{2,3},{3,4},{4,5},{5,6},{6,7},{7,8},{8,9},{9,10},{10,1... | collective-permute-start | bytes 196616 | tf_op jit(solution)/shard_map/ppermute | solution.py:18
  32.9 6.3 %collective-permute-start.8 = (f32[1,1,128,128]{3,2,1,0:T(8,128)S(1)}, f32[1,1,128,128]{3,2,1,0:T(8,128)S(1)}, u32[]{:S(2)}, u32[]{:S(2)}) collective-permute-start(f32[1,1,128,128]{3,2,1,0:T(8,128)S(1)} %get-tuple-element.126), channel_id=1, source_target_pairs={{0,1},{1,2},{2,3},{3,4},{4,5},{5,6},{6,7},{7,8},{8,9},{9,10},{10,1... | collective-permute-start | bytes 196616 | tf_op jit(solution)/shard_map/ppermute | solution.py:18
  44.2 6.5 %slice.668 = f32[5,8,64,128]{3,2,1,0:T(8,128)} slice(f32[5,8,128,128]{3,2,1,0:T(8,128)} %copy-done.7), slice={[0:5:1], [0:8:1], [1:128:2], [0:128:1]} | slice | bytes 2621440 | tf_op jit(solution)/shard_map/slice | solution.py:82
  50.7 6.5 %slice.667 = f32[5,8,64,128]{3,2,1,0:T(8,128)} slice(f32[5,8,128,128]{3,2,1,0:T(8,128)} %copy-done.7), slice={[0:5:1], [0:8:1], [0:128:2], [0:128:1]} | slice | bytes 2621440 | tf_op jit(solution)/shard_map/slice | solution.py:81
  57.3 6.6 %collective-permute-start.9 = (f32[5,1,64,128]{3,2,1,0:T(8,128)S(1)}, f32[5,1,64,128]{3,2,1,0:T(8,128)S(1)}, u32[]{:S(2)}, u32[]{:S(2)}) collective-permute-start(f32[5,1,64,128]{3,2,1,0:T(8,128)S(1)} %fusion.92), channel_id=1, source_target_pairs={{31,0},{0,1},{1,2},{2,3},{3,4},{4,5},{5,6},{6,7},{7,8},{8,9},{9,10... | collective-permute-start | bytes 491528 | tf_op jit(solution)/shard_map/ppermute | solution.py:29
  68.1 6.2 %collective-permute-start.11 = (f32[3,1,64,128]{3,2,1,0:T(8,128)S(1)}, f32[3,1,64,128]{3,2,1,0:T(8,128)S(1)}, u32[]{:S(2)}, u32[]{:S(2)}) collective-permute-start(f32[3,1,64,128]{3,2,1,0:T(8,128)S(1)} %get-tuple-element.118), channel_id=1, source_target_pairs={{0,1},{1,2},{2,3},{3,4},{4,5},{5,6},{6,7},{7,8},{8,9},{9,10},{10,1... | collective-permute-start | bytes 294920 | tf_op jit(solution)/shard_map/ppermute | solution.py:18
  78.9 6.2 %collective-permute-start.12 = (f32[4,2,64,128]{3,2,1,0:T(8,128)}, f32[4,2,64,128]{3,2,1,0:T(8,128)}, u32[]{:S(2)}, u32[]{:S(2)}) collective-permute-start(f32[4,2,64,128]{3,2,1,0:T(8,128)} %get-tuple-element.123), channel_id=1, source_target_pairs={{0,1},{1,2},{2,3},{3,4},{4,5},{5,6},{6,7},{7,8},{8,9},{9,10},{10,1... | collective-permute-start | bytes 786440 | tf_op jit(solution)/shard_map/ppermute | solution.py:18
  89.3 6.7 %collective-permute-done.13 = f32[4,2,64,128]{3,2,1,0:T(8,128)} collective-permute-done((f32[4,2,64,128]{3,2,1,0:T(8,128)}, f32[4,2,64,128]{3,2,1,0:T(8,128)}, u32[]{:S(2)}, u32[]{:S(2)}) %collective-permute-start.13) | collective-permute-done | bytes 262176 | tf_op jit(solution)/shard_map/ppermute | solution.py:21
  98.3 152.7 %while.12 = (s32[]{:T(128)}, f32[4,64,128]{2,1,0:T(8,128)S(1)}, pred[]{:T(512)}, f32[4,8,64,128]{3,2,1,0:T(8,128)}, f32[4,64,128]{2,1,0:T(8,128)S(1)}, /*index=5*/s32[]{:T(128)}) while((s32[]{:T(128)}, f32[4,64,128]{2,1,0:T(8,128)S(1)}, pred[]{:T(512)}, f32[4,8,64,128]{3,2,1,0:T(8,128)}, f32[4,64,128]{2,1,0:T(8,128)S(1)}, ...), condition=%wide.region_1.2_spmd, body=%wide.region_0.1_spmd.sunk | while | flops 2211842 | bytes 12779766 | solution.py:132
  98.4 6.2 %collective-permute-start.1 = (f32[1,2,64,128]{3,2,1,0:T(8,128)S(1)}, f32[1,2,64,128]{3,2,1,0:T(8,128)S(1)}, u32[]{:S(2)}, u32[]{:S(2)}) collective-permute-start(f32[1,2,64,128]{3,2,1,0:T(8,128)S(1)} %get-tuple-element.215), channel_id=1, source_target_pairs={{0,1},{1,2},{2,3},{3,4},{4,5},{5,6},{6,7},{7,8},{8,9},{9,10},{10,1... | collective-permute-start | bytes 196616 | tf_op jit(solution)/shard_map/while/body/eval_jaxpr/ppermute | solution.py:18
  110.4 8.1 %collective-permute-done.2 = f32[4,64,128]{2,1,0:T(8,128)S(1)} collective-permute-done((f32[4,64,128]{2,1,0:T(8,128)}, f32[4,64,128]{2,1,0:T(8,128)S(1)}, u32[]{:S(2)}, u32[]{:S(2)}) %collective-permute-start.2) | collective-permute-done | bytes 131104 | tf_op jit(solution)/shard_map/while/body/eval_jaxpr/ppermute | solution.py:35
  120.2 6.2 %collective-permute-start.1 = (f32[1,2,64,128]{3,2,1,0:T(8,128)S(1)}, f32[1,2,64,128]{3,2,1,0:T(8,128)S(1)}, u32[]{:S(2)}, u32[]{:S(2)}) collective-permute-start(f32[1,2,64,128]{3,2,1,0:T(8,128)S(1)} %get-tuple-element.215), channel_id=1, source_target_pairs={{0,1},{1,2},{2,3},{3,4},{4,5},{5,6},{6,7},{7,8},{8,9},{9,10},{10,1... | collective-permute-start | bytes 196616 | tf_op jit(solution)/shard_map/while/body/eval_jaxpr/ppermute | solution.py:18
  132.2 8.1 %collective-permute-done.2 = f32[4,64,128]{2,1,0:T(8,128)S(1)} collective-permute-done((f32[4,64,128]{2,1,0:T(8,128)}, f32[4,64,128]{2,1,0:T(8,128)S(1)}, u32[]{:S(2)}, u32[]{:S(2)}) %collective-permute-start.2) | collective-permute-done | bytes 131104 | tf_op jit(solution)/shard_map/while/body/eval_jaxpr/ppermute | solution.py:35
  142.0 6.2 %collective-permute-start.1 = (f32[1,2,64,128]{3,2,1,0:T(8,128)S(1)}, f32[1,2,64,128]{3,2,1,0:T(8,128)S(1)}, u32[]{:S(2)}, u32[]{:S(2)}) collective-permute-start(f32[1,2,64,128]{3,2,1,0:T(8,128)S(1)} %get-tuple-element.215), channel_id=1, source_target_pairs={{0,1},{1,2},{2,3},{3,4},{4,5},{5,6},{6,7},{7,8},{8,9},{9,10},{10,1... | collective-permute-start | bytes 196616 | tf_op jit(solution)/shard_map/while/body/eval_jaxpr/ppermute | solution.py:18
  154.1 8.1 %collective-permute-done.2 = f32[4,64,128]{2,1,0:T(8,128)S(1)} collective-permute-done((f32[4,64,128]{2,1,0:T(8,128)}, f32[4,64,128]{2,1,0:T(8,128)S(1)}, u32[]{:S(2)}, u32[]{:S(2)}) %collective-permute-start.2) | collective-permute-done | bytes 131104 | tf_op jit(solution)/shard_map/while/body/eval_jaxpr/ppermute | solution.py:35
  163.8 6.2 %collective-permute-start.1 = (f32[1,2,64,128]{3,2,1,0:T(8,128)S(1)}, f32[1,2,64,128]{3,2,1,0:T(8,128)S(1)}, u32[]{:S(2)}, u32[]{:S(2)}) collective-permute-start(f32[1,2,64,128]{3,2,1,0:T(8,128)S(1)} %get-tuple-element.215), channel_id=1, source_target_pairs={{0,1},{1,2},{2,3},{3,4},{4,5},{5,6},{6,7},{7,8},{8,9},{9,10},{10,1... | collective-permute-start | bytes 196616 | tf_op jit(solution)/shard_map/while/body/eval_jaxpr/ppermute | solution.py:18
  175.9 8.1 %collective-permute-done.2 = f32[4,64,128]{2,1,0:T(8,128)S(1)} collective-permute-done((f32[4,64,128]{2,1,0:T(8,128)}, f32[4,64,128]{2,1,0:T(8,128)S(1)}, u32[]{:S(2)}, u32[]{:S(2)}) %collective-permute-start.2) | collective-permute-done | bytes 131104 | tf_op jit(solution)/shard_map/while/body/eval_jaxpr/ppermute | solution.py:35
  185.7 6.2 %collective-permute-start.1 = (f32[1,2,64,128]{3,2,1,0:T(8,128)S(1)}, f32[1,2,64,128]{3,2,1,0:T(8,128)S(1)}, u32[]{:S(2)}, u32[]{:S(2)}) collective-permute-start(f32[1,2,64,128]{3,2,1,0:T(8,128)S(1)} %get-tuple-element.215), channel_id=1, source_target_pairs={{0,1},{1,2},{2,3},{3,4},{4,5},{5,6},{6,7},{7,8},{8,9},{9,10},{10,1... | collective-permute-start | bytes 196616 | tf_op jit(solution)/shard_map/while/body/eval_jaxpr/ppermute | solution.py:18
  197.7 8.1 %collective-permute-done.2 = f32[4,64,128]{2,1,0:T(8,128)S(1)} collective-permute-done((f32[4,64,128]{2,1,0:T(8,128)}, f32[4,64,128]{2,1,0:T(8,128)S(1)}, u32[]{:S(2)}, u32[]{:S(2)}) %collective-permute-start.2) | collective-permute-done | bytes 131104 | tf_op jit(solution)/shard_map/while/body/eval_jaxpr/ppermute | solution.py:35
  219.5 8.1 %collective-permute-done.2 = f32[4,64,128]{2,1,0:T(8,128)S(1)} collective-permute-done((f32[4,64,128]{2,1,0:T(8,128)}, f32[4,64,128]{2,1,0:T(8,128)S(1)}, u32[]{:S(2)}, u32[]{:S(2)}) %collective-permute-start.2) | collective-permute-done | bytes 131104 | tf_op jit(solution)/shard_map/while/body/eval_jaxpr/ppermute | solution.py:35
  241.3 8.1 %collective-permute-done.2 = f32[4,64,128]{2,1,0:T(8,128)S(1)} collective-permute-done((f32[4,64,128]{2,1,0:T(8,128)}, f32[4,64,128]{2,1,0:T(8,128)S(1)}, u32[]{:S(2)}, u32[]{:S(2)}) %collective-permute-start.2) | collective-permute-done | bytes 131104 | tf_op jit(solution)/shard_map/while/body/eval_jaxpr/ppermute | solution.py:35
  257.9 6.6 %collective-permute-done.15 = f32[1,2,64,128]{3,2,1,0:T(8,128)S(1)} collective-permute-done((f32[1,2,64,128]{3,2,1,0:T(8,128)S(1)}, f32[1,2,64,128]{3,2,1,0:T(8,128)S(1)}, u32[]{:S(2)}, u32[]{:S(2)}) %collective-permute-start.15) | collective-permute-done | bytes 65568 | tf_op jit(solution)/shard_map/ppermute | solution.py:21
  266.8 10.6 %collective-permute-done.16 = f32[2,1,128,128]{3,2,0,1:T(8,128)S(1)} collective-permute-done((f32[2,1,128,128]{3,2,0,1:T(8,128)S(1)}, f32[2,1,128,128]{3,2,0,1:T(8,128)S(1)}, u32[]{:S(2)}, u32[]{:S(2)}) %collective-permute-start.16) | collective-permute-done | bytes 131104 | tf_op jit(solution)/shard_map/ppermute | solution.py:29
  279.8 16.3 %collective-permute-done.17 = f32[8,128,128]{2,1,0:T(8,128)S(1)} collective-permute-done((f32[8,128,128]{2,1,0:T(8,128)S(1)}, f32[8,128,128]{2,1,0:T(8,128)S(1)}, u32[]{:S(2)}, u32[]{:S(2)}) %collective-permute-start.17) | collective-permute-done | bytes 524320 | tf_op jit(solution)/shard_map/ppermute | solution.py:35
  (270 shorter events, 123.4 us)
Async XLA Ops:
  1.1 16.0 %collective-permute-start.3 = (f32[3,1,128,128]{3,2,1,0:T(8,128)S(1)}, f32[3,1,128,128]{3,2,1,0:T(8,128)}, u32[]{:S(2)}, u32[]{:S(2)}) collective-permute-start(f32[3,1,128,128]{3,2,1,0:T(8,128)S(1)} %get-tuple-element.111), channel_id=1, source_target_pairs={{1,0},{2,1},{3,2},{4,3},{5,4},{6,5},{7,6},{8,7},{9,8},{10,9},{11,1... | collective-permute-start | bytes 589832 | tf_op jit(solution)/shard_map/ppermute | solution.py:21
  1.9 15.1 %collective-permute-start.4 = (f32[3,1,128,128]{3,2,1,0:T(8,128)S(1)}, f32[3,1,128,128]{3,2,1,0:T(8,128)}, u32[]{:S(2)}, u32[]{:S(2)}) collective-permute-start(f32[3,1,128,128]{3,2,1,0:T(8,128)S(1)} %get-tuple-element.112), channel_id=1, source_target_pairs={{0,1},{1,2},{2,3},{3,4},{4,5},{5,6},{6,7},{7,8},{8,9},{9,10},{10,1... | collective-permute-start | bytes 589832 | tf_op jit(solution)/shard_map/ppermute | solution.py:18
  22.8 8.6 %collective-permute-start.5 = (f32[1,1,128,128]{3,2,1,0:T(8,128)S(1)}, f32[1,1,128,128]{3,2,1,0:T(8,128)S(1)}, u32[]{:S(2)}, u32[]{:S(2)}) collective-permute-start(f32[1,1,128,128]{3,2,1,0:T(8,128)S(1)} %get-tuple-element.135), channel_id=1, source_target_pairs={{1,0},{2,1},{3,2},{4,3},{5,4},{6,5},{7,6},{8,7},{9,8},{10,9},{11,1... | collective-permute-start | bytes 196616 | tf_op jit(solution)/shard_map/ppermute | solution.py:21
  32.8 8.6 %collective-permute-start.7 = (f32[1,1,128,128]{3,2,1,0:T(8,128)S(1)}, f32[1,1,128,128]{3,2,1,0:T(8,128)S(1)}, u32[]{:S(2)}, u32[]{:S(2)}) collective-permute-start(f32[1,1,128,128]{3,2,1,0:T(8,128)S(1)} %get-tuple-element.125), channel_id=1, source_target_pairs={{1,0},{2,1},{3,2},{4,3},{5,4},{6,5},{7,6},{8,7},{9,8},{10,9},{11,1... | collective-permute-start | bytes 196616 | tf_op jit(solution)/shard_map/ppermute | solution.py:21
  57.3 10.1 %collective-permute-start.9 = (f32[5,1,64,128]{3,2,1,0:T(8,128)S(1)}, f32[5,1,64,128]{3,2,1,0:T(8,128)S(1)}, u32[]{:S(2)}, u32[]{:S(2)}) collective-permute-start(f32[5,1,64,128]{3,2,1,0:T(8,128)S(1)} %fusion.92), channel_id=1, source_target_pairs={{31,0},{0,1},{1,2},{2,3},{3,4},{4,5},{5,6},{6,7},{7,8},{8,9},{9,10... | collective-permute-start | bytes 491528 | tf_op jit(solution)/shard_map/ppermute | solution.py:29
  68.0 8.9 %collective-permute-start.10 = (f32[3,1,64,128]{3,2,1,0:T(8,128)S(1)}, f32[3,1,64,128]{3,2,1,0:T(8,128)S(1)}, u32[]{:S(2)}, u32[]{:S(2)}) collective-permute-start(f32[3,1,64,128]{3,2,1,0:T(8,128)S(1)} %get-tuple-element.117), channel_id=1, source_target_pairs={{1,0},{2,1},{3,2},{4,3},{5,4},{6,5},{7,6},{8,7},{9,8},{10,9},{11,1... | collective-permute-start | bytes 294920 | tf_op jit(solution)/shard_map/ppermute | solution.py:21
  68.1 8.8 %collective-permute-start.11 = (f32[3,1,64,128]{3,2,1,0:T(8,128)S(1)}, f32[3,1,64,128]{3,2,1,0:T(8,128)S(1)}, u32[]{:S(2)}, u32[]{:S(2)}) collective-permute-start(f32[3,1,64,128]{3,2,1,0:T(8,128)S(1)} %get-tuple-element.118), channel_id=1, source_target_pairs={{0,1},{1,2},{2,3},{3,4},{4,5},{5,6},{6,7},{7,8},{8,9},{9,10},{10,1... | collective-permute-start | bytes 294920 | tf_op jit(solution)/shard_map/ppermute | solution.py:18
  78.9 10.4 %collective-permute-start.12 = (f32[4,2,64,128]{3,2,1,0:T(8,128)}, f32[4,2,64,128]{3,2,1,0:T(8,128)}, u32[]{:S(2)}, u32[]{:S(2)}) collective-permute-start(f32[4,2,64,128]{3,2,1,0:T(8,128)} %get-tuple-element.123), channel_id=1, source_target_pairs={{0,1},{1,2},{2,3},{3,4},{4,5},{5,6},{6,7},{7,8},{8,9},{9,10},{10,1... | collective-permute-start | bytes 786440 | tf_op jit(solution)/shard_map/ppermute | solution.py:18
  85.1 10.9 %collective-permute-start.13 = (f32[4,2,64,128]{3,2,1,0:T(8,128)}, f32[4,2,64,128]{3,2,1,0:T(8,128)}, u32[]{:S(2)}, u32[]{:S(2)}) collective-permute-start(f32[4,2,64,128]{3,2,1,0:T(8,128)} %get-tuple-element.124), channel_id=1, source_target_pairs={{1,0},{2,1},{3,2},{4,3},{5,4},{6,5},{7,6},{8,7},{9,8},{10,9},{11,1... | collective-permute-start | bytes 786440 | tf_op jit(solution)/shard_map/ppermute | solution.py:21
  98.3 8.6 %collective-permute-start = (f32[1,2,64,128]{3,2,1,0:T(8,128)S(1)}, f32[1,2,64,128]{3,2,1,0:T(8,128)S(1)}, u32[]{:S(2)}, u32[]{:S(2)}) collective-permute-start(f32[1,2,64,128]{3,2,1,0:T(8,128)S(1)} %get-tuple-element.214), channel_id=1, source_target_pairs={{1,0},{2,1},{3,2},{4,3},{5,4},{6,5},{7,6},{8,7},{9,8},{10,9},{11,1... | collective-permute-start | bytes 196616 | tf_op jit(solution)/shard_map/while/body/eval_jaxpr/ppermute | solution.py:21
  108.5 10.0 %collective-permute-start.2 = (f32[4,64,128]{2,1,0:T(8,128)}, f32[4,64,128]{2,1,0:T(8,128)S(1)}, u32[]{:S(2)}, u32[]{:S(2)}) collective-permute-start(f32[4,64,128]{2,1,0:T(8,128)} %fusion.171), channel_id=1, source_target_pairs={{0,32},{32,64},{64,96},{96,128},{128,160},{160,192},{192,224},{1,3... | collective-permute-start | bytes 393224 | tf_op jit(solution)/shard_map/while/body/eval_jaxpr/ppermute | solution.py:35
  120.1 8.6 %collective-permute-start = (f32[1,2,64,128]{3,2,1,0:T(8,128)S(1)}, f32[1,2,64,128]{3,2,1,0:T(8,128)S(1)}, u32[]{:S(2)}, u32[]{:S(2)}) collective-permute-start(f32[1,2,64,128]{3,2,1,0:T(8,128)S(1)} %get-tuple-element.214), channel_id=1, source_target_pairs={{1,0},{2,1},{3,2},{4,3},{5,4},{6,5},{7,6},{8,7},{9,8},{10,9},{11,1... | collective-permute-start | bytes 196616 | tf_op jit(solution)/shard_map/while/body/eval_jaxpr/ppermute | solution.py:21
  130.3 10.0 %collective-permute-start.2 = (f32[4,64,128]{2,1,0:T(8,128)}, f32[4,64,128]{2,1,0:T(8,128)S(1)}, u32[]{:S(2)}, u32[]{:S(2)}) collective-permute-start(f32[4,64,128]{2,1,0:T(8,128)} %fusion.171), channel_id=1, source_target_pairs={{0,32},{32,64},{64,96},{96,128},{128,160},{160,192},{192,224},{1,3... | collective-permute-start | bytes 393224 | tf_op jit(solution)/shard_map/while/body/eval_jaxpr/ppermute | solution.py:35
  141.9 8.6 %collective-permute-start = (f32[1,2,64,128]{3,2,1,0:T(8,128)S(1)}, f32[1,2,64,128]{3,2,1,0:T(8,128)S(1)}, u32[]{:S(2)}, u32[]{:S(2)}) collective-permute-start(f32[1,2,64,128]{3,2,1,0:T(8,128)S(1)} %get-tuple-element.214), channel_id=1, source_target_pairs={{1,0},{2,1},{3,2},{4,3},{5,4},{6,5},{7,6},{8,7},{9,8},{10,9},{11,1... | collective-permute-start | bytes 196616 | tf_op jit(solution)/shard_map/while/body/eval_jaxpr/ppermute | solution.py:21
  152.1 10.0 %collective-permute-start.2 = (f32[4,64,128]{2,1,0:T(8,128)}, f32[4,64,128]{2,1,0:T(8,128)S(1)}, u32[]{:S(2)}, u32[]{:S(2)}) collective-permute-start(f32[4,64,128]{2,1,0:T(8,128)} %fusion.171), channel_id=1, source_target_pairs={{0,32},{32,64},{64,96},{96,128},{128,160},{160,192},{192,224},{1,3... | collective-permute-start | bytes 393224 | tf_op jit(solution)/shard_map/while/body/eval_jaxpr/ppermute | solution.py:35
  163.8 8.6 %collective-permute-start = (f32[1,2,64,128]{3,2,1,0:T(8,128)S(1)}, f32[1,2,64,128]{3,2,1,0:T(8,128)S(1)}, u32[]{:S(2)}, u32[]{:S(2)}) collective-permute-start(f32[1,2,64,128]{3,2,1,0:T(8,128)S(1)} %get-tuple-element.214), channel_id=1, source_target_pairs={{1,0},{2,1},{3,2},{4,3},{5,4},{6,5},{7,6},{8,7},{9,8},{10,9},{11,1... | collective-permute-start | bytes 196616 | tf_op jit(solution)/shard_map/while/body/eval_jaxpr/ppermute | solution.py:21
  174.0 10.0 %collective-permute-start.2 = (f32[4,64,128]{2,1,0:T(8,128)}, f32[4,64,128]{2,1,0:T(8,128)S(1)}, u32[]{:S(2)}, u32[]{:S(2)}) collective-permute-start(f32[4,64,128]{2,1,0:T(8,128)} %fusion.171), channel_id=1, source_target_pairs={{0,32},{32,64},{64,96},{96,128},{128,160},{160,192},{192,224},{1,3... | collective-permute-start | bytes 393224 | tf_op jit(solution)/shard_map/while/body/eval_jaxpr/ppermute | solution.py:35
  185.6 8.6 %collective-permute-start = (f32[1,2,64,128]{3,2,1,0:T(8,128)S(1)}, f32[1,2,64,128]{3,2,1,0:T(8,128)S(1)}, u32[]{:S(2)}, u32[]{:S(2)}) collective-permute-start(f32[1,2,64,128]{3,2,1,0:T(8,128)S(1)} %get-tuple-element.214), channel_id=1, source_target_pairs={{1,0},{2,1},{3,2},{4,3},{5,4},{6,5},{7,6},{8,7},{9,8},{10,9},{11,1... | collective-permute-start | bytes 196616 | tf_op jit(solution)/shard_map/while/body/eval_jaxpr/ppermute | solution.py:21
  195.8 10.0 %collective-permute-start.2 = (f32[4,64,128]{2,1,0:T(8,128)}, f32[4,64,128]{2,1,0:T(8,128)S(1)}, u32[]{:S(2)}, u32[]{:S(2)}) collective-permute-start(f32[4,64,128]{2,1,0:T(8,128)} %fusion.171), channel_id=1, source_target_pairs={{0,32},{32,64},{64,96},{96,128},{128,160},{160,192},{192,224},{1,3... | collective-permute-start | bytes 393224 | tf_op jit(solution)/shard_map/while/body/eval_jaxpr/ppermute | solution.py:35
  207.4 8.6 %collective-permute-start = (f32[1,2,64,128]{3,2,1,0:T(8,128)S(1)}, f32[1,2,64,128]{3,2,1,0:T(8,128)S(1)}, u32[]{:S(2)}, u32[]{:S(2)}) collective-permute-start(f32[1,2,64,128]{3,2,1,0:T(8,128)S(1)} %get-tuple-element.214), channel_id=1, source_target_pairs={{1,0},{2,1},{3,2},{4,3},{5,4},{6,5},{7,6},{8,7},{9,8},{10,9},{11,1... | collective-permute-start | bytes 196616 | tf_op jit(solution)/shard_map/while/body/eval_jaxpr/ppermute | solution.py:21
  217.6 10.0 %collective-permute-start.2 = (f32[4,64,128]{2,1,0:T(8,128)}, f32[4,64,128]{2,1,0:T(8,128)S(1)}, u32[]{:S(2)}, u32[]{:S(2)}) collective-permute-start(f32[4,64,128]{2,1,0:T(8,128)} %fusion.171), channel_id=1, source_target_pairs={{0,32},{32,64},{64,96},{96,128},{128,160},{160,192},{192,224},{1,3... | collective-permute-start | bytes 393224 | tf_op jit(solution)/shard_map/while/body/eval_jaxpr/ppermute | solution.py:35
  239.4 10.0 %collective-permute-start.2 = (f32[4,64,128]{2,1,0:T(8,128)}, f32[4,64,128]{2,1,0:T(8,128)S(1)}, u32[]{:S(2)}, u32[]{:S(2)}) collective-permute-start(f32[4,64,128]{2,1,0:T(8,128)} %fusion.171), channel_id=1, source_target_pairs={{0,32},{32,64},{64,96},{96,128},{128,160},{160,192},{192,224},{1,3... | collective-permute-start | bytes 393224 | tf_op jit(solution)/shard_map/while/body/eval_jaxpr/ppermute | solution.py:35
  266.7 10.7 %collective-permute-start.16 = (f32[2,1,128,128]{3,2,0,1:T(8,128)S(1)}, f32[2,1,128,128]{3,2,0,1:T(8,128)S(1)}, u32[]{:S(2)}, u32[]{:S(2)}) collective-permute-start(f32[2,1,128,128]{3,2,0,1:T(8,128)S(1)} %slice_bitcast_fusion.5), channel_id=1, source_target_pairs={{1,0},{2,1},{3,2},{4,3},{5,4},{6,5},{7,6},{8,7},{9,8},{10,9},{11,1... | collective-permute-start | bytes 393224 | tf_op jit(solution)/shard_map/ppermute | solution.py:29
  277.9 18.2 %collective-permute-start.17 = (f32[8,128,128]{2,1,0:T(8,128)S(1)}, f32[8,128,128]{2,1,0:T(8,128)S(1)}, u32[]{:S(2)}, u32[]{:S(2)}) collective-permute-start(f32[8,128,128]{2,1,0:T(8,128)S(1)} %slice_bitcast_fusion), channel_id=1, source_target_pairs={{0,32},{32,64},{64,96},{96,128},{128,160},{160,192},{192,224},{1,3... | collective-permute-start | bytes 1572872 | tf_op jit(solution)/shard_map/ppermute | solution.py:35
  (39 other events, 336.3 us)
where the time goes:
time: 298 us; the launch traced here: 297 us
  waiting for transfers between devices  125 us (42%)
  starting transfers between devices  103 us (35%)
  local copies, waits for them, and re-layouts  39 us (13%)
  other arithmetic  28.8 us (10%)
    ppermute x13, starting transfers between devices, padded_2(): lax.ppermute(lax.slice_in_dim(block, block.shape[dim] - width, None, axis...  79.1 us
    ppermute x8, waiting for transfers between devices, shifted_2(): return lax.ppermute(block, axis, route)  72.9 us
    ppermute x13, waiting for transfers between devices, padded_2(): lax.ppermute(lax.slice_in_dim(block, 0, width, axis=dim), axis, backward)  35.9 us
    ppermute x8, starting transfers between devices, shifted_2(): return lax.ppermute(block, axis, route)  15.3 us
    ppermute x2, waiting for transfers between devices, shifted(): return lax.ppermute(block, axis, route)  10.6 us
    slice x6, local copies, waits for them, and re-layouts, fine_force(): neighbours = neighbours + jnp.roll(middle, -1, 3) + jnp.roll(middle, 1, 3)  7.27 us
    ppermute x2, starting transfers between devices, shifted(): return lax.ppermute(block, axis, route)  6.67 us
    slice x2, local copies, waits for them, and re-layouts, restrict_second(): odds = values[:, :, 1::2]  6.64 us
  transfers between devices with their start and end apart: 36, of which 23 were waited for; matrix products, arithmetic and copies ran while one was open for 4% of the time, Pallas kernels for 0%

commit v1 on v0

v1 whole, which is shorter than its diff:
```python
import functools
import jax
import jax.numpy as jnp
from jax import lax
from jax.experimental import pallas as pl
from jax.experimental.pallas import tpu as pltpu
from jax.sharding import PartitionSpec as P

edge = 5.0 / 24.0
middle = 1.0 / 3.0
far = -1.0 / 24.0
substep = 0.5

VMEM = pltpu.CompilerParams(vmem_limit_bytes=40 * 1024 * 1024)


def roll(values, amount, axis):
    return pltpu.roll(values, amount % values.shape[axis], axis)


def around(values):
    return roll(values, 1, 0) + roll(values, -1, 0) + roll(values, 1, 1) + roll(values, -1, 1)


def cubic(values):
    return values - values * values * values


def cost(flops, moved):
    return pl.CostEstimate(flops=flops, bytes_accessed=moved, transcendentals=0)


def ring(values, axis, distance):
    count = lax.axis_size(axis)
    return lax.ppermute(values, axis, [(i, (i + distance) % count) for i in range(count)])


def swapped(values):
    count = lax.axis_size("tm")
    return lax.ppermute(values, "tm", [(i, i ^ 1) for i in range(count)])


def call(kernel, outs, scratch, *args, flops=10**6, scalars=0):
    moved = sum(a.size * 4 for a in args) + sum(4 * functools.reduce(lambda x, y: x * y, s) for s in outs)
    result = pl.pallas_call(
        kernel,
        out_shape=[jax.ShapeDtypeStruct(s, jnp.float32) for s in outs],
        in_specs=[pl.BlockSpec(memory_space=pltpu.SMEM)] * scalars
        + [pl.BlockSpec(memory_space=pltpu.VMEM)] * (len(args) - scalars),
        out_specs=[pl.BlockSpec(memory_space=pltpu.VMEM) for _ in outs],
        scratch_shapes=[pltpu.VMEM(s, jnp.float32) for s in scratch],
        compiler_params=VMEM,
        cost_estimate=cost(flops, moved),
    )(*args)
    return result


def coefficient_kernel(mob, rea, own, rightward, leftward):
    half = mob.shape[1] // 2
    for plane in range(4):
        m = 0.125 * mob[2 * plane, pl.ds(0, half, stride=2), :]
        r = 0.5 * rea[2 * plane, pl.ds(0, half, stride=2), :]
        own[0, plane] = m
        own[1, plane] = r
        leftward[0, plane] = m
        leftward[1, plane] = r
        if plane > 0:
            rightward[0, plane - 1] = m
            rightward[1, plane - 1] = r


def fine_kernel(
    nodes, mob, rea, left, right,
    v1_out, v2_out, coarse, terms, rightward, leftward,
    u, mw, rw, ca, cb, v1, v2, step, f1, jj, mix,
):
    half = mob.shape[1] // 2
    for m in range(3):
        for i in range(3):
            u[m, i] = left[3 * m + i]
            u[m, 11 + i] = right[3 * m + i]
    for i in range(2):
        mw[i] = left[9 + i]
        mw[10 + i] = right[9 + i]
        rw[i] = left[11 + i]
        rw[10 + i] = right[11 + i]

    @pl.loop(0, 8)
    def _(i):
        for m in range(3):
            u[m, i + 3] = nodes[m, i]
        mw[i + 2] = mob[i]
        rw[i + 2] = rea[i]

    @pl.loop(0, 14)
    def _(i):
        u0, u1, u2 = u[0, i], u[1, i], u[2, i]
        ca[i] = edge * u0 + middle * u1 + far * u2
        cb[i] = far * u0 + (middle - substep) * u1 + edge * u2

    @pl.loop(0, 12)
    def _(i):
        c0, c1, c2 = cubic(u[0, i + 1]), cubic(u[1, i + 1]), cubic(u[2, i + 1])
        a = ca[i + 1]
        b = cb[i + 1]
        lap_a = ca[i] + ca[i + 2] + around(a) - 6.0 * a
        lap_b = cb[i] + cb[i + 2] + around(b) - 6.0 * b
        v1[i] = u[0, i + 1] + mw[i] * lap_a + rw[i] * (edge * c0 + middle * c1 + far * c2)
        step[i] = mw[i] * lap_b + rw[i] * (far * c0 + (middle - substep) * c1 + edge * c2)

    @pl.loop(0, 10)
    def _(i):
        a = v1[i + 1]
        force = mw[i + 1] * (v1[i] + v1[i + 2] + around(a) - 6.0 * a) + rw[i + 1] * cubic(a)
        f1[i] = force
        v2[i] = a + (substep * force + step[i + 1])

    @pl.loop(0, 8)
    def _(i):
        a = v2[i + 1]
        b = u[0, i + 3]
        mm = mw[i + 2]
        rr = rw[i + 2]
        force = mm * (v2[i] + v2[i + 2] + around(a) - 6.0 * a) + rr * cubic(a)
        first = mm * (u[0, i + 2] + u[0, i + 4] + around(b) - 6.0 * b) + rr * cubic(b)
        second = middle * f1[i + 1]
        jj[0, i] = edge * first + second + far * force
        jj[1, i] = far * first + second + edge * force
        v1_out[i] = v1[i + 2]
        v2_out[i] = a

    def reduced(slot):
        even = mix[slot, pl.ds(0, half, stride=2), :]
        odd = mix[slot, pl.ds(1, half, stride=2), :]
        return 0.5 * even + 0.25 * (odd + roll(odd, 1, 0))

    @pl.loop(0, 4)
    def _(j):
        mix[0] = 0.5 * u[0, 2 * j + 3] + 0.25 * (u[0, 2 * j + 4] + u[0, 2 * j + 2])
        mix[1] = 0.5 * v1[2 * j + 2] + 0.25 * (v1[2 * j + 3] + v1[2 * j + 1])
        mix[2] = 0.5 * v2[2 * j + 1] + 0.25 * (v2[2 * j + 2] + v2[2 * j])
        before = jnp.maximum(2 * j - 1, 0)
        weight = jnp.where(j == 0, 0.0, 0.25)
        for m in range(2):
            mix[3 + m] = 0.5 * jj[m, 2 * j] + 0.25 * jj[m, 2 * j + 1] + weight * jj[m, before]
        for m in range(3):
            coarse[m, j] = reduced(m)
        for m in range(2):
            terms[m, j] = reduced(3 + m)

    for m in range(2):
        rightward[m] = coarse[m, 3]
        mix[m] = jj[m, 7]
        rightward[2 + m] = 0.25 * reduced(m)
    for m in range(3):
        leftward[m] = coarse[m, 0]


def half_force(mid, low, high, mob, rea):
    planar = low + high + roll(mid, 1, 0) + roll(mid, -1, 0)
    vertical = roll(mid, 1, 1) + roll(mid, -1, 1)
    return mob * (planar + 4.0 * vertical - 12.0 * mid) + rea * cubic(mid)


def term_kernel(coarse, terms, from_left, from_right, own, q, rightward, leftward, window):
    for m in range(2):
        window[m, 0] = from_left[m]
        window[m, 5] = from_right[m]
        for j in range(4):
            window[m, j + 1] = coarse[m, j]
    for m in range(2):
        for j in range(4):
            values = terms[m, j] - half_force(window[m, j + 1], window[m, j], window[m, j + 2], own[0, j], own[1, j])
            if j == 0:
                values = values + from_left[2 + m]
            q[4 * m + j] = values
            if m == 0:
                leftward[j] = values
                if j > 0:
                    rightward[j - 1] = values
            else:
                if j < 3:
                    leftward[4 + j] = values
                if j > 1:
                    rightward[1 + j] = values
    for j in range(4):
        rightward[5 + j] = coarse[0, j]
        leftward[7 + j] = window[0, j + 2]


def base_kernel(v1, v2, coarse, from_right, b1, b2, wide):
    half = coarse.shape[2]
    for m, v, b in ((1, v1, b1), (2, v2, b2)):
        widen(lambda j, m=m: coarse[m, j] if j < 4 else from_right[m], wide, half)
        for j in range(4):
            low = wide[j]
            b[2 * j] = v[2 * j] - low
            b[2 * j + 1] = v[2 * j + 1] - 0.5 * (low + wide[j + 1])


def widen(values, wide, half):
    for j in range(5):
        d = values(j)
        wide[j, pl.ds(0, half, stride=2), :] = d
        wide[j, pl.ds(1, half, stride=2), :] = 0.5 * (d + roll(d, -1, 0))


def pack_kernel(q, coarse, from_left, from_right, c_right, own, c_l, c_r, window, mw, rw):
    for i in range(3):
        window[i] = from_left[i]
        mw[i] = c_l[0, i]
        rw[i] = c_l[1, i]
    for i in range(4):
        window[3 + i] = q[i]
        window[7 + i] = from_right[i]
        mw[3 + i] = own[0, i]
        rw[3 + i] = own[1, i]
        mw[7 + i] = c_r[0, i]
        rw[7 + i] = c_r[1, i]
    for i in range(2):
        window[11 + i] = from_left[3 + i]
    for i in range(4):
        window[13 + i] = q[4 + i]
    for i in range(3):
        window[17 + i] = from_right[4 + i]
    for i in range(4):
        window[20 + i] = from_left[5 + i]
        window[24 + i] = coarse[0, i]
        window[29 + i] = from_right[7 + i]
    window[28] = c_right[0]


def sweep_kernel(first_turn, *refs):
    if first_turn:
        flags, mine, other, mw, rw, levels, last, x0, x1, x2, x3 = refs
    else:
        flags, mine, other, mw, rw, mid, low, high, levels, last, x0, x1, x2, x3 = refs

    def run(a, b):
        def own_start():
            @pl.loop(0, 13)
            def _(i):
                x0[i] = a[20 + i]

        if first_turn:
            own_start()
        else:
            pl.when(flags[1] == 0)(own_start)

            @pl.when(flags[1] != 0)
            def _():
                for i in range(4):
                    x0[i] = low[i]
                    x0[9 + i] = high[1 + i]
                for i in range(5):
                    x0[4 + i] = mid[i]

        @pl.loop(0, 11)
        def _(i):
            x1[i] = x0[i + 1] + half_force(x0[i + 1], x0[i], x0[i + 2], mw[i], rw[i]) + a[i]

        @pl.loop(0, 9)
        def _(i):
            x2[i] = x1[i + 1] + half_force(x1[i + 1], x1[i], x1[i + 2], mw[i + 1], rw[i + 1]) + a[11 + i]

        @pl.loop(0, 7)
        def _(i):
            x3[i] = x2[i + 1] + half_force(x2[i + 1], x2[i], x2[i + 2], mw[i + 2], rw[i + 2]) + b[2 + i]

        @pl.loop(0, 5)
        def _(i):
            end = x3[i + 1] + half_force(x3[i + 1], x3[i], x3[i + 2], mw[i + 3], rw[i + 3]) + b[13 + i]
            last[i] = end
            levels[0, i] = x0[i + 4]
            levels[1, i] = x1[i + 3]
            levels[2, i] = x2[i + 2]
            levels[3, i] = x3[i + 1]
            levels[4, i] = end

    pl.when(flags[0] == 0)(lambda: run(mine, other))
    pl.when(flags[0] != 0)(lambda: run(other, mine))


def final_kernel(flags, start, b1, b2, b_before, levels, out, wide):
    half = levels.shape[2]
    core = flags[0]
    for m, b in ((0, b_before), (1, b1), (2, b2)):

        def corrected(m=m, b=b):
            widen(lambda j: levels[2 * core + m, j], wide, half)
            for j in range(4):
                low = wide[j]
                out[0, m, 2 * j] = b[2 * j] + low
                out[0, m, 2 * j + 1] = b[2 * j + 1] + 0.5 * (low + wide[j + 1])

        if m == 0:
            pl.when(flags[2] != 0)(corrected)

            @pl.when(flags[2] == 0)
            def _():
                for i in range(8):
                    out[0, 0, i] = start[i]

        else:
            corrected()


def body(nodes, mobility, reaction):
    states = nodes[0]
    _, blocks, ny, nz = states.shape
    hy = ny // 2
    slice_index = lax.axis_index("tm")
    flags = jnp.stack([slice_index % 2, slice_index // 2, slice_index]).astype(jnp.int32)

    to_right = jnp.concatenate([states[:, 5:].reshape(9, ny, nz), mobility[6:], reaction[6:]])
    to_left = jnp.concatenate([states[:, :3].reshape(9, ny, nz), mobility[:2], reaction[:2]])
    left = ring(to_right, "space", 1)
    right = ring(to_left, "space", -1)

    own, c_to_right, c_to_left = call(
        coefficient_kernel, [(2, 4, hy, nz), (2, 3, hy, nz), (2, 4, hy, nz)], [], mobility, reaction
    )
    c_l = ring(c_to_right, "space", 1)
    c_r = ring(c_to_left, "space", -1)

    plane = (ny, nz)
    small = (hy, nz)
    v1, v2, coarse, terms, to_right, to_left = call(
        fine_kernel,
        [(8,) + plane, (8,) + plane, (3, 4) + small, (2, 4) + small, (4,) + small, (3,) + small],
        [(3, 14) + plane, (12,) + plane, (12,) + plane, (14,) + plane, (14,) + plane, (12,) + plane, (10,) + plane,
         (12,) + plane, (10,) + plane, (2, 8) + plane, (5,) + plane],
        states, mobility, reaction, left, right, flops=2 * 10**7,
    )
    from_left = ring(to_right, "space", 1)
    from_right = ring(to_left, "space", -1)
    q, to_right, to_left = call(
        term_kernel,
        [(8,) + small, (9,) + small, (11,) + small],
        [(2, 6) + small],
        coarse, terms, from_left, from_right, own,
    )
    q_left = ring(to_right, "space", 1)
    q_right = ring(to_left, "space", -1)
    b1, b2 = call(base_kernel, [(8,) + plane, (8,) + plane], [(5,) + plane], v1, v2, coarse, from_right)
    b_before = ring(b2, "tm", 1)
    mine, mw, rw = call(
        pack_kernel, [(33,) + small, (11,) + small, (11,) + small], [],
        q, coarse, q_left, q_right, from_right, own, c_l, c_r,
    )
    other = swapped(mine)
    sweep_outs = [(5, 5) + small, (5,) + small]
    sweep_scratch = [(13,) + small, (11,) + small, (9,) + small, (7,) + small]
    levels, last = call(
        functools.partial(sweep_kernel, True), sweep_outs, sweep_scratch, flags, mine, other, mw, rw, scalars=1
    )
    turns = lax.axis_size("tm") // 2
    for _ in range(turns - 1):
        mid = ring(last, "tm", 2)
        low = ring(mid, "space", 1)
        high = ring(mid, "space", -1)
        levels, last = call(
            functools.partial(sweep_kernel, False), sweep_outs, sweep_scratch,
            flags, mine, other, mw, rw, mid, low, high, scalars=1,
        )
    (out,) = call(
        final_kernel, [(1, 3, 8) + plane], [(5,) + plane], flags, states[0], b1, b2, b_before, levels, scalars=1
    )
    return out


def solution(mesh):
    return jax.shard_map(
        body,
        mesh=mesh,
        in_specs=(
            P("tm", None, "space", None, None),
            P("space", None, None),
            P("space", None, None),
        ),
        out_specs=P("tm", None, "space", None, None),
        check_vma=False,
    )
```

time: 298 us -> 156 us (0.52)
  starting transfers between devices: 103 us -> 28.1 us
  local copies, waits for them, and re-layouts: 39 us -> 2.67 us
  other arithmetic: 28.8 us -> 0.19 us
  waiting for transfers between devices: 125 us -> 99.3 us
  Pallas kernels: 0 us -> 25.3 us
    ppermute x36 -> x19, starting transfers between devices: 103 us -> 28.1 us  [the longest x18 28 us: ring(): lax.ppermute(values, axis, [(i, (i + distance) % count) for i in range(co...]
    slice x107 -> x2, local copies, waits for them, and re-layouts: 30.3 us -> 1.46 us  [the longest x1 1.43 us: body(): states[:, :3].reshape(9, ny, nz)]
    ppermute x36 -> x19, waiting for transfers between devices: 125 us -> 99.3 us  [the longest x18 96.7 us: ring(): lax.ppermute(values, axis, [(i, (i + distance) % count) for i in range(co...]
    pallas_call x0 -> x10, Pallas kernels: none -> 25.3 us  [call(): pl.pallas_call(kernel, out_shape=[jax.ShapeDtypeStruct(s, jnp.float32) fo...]
    add x21 -> x0, other arithmetic: 15.6 us -> none  [the longest x7 5.73 us: wide_sweep(): level_two = level_one + substep * second_force + margins[3][2:-2]]
    select_n x7 -> x0, other arithmetic: 6.44 us -> none  [wide_turn(): return jnp.where(slice_index == 0, own_start, arrived)]
    while x28 -> x0, local copies, waits for them, and re-layouts: 4.55 us -> none
    unnamed x29 -> x14, local copies, waits for them, and re-layouts: 3.58 us -> 0.13 us
  transfers between devices with their start and end apart: 36 -> 19, of which waited for: 23 -> 15; matrix products, arithmetic and copies ran while one was open for 4% -> 1% of each run, Pallas kernels for 0% -> 6%
where the time goes in v1:
time: 156 us
  waiting for transfers between devices  99.3 us (64%)
  starting transfers between devices  28.1 us (18%)
  Pallas kernels  25.3 us (16%)
  local copies, waits for them, and re-layouts  2.67 us (2%)
    ppermute x18, waiting for transfers between devices, ring(): lax.ppermute(values, axis, [(i, (i + distance) % count) for i in range(co...  96.7 us
    ppermute x18, starting transfers between devices, ring(): lax.ppermute(values, axis, [(i, (i + distance) % count) for i in range(co...  28 us
    pallas_call x10, Pallas kernels, call(): pl.pallas_call(kernel, out_shape=[jax.ShapeDtypeStruct(s, jnp.float32) fo...  25.3 us
  transfers between devices with their start and end apart: 19, of which 15 were waited for; matrix products, arithmetic and copies ran while one was open for 1% of the time, Pallas kernels for 6%

profile of v1, /device:TPU:190, one launch (start us, length us, event | category | flops | bytes accessed | tf_op | source)
XLA Modules:
  0.0 155.7 jit_solution(2103012528195051191)
XLA Ops:
  3.9 18.5 %collective-permute-done.left = f32[13,128,128]{2,1,0:T(8,128)S(1)} collective-permute-done((f32[13,128,128]{2,1,0:T(8,128)S(1)}, f32[13,128,128]{2,1,0:T(8,128)S(1)}, u32[]{:S(2)}, u32[]{:S(2)}) %collective-permute-start) | collective-permute-done | bytes 852000 | tf_op jit(solution)/shard_map/ppermute | solution.py:35
  22.4 4.7 %collective-permute-done.1.right = f32[13,128,128]{2,1,0:T(8,128)S(1)} collective-permute-done((f32[13,128,128]{2,1,0:T(8,128)S(1)}, f32[13,128,128]{2,1,0:T(8,128)S(1)}, u32[]{:S(2)}, u32[]{:S(2)}) %collective-permute-start.1) | collective-permute-done | bytes 852000 | tf_op jit(solution)/shard_map/ppermute | solution.py:35
  27.1 5.2 %shard_map.37 = (f32[8,128,128]{2,1,0:T(8,128)S(1)}, f32[8,128,128]{2,1,0:T(8,128)S(1)}, f32[3,4,64,128]{3,2,1,0:T(8,128)S(1)}, f32[2,4,64,128]{3,2,1,0:T(8,128)...) custom-call(f32[3,8,128,128]{3,2,1,0:T(8,128)S(1)} %bitcast.9, f32[8,128,128]{2,1,0:T(8,128)S(1)} %copy-done.1, ...), custom_call_target="tpu_custom_call" | custom-call | flops 20000000 | bytes 6258688 | tf_op jit(solution)/shard_map/pallas_call | solution.py:45
  34.4 6.9 %collective-permute-done.2.from_right.c_right = f32[3,64,128]{2,1,0:T(8,128)S(1)} collective-permute-done((f32[3,64,128]{2,1,0:T(8,128)S(1)}, f32[3,64,128]{2,1,0:T(8,128)S(1)}, u32[]{:S(2)}, u32[]{:S(2)}) %collective-permute-start.2) | collective-permute-done | bytes 98336 | tf_op jit(solution)/shard_map/ppermute | solution.py:35
  41.7 6.2 %collective-permute-start.5 = (f32[9,64,128]{2,1,0:T(8,128)S(1)}, f32[9,64,128]{2,1,0:T(8,128)S(1)}, u32[]{:S(2)}, u32[]{:S(2)}) collective-permute-start(f32[9,64,128]{2,1,0:T(8,128)S(1)} %get-tuple-element.36), channel_id=1, source_target_pairs={{0,1},{1,2},{2,3},{3,4},{4,5},{5,6},{6,7},{7,8},{8,9},{9,10},{10,1... | collective-permute-start | bytes 884744 | tf_op jit(solution)/shard_map/ppermute | solution.py:35
  47.9 6.2 %collective-permute-start.7 = (f32[2,3,64,128]{3,2,1,0:T(8,128)S(1)}, f32[2,3,64,128]{3,2,1,0:T(8,128)S(1)}, u32[]{:S(2)}, u32[]{:S(2)}) collective-permute-start(f32[2,3,64,128]{3,2,1,0:T(8,128)S(1)} %get-tuple-element.38), channel_id=1, source_target_pairs={{0,1},{1,2},{2,3},{3,4},{4,5},{5,6},{6,7},{7,8},{8,9},{9,10},{10,1... | collective-permute-start | bytes 589832 | tf_op jit(solution)/shard_map/ppermute | solution.py:35
  54.1 3.2 %collective-permute-done.7.c_l = f32[2,3,64,128]{3,2,1,0:T(8,128)S(1)} collective-permute-done((f32[2,3,64,128]{3,2,1,0:T(8,128)S(1)}, f32[2,3,64,128]{3,2,1,0:T(8,128)S(1)}, u32[]{:S(2)}, u32[]{:S(2)}) %collective-permute-start.7) | collective-permute-done | bytes 196640 | tf_op jit(solution)/shard_map/ppermute | solution.py:35
  57.3 2.0 %collective-permute-done.8.c_r = f32[2,4,64,128]{3,2,1,0:T(8,128)S(1)} collective-permute-done((f32[2,4,64,128]{3,2,1,0:T(8,128)S(1)}, f32[2,4,64,128]{3,2,1,0:T(8,128)S(1)}, u32[]{:S(2)}, u32[]{:S(2)}) %collective-permute-start.8) | collective-permute-done | bytes 262176 | tf_op jit(solution)/shard_map/ppermute | solution.py:35
  59.7 2.6 %collective-permute-done.9.refs_2_ = f32[33,64,128]{2,1,0:T(8,128)S(1)} collective-permute-done((f32[33,64,128]{2,1,0:T(8,128)S(1)}, f32[33,64,128]{2,1,0:T(8,128)S(1)}, u32[]{:S(2)}, u32[]{:S(2)}) %collective-permute-start.9) | collective-permute-done | bytes 1081376 | tf_op jit(solution)/shard_map/ppermute | solution.py:40
  62.3 4.5 %shard_map.42 = (f32[5,5,64,128]{3,2,1,0:T(8,128)}, f32[5,64,128]{2,1,0:T(8,128)S(1)}) custom-call(s32[3]{0:T(128)S(1)} %pad_add_fusion.refs_0_.flags, f32[33,64,128]{2,1,0:T(8,128)S(1)} %get-tuple-element.40.refs_1_, f32[33,64,128]{2,1,0:T(8,128)S(1)} %collective-permute-done.9.refs_2_, f32[11,64,128]{2,1,0:T(8,128)S(1)} %get-tuple-element.41.refs_3_, ...), custom_call_target="tpu_custom_call" | custom-call | flops 1000000 | bytes 3866636 | tf_op jit(solution)/shard_map/pallas_call | solution.py:45
  68.3 9.3 %collective-permute-done.10.refs_5_ = f32[5,64,128]{2,1,0:T(8,128)S(1)} collective-permute-done((f32[5,64,128]{2,1,0:T(8,128)S(1)}, f32[5,64,128]{2,1,0:T(8,128)S(1)}, u32[]{:S(2)}, u32[]{:S(2)}) %collective-permute-start.10) | collective-permute-done | bytes 163872 | tf_op jit(solution)/shard_map/ppermute | solution.py:35
  77.6 5.6 %collective-permute-start.11 = (f32[5,64,128]{2,1,0:T(8,128)S(1)}, f32[5,64,128]{2,1,0:T(8,128)S(1)}, u32[]{:S(2)}, u32[]{:S(2)}) collective-permute-start(f32[5,64,128]{2,1,0:T(8,128)S(1)} %collective-permute-done.10.refs_5_), channel_id=1, source_target_pairs={{0,1},{1,2},{2,3},{3,4},{4,5},{5,6},{6,7},{7,8},{8,9},{9,10},{10,1... | collective-permute-start | bytes 491528 | tf_op jit(solution)/shard_map/ppermute | solution.py:35
  83.1 3.3 %collective-permute-done.11.refs_6_ = f32[5,64,128]{2,1,0:T(8,128)S(1)} collective-permute-done((f32[5,64,128]{2,1,0:T(8,128)S(1)}, f32[5,64,128]{2,1,0:T(8,128)S(1)}, u32[]{:S(2)}, u32[]{:S(2)}) %collective-permute-start.11) | collective-permute-done | bytes 163872 | tf_op jit(solution)/shard_map/ppermute | solution.py:35
  86.4 6.4 %collective-permute-done.12.refs_7_ = f32[5,64,128]{2,1,0:T(8,128)S(1)} collective-permute-done((f32[5,64,128]{2,1,0:T(8,128)S(1)}, f32[5,64,128]{2,1,0:T(8,128)S(1)}, u32[]{:S(2)}, u32[]{:S(2)}) %collective-permute-start.12) | collective-permute-done | bytes 163872 | tf_op jit(solution)/shard_map/ppermute | solution.py:35
  92.9 4.5 %shard_map.43 = (f32[5,5,64,128]{3,2,1,0:T(8,128)}, f32[5,64,128]{2,1,0:T(8,128)S(1)}) custom-call(s32[3]{0:T(128)S(1)} %pad_add_fusion.refs_0_.flags, f32[33,64,128]{2,1,0:T(8,128)S(1)} %get-tuple-element.40.refs_1_, f32[33,64,128]{2,1,0:T(8,128)S(1)} %collective-permute-done.9.refs_2_, f32[11,64,128]{2,1,0:T(8,128)S(1)} %get-tuple-element.41.refs_3_, ...), custom_call_target="tpu_custom_call" | custom-call | flops 1000000 | bytes 4358156 | tf_op jit(solution)/shard_map/pallas_call | solution.py:45
  97.3 9.6 %collective-permute-done.13.refs_5_ = f32[5,64,128]{2,1,0:T(8,128)S(1)} collective-permute-done((f32[5,64,128]{2,1,0:T(8,128)S(1)}, f32[5,64,128]{2,1,0:T(8,128)S(1)}, u32[]{:S(2)}, u32[]{:S(2)}) %collective-permute-start.13) | collective-permute-done | bytes 163872 | tf_op jit(solution)/shard_map/ppermute | solution.py:35
  109.2 3.0 %collective-permute-done.14.refs_6_ = f32[5,64,128]{2,1,0:T(8,128)S(1)} collective-permute-done((f32[5,64,128]{2,1,0:T(8,128)S(1)}, f32[5,64,128]{2,1,0:T(8,128)S(1)}, u32[]{:S(2)}, u32[]{:S(2)}) %collective-permute-start.14) | collective-permute-done | bytes 163872 | tf_op jit(solution)/shard_map/ppermute | solution.py:35
  112.3 15.8 %collective-permute-done.15.refs_7_ = f32[5,64,128]{2,1,0:T(8,128)S(1)} collective-permute-done((f32[5,64,128]{2,1,0:T(8,128)S(1)}, f32[5,64,128]{2,1,0:T(8,128)S(1)}, u32[]{:S(2)}, u32[]{:S(2)}) %collective-permute-start.15) | collective-permute-done | bytes 163872 | tf_op jit(solution)/shard_map/ppermute | solution.py:35
  128.1 4.5 %shard_map.44 = (f32[5,5,64,128]{3,2,1,0:T(8,128)}, f32[5,64,128]{2,1,0:T(8,128)S(1)}) custom-call(s32[3]{0:T(128)S(1)} %pad_add_fusion.refs_0_.flags, f32[33,64,128]{2,1,0:T(8,128)S(1)} %get-tuple-element.40.refs_1_, f32[33,64,128]{2,1,0:T(8,128)S(1)} %collective-permute-done.9.refs_2_, f32[11,64,128]{2,1,0:T(8,128)S(1)} %get-tuple-element.41.refs_3_, ...), custom_call_target="tpu_custom_call" | custom-call | flops 1000000 | bytes 4358156 | tf_op jit(solution)/shard_map/pallas_call | solution.py:45
  132.6 7.4 %collective-permute-done.16.refs_5_ = f32[5,64,128]{2,1,0:T(8,128)S(1)} collective-permute-done((f32[5,64,128]{2,1,0:T(8,128)S(1)}, f32[5,64,128]{2,1,0:T(8,128)S(1)}, u32[]{:S(2)}, u32[]{:S(2)}) %collective-permute-start.16) | collective-permute-done | bytes 163872 | tf_op jit(solution)/shard_map/ppermute | solution.py:35
  140.0 2.0 %collective-permute-start.18 = (f32[5,64,128]{2,1,0:T(8,128)S(1)}, f32[5,64,128]{2,1,0:T(8,128)S(1)}, u32[]{:S(2)}, u32[]{:S(2)}) collective-permute-start(f32[5,64,128]{2,1,0:T(8,128)S(1)} %collective-permute-done.16.refs_5_), channel_id=1, source_target_pairs={{0,31},{1,0},{2,1},{3,2},{4,3},{5,4},{6,5},{7,6},{8,7},{9,8},{10,9... | collective-permute-start | bytes 491528 | tf_op jit(solution)/shard_map/ppermute | solution.py:35
  143.1 2.2 %collective-permute-done.17.refs_6_ = f32[5,64,128]{2,1,0:T(8,128)S(1)} collective-permute-done((f32[5,64,128]{2,1,0:T(8,128)S(1)}, f32[5,64,128]{2,1,0:T(8,128)S(1)}, u32[]{:S(2)}, u32[]{:S(2)}) %collective-permute-start.17) | collective-permute-done | bytes 163872 | tf_op jit(solution)/shard_map/ppermute | solution.py:35
  145.3 4.2 %collective-permute-done.18.refs_7_ = f32[5,64,128]{2,1,0:T(8,128)S(1)} collective-permute-done((f32[5,64,128]{2,1,0:T(8,128)S(1)}, f32[5,64,128]{2,1,0:T(8,128)S(1)}, u32[]{:S(2)}, u32[]{:S(2)}) %collective-permute-start.18) | collective-permute-done | bytes 163872 | tf_op jit(solution)/shard_map/ppermute | solution.py:35
  149.5 4.2 %shard_map.45 = (f32[5,5,64,128]{3,2,1,0:T(8,128)S(1)}, f32[5,64,128]{2,1,0:T(8,128)}) custom-call(s32[3]{0:T(128)S(1)} %pad_add_fusion.refs_0_.flags, f32[33,64,128]{2,1,0:T(8,128)S(1)} %get-tuple-element.40.refs_1_, f32[33,64,128]{2,1,0:T(8,128)S(1)} %collective-permute-done.9.refs_2_, f32[11,64,128]{2,1,0:T(8,128)S(1)} %get-tuple-element.41.refs_3_, ...), custom_call_target="tpu_custom_call" | custom-call | flops 1000000 | bytes 4358156 | tf_op jit(solution)/shard_map/pallas_call | solution.py:45
  (44 shorter events, 13.4 us)
Async XLA Ops:
  1.6 25.5 %copy-start = (f32[1,3,8,128,128]{4,3,2,1,0:T(8,128)S(1)}, f32[1,3,8,128,128]{4,3,2,1,0:T(8,128)}, u32[]{:S(2)}) copy-start(f32[1,3,8,128,128]{4,3,2,1,0:T(8,128)} %param.3) | copy-start | bytes 4718596
  1.7 20.8 %collective-permute-start = (f32[13,128,128]{2,1,0:T(8,128)S(1)}, f32[13,128,128]{2,1,0:T(8,128)S(1)}, u32[]{:S(2)}, u32[]{:S(2)}) collective-permute-start(f32[13,128,128]{2,1,0:T(8,128)S(1)} %pad_maximum_fusion), channel_id=1, source_target_pairs={{0,1},{1,2},{2,3},{3,4},{4,5},{5,6},{6,7},{7,8},{8,9},{9,10},{10,1... | collective-permute-start | bytes 2555912 | tf_op jit(solution)/shard_map/ppermute | solution.py:35
  2.4 24.7 %collective-permute-start.1 = (f32[13,128,128]{2,1,0:T(8,128)S(1)}, f32[13,128,128]{2,1,0:T(8,128)S(1)}, u32[]{:S(2)}, u32[]{:S(2)}) collective-permute-start(f32[13,128,128]{2,1,0:T(8,128)S(1)} %pad_maximum_fusion.1), channel_id=1, source_target_pairs={{0,31},{1,0},{2,1},{3,2},{4,3},{5,4},{6,5},{7,6},{8,7},{9,8},{10,9... | collective-permute-start | bytes 2555912 | tf_op jit(solution)/shard_map/ppermute | solution.py:35
  32.3 27.2 %copy-start.3 = (f32[8,128,128]{2,1,0:T(8,128)}, f32[8,128,128]{2,1,0:T(8,128)S(1)}, u32[]{:S(2)}) copy-start(f32[8,128,128]{2,1,0:T(8,128)S(1)} %get-tuple-element.26.v1) | copy-start | bytes 1572868
  32.3 27.2 %copy-start.5 = (f32[8,128,128]{2,1,0:T(8,128)}, f32[8,128,128]{2,1,0:T(8,128)S(1)}, u32[]{:S(2)}) copy-start(f32[8,128,128]{2,1,0:T(8,128)S(1)} %get-tuple-element.27.v2) | copy-start | bytes 1572868
  32.3 9.1 %collective-permute-start.4 = (f32[4,64,128]{2,1,0:T(8,128)S(1)}, f32[4,64,128]{2,1,0:T(8,128)S(1)}, u32[]{:S(2)}, u32[]{:S(2)}) collective-permute-start(f32[4,64,128]{2,1,0:T(8,128)S(1)} %get-tuple-element.33), channel_id=1, source_target_pairs={{0,1},{1,2},{2,3},{3,4},{4,5},{5,6},{6,7},{7,8},{8,9},{9,10},{10,1... | collective-permute-start | bytes 393224 | tf_op jit(solution)/shard_map/ppermute | solution.py:35
  32.5 8.8 %collective-permute-start.2 = (f32[3,64,128]{2,1,0:T(8,128)S(1)}, f32[3,64,128]{2,1,0:T(8,128)S(1)}, u32[]{:S(2)}, u32[]{:S(2)}) collective-permute-start(f32[3,64,128]{2,1,0:T(8,128)S(1)} %get-tuple-element.29), channel_id=1, source_target_pairs={{0,31},{1,0},{2,1},{3,2},{4,3},{5,4},{6,5},{7,6},{8,7},{9,8},{10,9... | collective-permute-start | bytes 294920 | tf_op jit(solution)/shard_map/ppermute | solution.py:35
  41.6 17.8 %collective-permute-start.6 = (f32[11,64,128]{2,1,0:T(8,128)S(1)}, f32[11,64,128]{2,1,0:T(8,128)S(1)}, u32[]{:S(2)}, u32[]{:S(2)}) collective-permute-start(f32[11,64,128]{2,1,0:T(8,128)S(1)} %get-tuple-element.37), channel_id=1, source_target_pairs={{0,31},{1,0},{2,1},{3,2},{4,3},{5,4},{6,5},{7,6},{8,7},{9,8},{10,9... | collective-permute-start | bytes 1081352 | tf_op jit(solution)/shard_map/ppermute | solution.py:35
  41.7 17.7 %collective-permute-start.5 = (f32[9,64,128]{2,1,0:T(8,128)S(1)}, f32[9,64,128]{2,1,0:T(8,128)S(1)}, u32[]{:S(2)}, u32[]{:S(2)}) collective-permute-start(f32[9,64,128]{2,1,0:T(8,128)S(1)} %get-tuple-element.36), channel_id=1, source_target_pairs={{0,1},{1,2},{2,3},{3,4},{4,5},{5,6},{6,7},{7,8},{8,9},{9,10},{10,1... | collective-permute-start | bytes 884744 | tf_op jit(solution)/shard_map/ppermute | solution.py:35
  47.9 11.4 %collective-permute-start.8 = (f32[2,4,64,128]{3,2,1,0:T(8,128)S(1)}, f32[2,4,64,128]{3,2,1,0:T(8,128)S(1)}, u32[]{:S(2)}, u32[]{:S(2)}) collective-permute-start(f32[2,4,64,128]{3,2,1,0:T(8,128)S(1)} %get-tuple-element.39), channel_id=1, source_target_pairs={{0,31},{1,0},{2,1},{3,2},{4,3},{5,4},{6,5},{7,6},{8,7},{9,8},{10,9... | collective-permute-start | bytes 786440 | tf_op jit(solution)/shard_map/ppermute | solution.py:35
  47.9 9.4 %collective-permute-start.7 = (f32[2,3,64,128]{3,2,1,0:T(8,128)S(1)}, f32[2,3,64,128]{3,2,1,0:T(8,128)S(1)}, u32[]{:S(2)}, u32[]{:S(2)}) collective-permute-start(f32[2,3,64,128]{3,2,1,0:T(8,128)S(1)} %get-tuple-element.38), channel_id=1, source_target_pairs={{0,1},{1,2},{2,3},{3,4},{4,5},{5,6},{6,7},{7,8},{8,9},{9,10},{10,1... | collective-permute-start | bytes 589832 | tf_op jit(solution)/shard_map/ppermute | solution.py:35
  59.5 2.8 %collective-permute-start.9 = (f32[33,64,128]{2,1,0:T(8,128)S(1)}, f32[33,64,128]{2,1,0:T(8,128)S(1)}, u32[]{:S(2)}, u32[]{:S(2)}) collective-permute-start(f32[33,64,128]{2,1,0:T(8,128)S(1)} %get-tuple-element.40.refs_1_), channel_id=1, source_target_pairs={{0,32},{32,0},{64,96},{96,64},{128,160},{160,128},{192,224},{224,1... | collective-permute-start | bytes 3244040 | tf_op jit(solution)/shard_map/ppermute | solution.py:40
  66.8 42.2 %copy-start.4 = (f32[8,128,128]{2,1,0:T(8,128)S(1)}, f32[8,128,128]{2,1,0:T(8,128)}, u32[]{:S(2)}) copy-start(f32[8,128,128]{2,1,0:T(8,128)} %copy-done.3) | copy-start | bytes 1572868
  66.8 42.2 %copy-start.6 = (f32[8,128,128]{2,1,0:T(8,128)S(1)}, f32[8,128,128]{2,1,0:T(8,128)}, u32[]{:S(2)}) copy-start(f32[8,128,128]{2,1,0:T(8,128)} %copy-done.5) | copy-start | bytes 1572868
  66.8 10.8 %collective-permute-start.10 = (f32[5,64,128]{2,1,0:T(8,128)S(1)}, f32[5,64,128]{2,1,0:T(8,128)S(1)}, u32[]{:S(2)}, u32[]{:S(2)}) collective-permute-start(f32[5,64,128]{2,1,0:T(8,128)S(1)} %get-tuple-element.43), channel_id=1, source_target_pairs={{0,64},{32,96},{64,128},{96,160},{128,192},{160,224},{192,0},{224,... | collective-permute-start | bytes 491528 | tf_op jit(solution)/shard_map/ppermute | solution.py:35
  77.6 8.9 %collective-permute-start.11 = (f32[5,64,128]{2,1,0:T(8,128)S(1)}, f32[5,64,128]{2,1,0:T(8,128)S(1)}, u32[]{:S(2)}, u32[]{:S(2)}) collective-permute-start(f32[5,64,128]{2,1,0:T(8,128)S(1)} %collective-permute-done.10.refs_5_), channel_id=1, source_target_pairs={{0,1},{1,2},{2,3},{3,4},{4,5},{5,6},{6,7},{7,8},{8,9},{9,10},{10,1... | collective-permute-start | bytes 491528 | tf_op jit(solution)/shard_map/ppermute | solution.py:35
  83.1 9.7 %collective-permute-start.12 = (f32[5,64,128]{2,1,0:T(8,128)S(1)}, f32[5,64,128]{2,1,0:T(8,128)S(1)}, u32[]{:S(2)}, u32[]{:S(2)}) collective-permute-start(f32[5,64,128]{2,1,0:T(8,128)S(1)} %collective-permute-done.10.refs_5_), channel_id=1, source_target_pairs={{0,31},{1,0},{2,1},{3,2},{4,3},{5,4},{6,5},{7,6},{8,7},{9,8},{10,9... | collective-permute-start | bytes 491528 | tf_op jit(solution)/shard_map/ppermute | solution.py:35
  97.3 9.6 %collective-permute-start.13 = (f32[5,64,128]{2,1,0:T(8,128)S(1)}, f32[5,64,128]{2,1,0:T(8,128)S(1)}, u32[]{:S(2)}, u32[]{:S(2)}) collective-permute-start(f32[5,64,128]{2,1,0:T(8,128)S(1)} %get-tuple-element.44), channel_id=1, source_target_pairs={{0,64},{32,96},{64,128},{96,160},{128,192},{160,224},{192,0},{224,... | collective-permute-start | bytes 491528 | tf_op jit(solution)/shard_map/ppermute | solution.py:35
  107.0 5.3 %collective-permute-start.14 = (f32[5,64,128]{2,1,0:T(8,128)S(1)}, f32[5,64,128]{2,1,0:T(8,128)S(1)}, u32[]{:S(2)}, u32[]{:S(2)}) collective-permute-start(f32[5,64,128]{2,1,0:T(8,128)S(1)} %collective-permute-done.13.refs_5_), channel_id=1, source_target_pairs={{0,1},{1,2},{2,3},{3,4},{4,5},{5,6},{6,7},{7,8},{8,9},{9,10},{10,1... | collective-permute-start | bytes 491528 | tf_op jit(solution)/shard_map/ppermute | solution.py:35
  107.7 20.4 %collective-permute-start.15 = (f32[5,64,128]{2,1,0:T(8,128)S(1)}, f32[5,64,128]{2,1,0:T(8,128)S(1)}, u32[]{:S(2)}, u32[]{:S(2)}) collective-permute-start(f32[5,64,128]{2,1,0:T(8,128)S(1)} %collective-permute-done.13.refs_5_), channel_id=1, source_target_pairs={{0,31},{1,0},{2,1},{3,2},{4,3},{5,4},{6,5},{7,6},{8,7},{9,8},{10,9... | collective-permute-start | bytes 491528 | tf_op jit(solution)/shard_map/ppermute | solution.py:35
  109.1 44.6 %collective-permute-start.3 = (f32[8,128,128]{2,1,0:T(8,128)S(1)}, f32[8,128,128]{2,1,0:T(8,128)S(1)}, u32[]{:S(2)}, u32[]{:S(2)}) collective-permute-start(f32[8,128,128]{2,1,0:T(8,128)S(1)} %get-tuple-element.31.b2), channel_id=1, source_target_pairs={{0,32},{32,64},{64,96},{96,128},{128,160},{160,192},{192,224},{224... | collective-permute-start | bytes 1572872 | tf_op jit(solution)/shard_map/ppermute | solution.py:35
  132.6 7.4 %collective-permute-start.16 = (f32[5,64,128]{2,1,0:T(8,128)S(1)}, f32[5,64,128]{2,1,0:T(8,128)S(1)}, u32[]{:S(2)}, u32[]{:S(2)}) collective-permute-start(f32[5,64,128]{2,1,0:T(8,128)S(1)} %get-tuple-element.45), channel_id=1, source_target_pairs={{0,64},{32,96},{64,128},{96,160},{128,192},{160,224},{192,0},{224,... | collective-permute-start | bytes 491528 | tf_op jit(solution)/shard_map/ppermute | solution.py:35
  140.0 5.3 %collective-permute-start.17 = (f32[5,64,128]{2,1,0:T(8,128)S(1)}, f32[5,64,128]{2,1,0:T(8,128)S(1)}, u32[]{:S(2)}, u32[]{:S(2)}) collective-permute-start(f32[5,64,128]{2,1,0:T(8,128)S(1)} %collective-permute-done.16.refs_5_), channel_id=1, source_target_pairs={{0,1},{1,2},{2,3},{3,4},{4,5},{5,6},{6,7},{7,8},{8,9},{9,10},{10,1... | collective-permute-start | bytes 491528 | tf_op jit(solution)/shard_map/ppermute | solution.py:35
  140.0 9.5 %collective-permute-start.18 = (f32[5,64,128]{2,1,0:T(8,128)S(1)}, f32[5,64,128]{2,1,0:T(8,128)S(1)}, u32[]{:S(2)}, u32[]{:S(2)}) collective-permute-start(f32[5,64,128]{2,1,0:T(8,128)S(1)} %collective-permute-done.16.refs_5_), channel_id=1, source_target_pairs={{0,31},{1,0},{2,1},{3,2},{4,3},{5,4},{6,5},{7,6},{8,7},{9,8},{10,9... | collective-permute-start | bytes 491528 | tf_op jit(solution)/shard_map/ppermute | solution.py:35
  (2 other events, 3.0 us)

commit v2 on v1

v2 whole, which is shorter than its diff:
```python
import functools
import jax
import jax.numpy as jnp
from jax import lax
from jax.experimental import pallas as pl
from jax.experimental.pallas import tpu as pltpu
from jax.sharding import PartitionSpec as P

edge = 5.0 / 24.0
middle = 1.0 / 3.0
far = -1.0 / 24.0
substep = 0.5


def roll(values, amount, axis):
    return pltpu.roll(values, amount % values.shape[axis], axis)


def around(values):
    return roll(values, 1, 0) + roll(values, -1, 0) + roll(values, 1, 1) + roll(values, -1, 1)


def cubic(values):
    return values - values * values * values


def cost(flops, moved):
    return pl.CostEstimate(flops=flops, bytes_accessed=moved, transcendentals=0)


def ring(values, axis, distance):
    count = lax.axis_size(axis)
    return lax.ppermute(values, axis, [(i, (i + distance) % count) for i in range(count)])


def together(*values):
    return lax.optimization_barrier(values)


def swapped(values):
    count = lax.axis_size("tm")
    return lax.ppermute(values, "tm", [(i, i ^ 1) for i in range(count)])


def call(kernel, outs, scratch, *args, flops=10**6, scalars=0, limit=8):
    moved = sum(a.size * 4 for a in args) + sum(4 * functools.reduce(lambda x, y: x * y, s) for s in outs)
    result = pl.pallas_call(
        kernel,
        out_shape=[jax.ShapeDtypeStruct(s, jnp.float32) for s in outs],
        in_specs=[pl.BlockSpec(memory_space=pltpu.SMEM)] * scalars
        + [pl.BlockSpec(memory_space=pltpu.VMEM)] * (len(args) - scalars),
        out_specs=[pl.BlockSpec(memory_space=pltpu.VMEM) for _ in outs],
        scratch_shapes=[pltpu.VMEM(s, jnp.float32) for s in scratch],
        compiler_params=pltpu.CompilerParams(vmem_limit_bytes=limit * 1024 * 1024),
        cost_estimate=cost(flops, moved),
    )(*args)
    return result


def coefficient_kernel(mob, rea, own, rightward, leftward):
    half = mob.shape[1] // 2
    for k, (source, scale) in enumerate(((mob, 0.125), (rea, 0.5))):
        for j in range(4):
            own[k, j] = scale * source[2 * j, pl.ds(0, half, stride=2), :]
        for j in range(2):
            rightward[k, pl.ds(j * half, half), :] = own[k, j + 1]
        for j in range(3):
            place = 3 * k + j
            leftward[place // 2, pl.ds(place % 2 * half, half), :] = own[k, j + 1]


def window_kernel(own, left, right, mw, rw):
    half = own.shape[2]
    for k, (out, scale) in enumerate(((mw, 0.125), (rw, 0.5))):
        for j in range(2):
            out[j] = left[13 + k, pl.ds(j * half, half), :]
        out[2] = scale * left[9 + 2 * k, pl.ds(0, half, stride=2), :]
        for j in range(4):
            out[3 + j] = own[k, j]
        out[7] = scale * right[9 + 2 * k, pl.ds(0, half, stride=2), :]
        for j in range(3):
            place = 3 * k + j
            out[8 + j] = right[13 + place // 2, pl.ds(place % 2 * half, half), :]


def widen(d, wide, j):
    half = d.shape[0]
    wide[j, pl.ds(0, half, stride=2), :] = d
    wide[j, pl.ds(1, half, stride=2), :] = 0.5 * (d + roll(d, -1, 0))


def half_force(mid, low, high, mob, rea):
    planar = low + high + roll(mid, 1, 0) + roll(mid, -1, 0)
    vertical = roll(mid, 1, 1) + roll(mid, -1, 1)
    return mob * (planar + 4.0 * vertical - 12.0 * mid) + rea * cubic(mid)


def fine_kernel(
    nodes, mob, rea, left, right, own,
    b1, b2, q, start, coarse, share, rightward, leftward,
    u, mw, rw, ca, cb, v1, v2, step, f1, jj, mix,
):
    half = mob.shape[1] // 2
    for m in range(3):
        for i in range(3):
            u[m, i] = left[3 * m + i]
            u[m, 11 + i] = right[3 * m + i]
    for i in range(2):
        mw[i] = left[9 + i]
        mw[10 + i] = right[9 + i]
        rw[i] = left[11 + i]
        rw[10 + i] = right[11 + i]

    @pl.loop(0, 8)
    def _(i):
        for m in range(3):
            u[m, i + 3] = nodes[m, i]
        mw[i + 2] = mob[i]
        rw[i + 2] = rea[i]

    @pl.loop(0, 14)
    def _(i):
        u0, u1, u2 = u[0, i], u[1, i], u[2, i]
        ca[i] = edge * u0 + middle * u1 + far * u2
        cb[i] = far * u0 + (middle - substep) * u1 + edge * u2

    @pl.loop(0, 12)
    def _(i):
        c0, c1, c2 = cubic(u[0, i + 1]), cubic(u[1, i + 1]), cubic(u[2, i + 1])
        a = ca[i + 1]
        b = cb[i + 1]
        lap_a = ca[i] + ca[i + 2] + around(a) - 6.0 * a
        lap_b = cb[i] + cb[i + 2] + around(b) - 6.0 * b
        v1[i] = u[0, i + 1] + mw[i] * lap_a + rw[i] * (edge * c0 + middle * c1 + far * c2)
        step[i] = mw[i] * lap_b + rw[i] * (far * c0 + (middle - substep) * c1 + edge * c2)

    @pl.loop(0, 10)
    def _(i):
        a = v1[i + 1]
        force = mw[i + 1] * (v1[i] + v1[i + 2] + around(a) - 6.0 * a) + rw[i + 1] * cubic(a)
        f1[i] = force
        v2[i] = a + (substep * force + step[i + 1])

    @pl.loop(0, 8)
    def _(i):
        a = v2[i + 1]
        b = u[0, i + 3]
        mm = mw[i + 2]
        rr = rw[i + 2]
        force = mm * (v2[i] + v2[i + 2] + around(a) - 6.0 * a) + rr * cubic(a)
        first = mm * (u[0, i + 2] + u[0, i + 4] + around(b) - 6.0 * b) + rr * cubic(b)
        second = middle * f1[i + 1]
        jj[0, i] = edge * first + second + far * force
        jj[1, i] = far * first + second + edge * force

    def reduced(slot):
        even = mix[slot, pl.ds(0, half, stride=2), :]
        odd = mix[slot, pl.ds(1, half, stride=2), :]
        return 0.5 * even + 0.25 * (odd + roll(odd, 1, 0))

    @pl.loop(0, 6)
    def _(j):
        mix[0] = 0.5 * u[0, 2 * j + 1] + 0.25 * (u[0, 2 * j + 2] + u[0, 2 * j])
        start[j] = reduced(0)

    @pl.loop(0, 4)
    def _(j):
        mix[1] = 0.5 * v1[2 * j + 2] + 0.25 * (v1[2 * j + 3] + v1[2 * j + 1])
        mix[2] = 0.5 * v2[2 * j + 1] + 0.25 * (v2[2 * j + 2] + v2[2 * j])
        before = jnp.maximum(2 * j - 1, 0)
        weight = jnp.where(j == 0, 0.0, 0.25)
        for m in range(2):
            mix[3 + m] = 0.5 * jj[m, 2 * j] + 0.25 * jj[m, 2 * j + 1] + weight * jj[m, before]
        for m in range(2):
            coarse[m, j] = reduced(1 + m)
        for m in range(2):
            q[4 * m + j] = reduced(3 + m)

    for m in range(2):
        mix[m] = jj[m, 7]
        share[m] = 0.25 * reduced(m)

    empty = jnp.zeros_like(share[0])
    for j in range(4):
        q[j] = q[j] - half_force(start[j + 1], start[j], start[j + 2], own[0, j], own[1, j])
        low = coarse[0, j - 1] if j > 0 else empty
        high = coarse[0, j + 1] if j < 3 else empty
        q[4 + j] = q[4 + j] - half_force(coarse[0, j], low, high, own[0, j], own[1, j])

    for i in range(3):
        rightward[i] = q[1 + i]
        rightward[5 + i] = start[1 + i]
        leftward[4 + i] = q[4 + i]
    for i in range(2):
        rightward[3 + i] = q[6 + i]
        rightward[9 + i] = share[i]
        leftward[11 + i] = coarse[i, 0]
    rightward[8] = coarse[0, 3]
    for i in range(4):
        leftward[i] = q[i]
        leftward[7 + i] = start[2 + i]

    for m, v, first, b in ((0, v1, 2, b1), (1, v2, 1, b2)):
        for j in range(4):
            widen(coarse[m, j], mix, j)
        mix[4] = jnp.zeros_like(mix[4])
        for j in range(4):
            low = mix[j]
            b[2 * j] = v[2 * j + first] - low
            b[2 * j + 1] = v[2 * j + 1 + first] - 0.5 * (low + mix[j + 1])


def pack_kernel(q, start, c1, share, from_left, from_right, mw, window):
    window[0] = from_left[0]
    window[1] = from_left[1]
    window[2] = from_left[2]
    window[3] = q[0] + from_left[9]
    for i in range(1, 4):
        window[3 + i] = q[i]
        window[7 + i] = from_right[i]
    window[7] = from_right[0] + share[0]
    window[11] = from_left[3]
    window[12] = from_left[4] - mw[2] * c1[0]
    window[13] = q[4] + from_left[10] - mw[3] * from_left[8]
    window[14] = q[5]
    window[15] = q[6]
    window[16] = q[7] - mw[6] * from_right[11]
    window[17] = from_right[4] + share[1] - mw[7] * c1[3]
    window[18] = from_right[5]
    window[19] = from_right[6]
    for i in range(3):
        window[20 + i] = from_left[5 + i]
    for i in range(6):
        window[23 + i] = start[i]
    for i in range(4):
        window[29 + i] = from_right[7 + i]
    for i in range(2):
        window[33 + i] = from_right[11 + i]


def order(first, second, out):
    for i in range(20):
        out[i] = first[i]
    for i in range(7):
        out[20 + i] = second[2 + i]
    for i in range(5):
        out[27 + i] = second[13 + i]
    for i in range(2):
        out[32 + i] = first[33 + i]
        out[34 + i] = second[33 + i]
    for i in range(13):
        out[36 + i] = first[20 + i]


def sweep(x0, q, mw, rw, last, levels, x1, x2, x3):
    def level(source, target, count, terms, shift):
        for i in range(count):
            mid = source[i + 1]
            force = half_force(mid, source[i], source[i + 2], mw[i + shift], rw[i + shift])
            target[i] = mid + force + q[terms + i]

    level(x0, x1, 11, 0, 0)
    level(x1, x2, 9, 11, 1)
    level(x2, x3, 7, 20, 2)
    level(x3, last, 5, 27, 3)
    last[5] = q[35]
    if levels is not None:
        for i in range(4):
            levels[0, i] = x0[i + 4]
            levels[1, i] = x1[i + 3]
            levels[2, i] = x2[i + 2]
            levels[3, i] = x3[i + 1]
            levels[4, i] = last[i]
        levels[1, 4] = x1[7] - q[32]
        levels[2, 4] = x2[6] - q[33]
        levels[3, 4] = x3[5] - q[34]
        levels[4, 4] = last[4] - q[35]


def first_kernel(flags, mine, other, mw, rw, last, ordered, x1, x2, x3):
    pl.when(flags[0] == 0)(lambda: order(mine, other, ordered))
    pl.when(flags[0] != 0)(lambda: order(other, mine, ordered))
    sweep(ordered.at[pl.ds(36, 13)], ordered, mw, rw, last, None, x1, x2, x3)


def turn_kernel(final, flags, ordered, mw, rw, mid, low, high, last, *refs):
    levels = refs[0] if final else None
    x0, x1, x2, x3 = refs[-4:]

    @pl.when(flags[1] == 0)
    def _():
        for i in range(13):
            x0[i] = ordered[36 + i]

    @pl.when(flags[1] != 0)
    def _():
        for i in range(4):
            x0[i] = low[i]
            x0[9 + i] = high[i]
        for i in range(5):
            x0[4 + i] = mid[i]

    sweep(x0, ordered, mw, rw, last, levels, x1, x2, x3)
    if final:
        levels[0, 4] = mid[4] - mid[5]


def final_kernel(flags, start, b1, b2, b_before, levels, out, wide):
    core = flags[0]
    for m, b in ((0, b_before), (1, b1), (2, b2)):

        def corrected(m=m, b=b):
            for j in range(5):
                widen(levels[2 * core + m, j], wide, j)
            for j in range(4):
                low = wide[j]
                out[0, m, 2 * j] = b[2 * j] + low
                out[0, m, 2 * j + 1] = b[2 * j + 1] + 0.5 * (low + wide[j + 1])

        if m == 0:
            pl.when(flags[2] != 0)(corrected)

            @pl.when(flags[2] == 0)
            def _():
                for i in range(8):
                    out[0, 0, i] = start[i]

        else:
            corrected()


def body(nodes, mobility, reaction):
    states = nodes[0]
    _, blocks, ny, nz = states.shape
    hy = ny // 2
    plane = (ny, nz)
    small = (hy, nz)
    slice_index = lax.axis_index("tm")
    flags = jnp.stack([slice_index % 2, slice_index // 2, slice_index]).astype(jnp.int32)

    own, c_to_right, c_to_left = call(
        coefficient_kernel, [(2, 4) + small, (2,) + plane, (3,) + plane], [], mobility, reaction
    )
    to_right = jnp.concatenate([states[:, 5:].reshape((9,) + plane), mobility[6:], reaction[6:], c_to_right])
    to_left = jnp.concatenate([states[:, :3].reshape((9,) + plane), mobility[:2], reaction[:2], c_to_left])
    left = ring(to_right, "space", 1)
    right = ring(to_left, "space", -1)
    b1, b2, q, start, coarse, share, to_right, to_left = call(
        fine_kernel,
        [(8,) + plane, (8,) + plane, (8,) + small, (6,) + small, (2, 4) + small, (2,) + small, (11,) + small, (13,) + small],
        [(3, 14) + plane, (12,) + plane, (12,) + plane, (14,) + plane, (14,) + plane, (12,) + plane, (10,) + plane,
         (12,) + plane, (10,) + plane, (2, 8) + plane, (5,) + plane],
        states, mobility, reaction, left, right, own, flops=2 * 10**7, limit=16,
    )
    q_left = ring(to_right, "space", 1)
    q_right = ring(to_left, "space", -1)
    b_before = ring(b2, "tm", 1)
    mw, rw = call(window_kernel, [(11,) + small, (11,) + small], [], own, left, right)
    (mine,) = call(pack_kernel, [(35,) + small], [], q, start, coarse[0], share, q_left, q_right, mw)
    other = swapped(mine)
    levels_shape = [(11,) + small, (9,) + small, (7,) + small]
    last, ordered = call(
        first_kernel, [(6,) + small, (49,) + small], levels_shape, flags, mine, other, mw, rw, scalars=1
    )
    turns = lax.axis_size("tm") // 2
    for turn in range(1, turns):
        final = turn == turns - 1
        mid = ring(last, "tm", 2)
        if turn == 1:
            mid, b_before = together(mid, b_before)
        low = ring(mid[0:4], "space", 1)
        high = ring(mid[1:5], "space", -1)
        last, *levels = call(
            functools.partial(turn_kernel, final), [(6,) + small] + [(5, 5) + small] * final, [(13,) + small] + levels_shape,
            flags, ordered, mw, rw, mid, low, high, scalars=1,
        )
    (out,) = call(
        final_kernel, [(1, 3, 8) + plane], [(5,) + plane], flags, states[0], b1, b2, b_before, levels[0], scalars=1,
    )
    return out


def solution(mesh):
    return jax.shard_map(
        body,
        mesh=mesh,
        in_specs=(
            P("tm", None, "space", None, None),
            P("space", None, None),
            P("space", None, None),
        ),
        out_specs=P("tm", None, "space", None, None),
        check_vma=False,
    )
```

time: 156 us -> 142 us (0.910)
  the two profiles are of different devices: /device:TPU:190 before, /device:TPU:30 now
where the time goes in v2:
time: 142 us
  waiting for transfers between devices  89 us (63%)
  starting transfers between devices  33 us (23%)
  Pallas kernels  16.1 us (11%)
  local copies, waits for them, and re-layouts  3.55 us (2%)
    ppermute x14, waiting for transfers between devices, ring(): lax.ppermute(values, axis, [(i, (i + distance) % count) for i in range(co...  86.7 us
    ppermute x14, starting transfers between devices, ring(): lax.ppermute(values, axis, [(i, (i + distance) % count) for i in range(co...  33 us
    pallas_call x9, Pallas kernels, call(): pl.pallas_call(kernel, out_shape=[jax.ShapeDtypeStruct(s, jnp.float32) fo...  16.1 us
  transfers between devices with their start and end apart: 15, of which 15 were waited for; matrix products, arithmetic and copies ran while one was open for 0% of the time, Pallas kernels for 2%

profile of v2, /device:TPU:30, one launch (start us, length us, event | category | flops | bytes accessed | tf_op | source)
XLA Modules:
  0.0 142.2 jit_solution(12704856893096167266)
XLA Ops:
  4.5 5.6 %collective-permute-start = (f32[15,128,128]{2,1,0:T(8,128)S(1)}, f32[15,128,128]{2,1,0:T(8,128)S(1)}, u32[]{:S(2)}, u32[]{:S(2)}) collective-permute-start(f32[15,128,128]{2,1,0:T(8,128)S(1)} %pad_maximum_fusion.1), channel_id=1, source_target_pairs={{0,1},{1,2},{2,3},{3,4},{4,5},{5,6},{6,7},{7,8},{8,9},{9,10},{10,1... | collective-permute-start | bytes 2949128 | tf_op jit(solution)/shard_map/ppermute | solution.py:33
  10.1 20.7 %collective-permute-done.left = f32[15,128,128]{2,1,0:T(8,128)S(1)} collective-permute-done((f32[15,128,128]{2,1,0:T(8,128)S(1)}, f32[15,128,128]{2,1,0:T(8,128)S(1)}, u32[]{:S(2)}, u32[]{:S(2)}) %collective-permute-start) | collective-permute-done | bytes 983072 | tf_op jit(solution)/shard_map/ppermute | solution.py:33
  30.9 2.0 %collective-permute-done.1.right = f32[16,128,128]{2,1,0:T(8,128)S(1)} collective-permute-done((f32[16,128,128]{2,1,0:T(8,128)S(1)}, f32[16,128,128]{2,1,0:T(8,128)S(1)}, u32[]{:S(2)}, u32[]{:S(2)}) %collective-permute-start.1) | collective-permute-done | bytes 1048608 | tf_op jit(solution)/shard_map/ppermute | solution.py:33
  32.8 6.4 %shard_map.38 = (f32[8,128,128]{2,1,0:T(8,128)S(1)}, f32[8,128,128]{2,1,0:T(8,128)}, f32[8,64,128]{2,1,0:T(8,128)S(1)}, f32[6,64,128]{2,1,0:T(8,128)S(1)}, f32[2...) custom-call(f32[3,8,128,128]{3,2,1,0:T(8,128)S(1)} %bitcast.11, ...), custom_call_target="tpu_custom_call" | custom-call | flops 20000000 | bytes 7536640 | tf_op jit(solution)/shard_map/pallas_call | solution.py:47
  39.3 6.2 %collective-permute-start.2 = (f32[11,64,128]{2,1,0:T(8,128)S(1)}, f32[11,64,128]{2,1,0:T(8,128)S(1)}, u32[]{:S(2)}, u32[]{:S(2)}) collective-permute-start(f32[11,64,128]{2,1,0:T(8,128)S(1)} %get-tuple-element.32), channel_id=1, source_target_pairs={{0,1},{1,2},{2,3},{3,4},{4,5},{5,6},{6,7},{7,8},{8,9},{9,10},{10,1... | collective-permute-start | bytes 1081352 | tf_op jit(solution)/shard_map/ppermute | solution.py:33
  45.6 6.4 %collective-permute-done.2.from_left = f32[11,64,128]{2,1,0:T(8,128)S(1)} collective-permute-done((f32[11,64,128]{2,1,0:T(8,128)S(1)}, f32[11,64,128]{2,1,0:T(8,128)S(1)}, u32[]{:S(2)}, u32[]{:S(2)}) %collective-permute-start.2) | collective-permute-done | bytes 360480 | tf_op jit(solution)/shard_map/ppermute | solution.py:33
  52.0 2.1 %collective-permute-done.3.from_right = f32[13,64,128]{2,1,0:T(8,128)S(1)} collective-permute-done((f32[13,64,128]{2,1,0:T(8,128)S(1)}, f32[13,64,128]{2,1,0:T(8,128)S(1)}, u32[]{:S(2)}, u32[]{:S(2)}) %collective-permute-start.3) | collective-permute-done | bytes 426016 | tf_op jit(solution)/shard_map/ppermute | solution.py:33
  54.9 2.3 %collective-permute-done.4.other = f32[35,64,128]{2,1,0:T(8,128)} collective-permute-done((f32[35,64,128]{2,1,0:T(8,128)S(1)}, f32[35,64,128]{2,1,0:T(8,128)}, u32[]{:S(2)}, u32[]{:S(2)}) %collective-permute-start.4) | collective-permute-done | bytes 1146912 | tf_op jit(solution)/shard_map/ppermute | solution.py:42
  57.3 2.2 %shard_map.41 = (f32[6,64,128]{2,1,0:T(8,128)S(1)}, f32[49,64,128]{2,1,0:T(8,128)S(1)}) custom-call(s32[3]{0:T(128)S(1)} %pad_add_fusion.flags, f32[35,64,128]{2,1,0:T(8,128)S(1)} %shard_map.40.mine, f32[35,64,128]{2,1,0:T(8,128)} %collective-permute-done.4.other, f32[11,64,128]{2,1,0:T(8,128)S(1)} %get-tuple-element.34.mw, ...), custom_call_target="tpu_custom_call" | custom-call | flops 1000000 | bytes 4816908 | tf_op jit(solution)/shard_map/pallas_call | solution.py:47
  59.5 3.3 %collective-permute-start.5 = (f32[6,64,128]{2,1,0:T(8,128)S(1)}, f32[6,64,128]{2,1,0:T(8,128)S(1)}, u32[]{:S(2)}, u32[]{:S(2)}) collective-permute-start(f32[6,64,128]{2,1,0:T(8,128)S(1)} %get-tuple-element.36), channel_id=1, source_target_pairs={{0,64},{32,96},{64,128},{96,160},{128,192},{160,224},{192,0},{224,... | collective-permute-start | bytes 589832 | tf_op jit(solution)/shard_map/ppermute | solution.py:33
  62.8 10.0 %collective-permute-done.6.b_before = f32[8,128,128]{2,1,0:T(8,128)} collective-permute-done((f32[8,128,128]{2,1,0:T(8,128)}, f32[8,128,128]{2,1,0:T(8,128)}, u32[]{:S(2)}, u32[]{:S(2)}) %collective-permute-start.6) | collective-permute-done | bytes 524320 | tf_op jit(solution)/shard_map/ppermute | solution.py:33
  73.2 11.4 %collective-permute-start.7 = (f32[4,64,128]{2,1,0:T(8,128)S(1)}, f32[4,64,128]{2,1,0:T(8,128)S(1)}, u32[]{:S(2)}, u32[]{:S(2)}) collective-permute-start(f32[4,64,128]{2,1,0:T(8,128)S(1)} %get-tuple-element.52), channel_id=1, source_target_pairs={{0,1},{1,2},{2,3},{3,4},{4,5},{5,6},{6,7},{7,8},{8,9},{9,10},{10,1... | collective-permute-start | bytes 393224 | tf_op jit(solution)/shard_map/ppermute | solution.py:33
  84.6 3.1 %collective-permute-done.7.low = f32[4,64,128]{2,1,0:T(8,128)S(1)} collective-permute-done((f32[4,64,128]{2,1,0:T(8,128)S(1)}, f32[4,64,128]{2,1,0:T(8,128)S(1)}, u32[]{:S(2)}, u32[]{:S(2)}) %collective-permute-start.7) | collective-permute-done | bytes 131104 | tf_op jit(solution)/shard_map/ppermute | solution.py:33
  87.6 7.0 %collective-permute-done.8.high = f32[4,64,128]{2,1,0:T(8,128)S(1)} collective-permute-done((f32[4,64,128]{2,1,0:T(8,128)S(1)}, f32[4,64,128]{2,1,0:T(8,128)S(1)}, u32[]{:S(2)}, u32[]{:S(2)}) %collective-permute-start.8) | collective-permute-done | bytes 131104 | tf_op jit(solution)/shard_map/ppermute | solution.py:33
  96.1 10.2 %collective-permute-done.9.mid = f32[6,64,128]{2,1,0:T(8,128)S(1)} collective-permute-done((f32[6,64,128]{2,1,0:T(8,128)S(1)}, f32[6,64,128]{2,1,0:T(8,128)S(1)}, u32[]{:S(2)}, u32[]{:S(2)}) %collective-permute-start.9) | collective-permute-done | bytes 196640 | tf_op jit(solution)/shard_map/ppermute | solution.py:33
  106.4 2.0 %collective-permute-start.11 = (f32[4,64,128]{2,1,0:T(8,128)S(1)}, f32[4,64,128]{2,1,0:T(8,128)S(1)}, u32[]{:S(2)}, u32[]{:S(2)}) collective-permute-start(f32[4,64,128]{2,1,0:T(8,128)S(1)} %get-tuple-element.49), channel_id=1, source_target_pairs={{0,31},{1,0},{2,1},{3,2},{4,3},{5,4},{6,5},{7,6},{8,7},{9,8},{10,9... | collective-permute-start | bytes 393224 | tf_op jit(solution)/shard_map/ppermute | solution.py:33
  108.4 3.4 %collective-permute-done.10.low = f32[4,64,128]{2,1,0:T(8,128)S(1)} collective-permute-done((f32[4,64,128]{2,1,0:T(8,128)S(1)}, f32[4,64,128]{2,1,0:T(8,128)S(1)}, u32[]{:S(2)}, u32[]{:S(2)}) %collective-permute-start.10) | collective-permute-done | bytes 131104 | tf_op jit(solution)/shard_map/ppermute | solution.py:33
  111.8 4.5 %collective-permute-done.11.high = f32[4,64,128]{2,1,0:T(8,128)S(1)} collective-permute-done((f32[4,64,128]{2,1,0:T(8,128)S(1)}, f32[4,64,128]{2,1,0:T(8,128)S(1)}, u32[]{:S(2)}, u32[]{:S(2)}) %collective-permute-start.11) | collective-permute-done | bytes 131104 | tf_op jit(solution)/shard_map/ppermute | solution.py:33
  118.5 9.7 %collective-permute-done.12.mid = f32[6,64,128]{2,1,0:T(8,128)S(1)} collective-permute-done((f32[6,64,128]{2,1,0:T(8,128)S(1)}, f32[6,64,128]{2,1,0:T(8,128)S(1)}, u32[]{:S(2)}, u32[]{:S(2)}) %collective-permute-start.12) | collective-permute-done | bytes 196640 | tf_op jit(solution)/shard_map/ppermute | solution.py:33
  128.3 2.0 %collective-permute-start.14 = (f32[4,64,128]{2,1,0:T(8,128)S(1)}, f32[4,64,128]{2,1,0:T(8,128)S(1)}, u32[]{:S(2)}, u32[]{:S(2)}) collective-permute-start(f32[4,64,128]{2,1,0:T(8,128)S(1)} %get-tuple-element.47), channel_id=1, source_target_pairs={{0,31},{1,0},{2,1},{3,2},{4,3},{5,4},{6,5},{7,6},{8,7},{9,8},{10,9... | collective-permute-start | bytes 393224 | tf_op jit(solution)/shard_map/ppermute | solution.py:33
  130.4 2.9 %collective-permute-done.13.low = f32[4,64,128]{2,1,0:T(8,128)S(1)} collective-permute-done((f32[4,64,128]{2,1,0:T(8,128)S(1)}, f32[4,64,128]{2,1,0:T(8,128)S(1)}, u32[]{:S(2)}, u32[]{:S(2)}) %collective-permute-start.13) | collective-permute-done | bytes 131104 | tf_op jit(solution)/shard_map/ppermute | solution.py:33
  133.3 4.3 %collective-permute-done.14.high = f32[4,64,128]{2,1,0:T(8,128)S(1)} collective-permute-done((f32[4,64,128]{2,1,0:T(8,128)S(1)}, f32[4,64,128]{2,1,0:T(8,128)S(1)}, u32[]{:S(2)}, u32[]{:S(2)}) %collective-permute-start.14) | collective-permute-done | bytes 131104 | tf_op jit(solution)/shard_map/ppermute | solution.py:33
  137.6 2.1 %shard_map.44 = (f32[6,64,128]{2,1,0:T(8,128)}, f32[5,5,64,128]{3,2,1,0:T(8,128)S(1)}) custom-call(s32[3]{0:T(128)S(1)} %pad_add_fusion.flags, f32[49,64,128]{2,1,0:T(8,128)S(1)} %get-tuple-element.38.ordered, f32[11,64,128]{2,1,0:T(8,128)S(1)} %get-tuple-element.34.mw, f32[11,64,128]{2,1,0:T(8,128)S(1)} %get-tuple-element.35.rw, ...), custom_call_target="tpu_custom_call" | custom-call | flops 1000000 | bytes 3801100 | tf_op jit(solution)/shard_map/pallas_call | solution.py:47
  139.6 2.6 %shard_map.45 = f32[1,3,8,128,128]{4,3,2,1,0:T(8,128)} custom-call(s32[3]{0:T(128)S(1)} %pad_add_fusion.flags, f32[8,128,128]{2,1,0:T(8,128)S(1)} %slice_bitcast_fusion.start, f32[8,128,128]{2,1,0:T(8,128)S(1)} %copy-done.6, f32[8,128,128]{2,1,0:T(8,128)} %get-tuple-element.27.b2, f32[8,128,128]{2,1,0:T(8,128)} %collective-permute-done.6.b_before, ...), custom_call_target="tpu_custom_call" | custom-call | flops 1000000 | bytes 4489228 | tf_op jit(solution)/shard_map/pallas_call | solution.py:47
  (39 shorter events, 9.5 us)
Async XLA Ops:
  0.0 3.4 %copy-start = (f32[1,3,8,128,128]{4,3,2,1,0:T(8,128)S(1)}, f32[1,3,8,128,128]{4,3,2,1,0:T(8,128)}, u32[]{:S(2)}) copy-start(f32[1,3,8,128,128]{4,3,2,1,0:T(8,128)} %param.3) | copy-start | bytes 4718596
  1.3 1.0 copy-start.1
  2.3 1.0 copy-start.3
  3.5 29.3 %copy-start.2 = (f32[8,128,128]{2,1,0:T(8,128)S(1)}, f32[8,128,128]{2,1,0:T(8,128)}, u32[]{:S(2)}) copy-start(f32[8,128,128]{2,1,0:T(8,128)} %mob.3) | copy-start | bytes 1572868
  3.5 29.3 %copy-start.4 = (f32[8,128,128]{2,1,0:T(8,128)S(1)}, f32[8,128,128]{2,1,0:T(8,128)}, u32[]{:S(2)}) copy-start(f32[8,128,128]{2,1,0:T(8,128)} %rea.3) | copy-start | bytes 1572868
  3.6 29.2 %collective-permute-start.1 = (f32[16,128,128]{2,1,0:T(8,128)S(1)}, f32[16,128,128]{2,1,0:T(8,128)S(1)}, u32[]{:S(2)}, u32[]{:S(2)}) collective-permute-start(f32[16,128,128]{2,1,0:T(8,128)S(1)} %pad_maximum_fusion), channel_id=1, source_target_pairs={{0,31},{1,0},{2,1},{3,2},{4,3},{5,4},{6,5},{7,6},{8,7},{9,8},{10,9... | collective-permute-start | bytes 3145736 | tf_op jit(solution)/shard_map/ppermute | solution.py:33
  4.5 26.3 %collective-permute-start = (f32[15,128,128]{2,1,0:T(8,128)S(1)}, f32[15,128,128]{2,1,0:T(8,128)S(1)}, u32[]{:S(2)}, u32[]{:S(2)}) collective-permute-start(f32[15,128,128]{2,1,0:T(8,128)S(1)} %pad_maximum_fusion.1), channel_id=1, source_target_pairs={{0,1},{1,2},{2,3},{3,4},{4,5},{5,6},{6,7},{7,8},{8,9},{9,10},{10,1... | collective-permute-start | bytes 2949128 | tf_op jit(solution)/shard_map/ppermute | solution.py:33
  39.2 15.0 %copy-start.5 = (f32[8,128,128]{2,1,0:T(8,128)}, f32[8,128,128]{2,1,0:T(8,128)S(1)}, u32[]{:S(2)}) copy-start(f32[8,128,128]{2,1,0:T(8,128)S(1)} %get-tuple-element.26.b1) | copy-start | bytes 1572868
  39.2 14.9 %collective-permute-start.3 = (f32[13,64,128]{2,1,0:T(8,128)S(1)}, f32[13,64,128]{2,1,0:T(8,128)S(1)}, u32[]{:S(2)}, u32[]{:S(2)}) collective-permute-start(f32[13,64,128]{2,1,0:T(8,128)S(1)} %get-tuple-element.33), channel_id=1, source_target_pairs={{0,31},{1,0},{2,1},{3,2},{4,3},{5,4},{6,5},{7,6},{8,7},{9,8},{10,9... | collective-permute-start | bytes 1277960 | tf_op jit(solution)/shard_map/ppermute | solution.py:33
  39.3 12.8 %collective-permute-start.2 = (f32[11,64,128]{2,1,0:T(8,128)S(1)}, f32[11,64,128]{2,1,0:T(8,128)S(1)}, u32[]{:S(2)}, u32[]{:S(2)}) collective-permute-start(f32[11,64,128]{2,1,0:T(8,128)S(1)} %get-tuple-element.32), channel_id=1, source_target_pairs={{0,1},{1,2},{2,3},{3,4},{4,5},{5,6},{6,7},{7,8},{8,9},{9,10},{10,1... | collective-permute-start | bytes 1081352 | tf_op jit(solution)/shard_map/ppermute | solution.py:33
  54.3 3.0 %collective-permute-start.4 = (f32[35,64,128]{2,1,0:T(8,128)S(1)}, f32[35,64,128]{2,1,0:T(8,128)}, u32[]{:S(2)}, u32[]{:S(2)}) collective-permute-start(f32[35,64,128]{2,1,0:T(8,128)S(1)} %shard_map.40.mine), channel_id=1, source_target_pairs={{0,32},{32,0},{64,96},{96,64},{128,160},{160,128},{192,224},{224,1... | collective-permute-start | bytes 3440648 | tf_op jit(solution)/shard_map/ppermute | solution.py:42
  54.4 18.5 %collective-permute-start.6 = (f32[8,128,128]{2,1,0:T(8,128)}, f32[8,128,128]{2,1,0:T(8,128)}, u32[]{:S(2)}, u32[]{:S(2)}) collective-permute-start(f32[8,128,128]{2,1,0:T(8,128)} %get-tuple-element.27.b2), channel_id=1, source_target_pairs={{0,32},{32,64},{64,96},{96,128},{128,160},{160,192},{192,224},{224... | collective-permute-start | bytes 1572872 | tf_op jit(solution)/shard_map/ppermute | solution.py:33
  59.5 13.7 %collective-permute-start.5 = (f32[6,64,128]{2,1,0:T(8,128)S(1)}, f32[6,64,128]{2,1,0:T(8,128)S(1)}, u32[]{:S(2)}, u32[]{:S(2)}) collective-permute-start(f32[6,64,128]{2,1,0:T(8,128)S(1)} %get-tuple-element.36), channel_id=1, source_target_pairs={{0,64},{32,96},{64,128},{96,160},{128,192},{160,224},{192,0},{224,... | collective-permute-start | bytes 589832 | tf_op jit(solution)/shard_map/ppermute | solution.py:33
  73.2 14.4 %collective-permute-start.7 = (f32[4,64,128]{2,1,0:T(8,128)S(1)}, f32[4,64,128]{2,1,0:T(8,128)S(1)}, u32[]{:S(2)}, u32[]{:S(2)}) collective-permute-start(f32[4,64,128]{2,1,0:T(8,128)S(1)} %get-tuple-element.52), channel_id=1, source_target_pairs={{0,1},{1,2},{2,3},{3,4},{4,5},{5,6},{6,7},{7,8},{8,9},{9,10},{10,1... | collective-permute-start | bytes 393224 | tf_op jit(solution)/shard_map/ppermute | solution.py:33
  84.6 10.1 %collective-permute-start.8 = (f32[4,64,128]{2,1,0:T(8,128)S(1)}, f32[4,64,128]{2,1,0:T(8,128)S(1)}, u32[]{:S(2)}, u32[]{:S(2)}) collective-permute-start(f32[4,64,128]{2,1,0:T(8,128)S(1)} %get-tuple-element.51), channel_id=1, source_target_pairs={{0,31},{1,0},{2,1},{3,2},{4,3},{5,4},{6,5},{7,6},{8,7},{9,8},{10,9... | collective-permute-start | bytes 393224 | tf_op jit(solution)/shard_map/ppermute | solution.py:33
  96.0 10.3 %collective-permute-start.9 = (f32[6,64,128]{2,1,0:T(8,128)S(1)}, f32[6,64,128]{2,1,0:T(8,128)S(1)}, u32[]{:S(2)}, u32[]{:S(2)}) collective-permute-start(f32[6,64,128]{2,1,0:T(8,128)S(1)} %shard_map.42), channel_id=1, source_target_pairs={{0,64},{32,96},{64,128},{96,160},{128,192},{160,224},{192,0},{224,... | collective-permute-start | bytes 589832 | tf_op jit(solution)/shard_map/ppermute | solution.py:33
  106.3 5.5 %collective-permute-start.10 = (f32[4,64,128]{2,1,0:T(8,128)S(1)}, f32[4,64,128]{2,1,0:T(8,128)S(1)}, u32[]{:S(2)}, u32[]{:S(2)}) collective-permute-start(f32[4,64,128]{2,1,0:T(8,128)S(1)} %get-tuple-element.50), channel_id=1, source_target_pairs={{0,1},{1,2},{2,3},{3,4},{4,5},{5,6},{6,7},{7,8},{8,9},{9,10},{10,1... | collective-permute-start | bytes 393224 | tf_op jit(solution)/shard_map/ppermute | solution.py:33
  106.4 9.9 %collective-permute-start.11 = (f32[4,64,128]{2,1,0:T(8,128)S(1)}, f32[4,64,128]{2,1,0:T(8,128)S(1)}, u32[]{:S(2)}, u32[]{:S(2)}) collective-permute-start(f32[4,64,128]{2,1,0:T(8,128)S(1)} %get-tuple-element.49), channel_id=1, source_target_pairs={{0,31},{1,0},{2,1},{3,2},{4,3},{5,4},{6,5},{7,6},{8,7},{9,8},{10,9... | collective-permute-start | bytes 393224 | tf_op jit(solution)/shard_map/ppermute | solution.py:33
  117.7 10.5 %collective-permute-start.12 = (f32[6,64,128]{2,1,0:T(8,128)S(1)}, f32[6,64,128]{2,1,0:T(8,128)S(1)}, u32[]{:S(2)}, u32[]{:S(2)}) collective-permute-start(f32[6,64,128]{2,1,0:T(8,128)S(1)} %shard_map.43), channel_id=1, source_target_pairs={{0,64},{32,96},{64,128},{96,160},{128,192},{160,224},{192,0},{224,... | collective-permute-start | bytes 589832 | tf_op jit(solution)/shard_map/ppermute | solution.py:33
  128.2 5.0 %collective-permute-start.13 = (f32[4,64,128]{2,1,0:T(8,128)S(1)}, f32[4,64,128]{2,1,0:T(8,128)S(1)}, u32[]{:S(2)}, u32[]{:S(2)}) collective-permute-start(f32[4,64,128]{2,1,0:T(8,128)S(1)} %get-tuple-element.48), channel_id=1, source_target_pairs={{0,1},{1,2},{2,3},{3,4},{4,5},{5,6},{6,7},{7,8},{8,9},{9,10},{10,1... | collective-permute-start | bytes 393224 | tf_op jit(solution)/shard_map/ppermute | solution.py:33
  128.3 9.3 %collective-permute-start.14 = (f32[4,64,128]{2,1,0:T(8,128)S(1)}, f32[4,64,128]{2,1,0:T(8,128)S(1)}, u32[]{:S(2)}, u32[]{:S(2)}) collective-permute-start(f32[4,64,128]{2,1,0:T(8,128)S(1)} %get-tuple-element.47), channel_id=1, source_target_pairs={{0,31},{1,0},{2,1},{3,2},{4,3},{5,4},{6,5},{7,6},{8,7},{9,8},{10,9... | collective-permute-start | bytes 393224 | tf_op jit(solution)/shard_map/ppermute | solution.py:33
  130.4 9.3 %copy-start.6 = (f32[8,128,128]{2,1,0:T(8,128)S(1)}, f32[8,128,128]{2,1,0:T(8,128)}, u32[]{:S(2)}) copy-start(f32[8,128,128]{2,1,0:T(8,128)} %copy-done.5) | copy-start | bytes 1572868

commit v3 on v2

v3 whole, which is shorter than its diff:
```python
import functools
import jax
import jax.numpy as jnp
from jax import lax
from jax.experimental import pallas as pl
from jax.experimental.pallas import tpu as pltpu
from jax.sharding import PartitionSpec as P

edge = 5.0 / 24.0
middle = 1.0 / 3.0
far = -1.0 / 24.0
substep = 0.5


def roll(values, amount, axis):
    return pltpu.roll(values, amount % values.shape[axis], axis)


def around(values):
    return roll(values, 1, 0) + roll(values, -1, 0) + roll(values, 1, 1) + roll(values, -1, 1)


def cubic(values):
    return values - values * values * values


def cost(flops, moved):
    return pl.CostEstimate(flops=flops, bytes_accessed=moved, transcendentals=0)


def ring(values, axis, distance):
    count = lax.axis_size(axis)
    return lax.ppermute(values, axis, [(i, (i + distance) % count) for i in range(count)])


def together(*values):
    return lax.optimization_barrier(values)


def swapped(values):
    count = lax.axis_size("tm")
    return lax.ppermute(values, "tm", [(i, i ^ 1) for i in range(count)])


def call(kernel, outs, scratch, *args, flops=10**6, scalars=0, limit=8):
    moved = sum(a.size * 4 for a in args) + sum(4 * functools.reduce(lambda x, y: x * y, s) for s in outs)
    result = pl.pallas_call(
        kernel,
        out_shape=[jax.ShapeDtypeStruct(s, jnp.float32) for s in outs],
        in_specs=[pl.BlockSpec(memory_space=pltpu.SMEM)] * scalars
        + [pl.BlockSpec(memory_space=pltpu.VMEM)] * (len(args) - scalars),
        out_specs=[pl.BlockSpec(memory_space=pltpu.VMEM) for _ in outs],
        scratch_shapes=[pltpu.VMEM(s, jnp.float32) for s in scratch],
        compiler_params=pltpu.CompilerParams(vmem_limit_bytes=limit * 1024 * 1024),
        cost_estimate=cost(flops, moved),
    )(*args)
    return result


def laplace(mid, *beside):
    total = around(mid) - 6.0 * mid
    for values in beside:
        total = total + values
    return total


def leading(x0, x1, x2):
    return edge * x0 + middle * x1 + far * x2


def trailing(x0, x1, x2):
    return far * x0 + (middle - substep) * x1 + edge * x2


def cubics(nodes, plane):
    return [cubic(nodes[m, plane]) for m in range(3)]


def edge_kernel(flags, nodes, mob, rea, own, rightward, leftward, mix):
    half = mob.shape[1] // 2
    for k, (source, scale) in enumerate(((mob, 0.125), (rea, 0.5))):
        for j in range(4):
            own[k, j] = scale * source[2 * j, pl.ds(0, half, stride=2), :]

    for core in range(2):

        @pl.when(flags[0] == core)
        def _():
            for j in range(3):
                for out in (rightward, leftward):
                    out[8 + j // 2, pl.ds(j % 2 * half, half), :] = own[core, j + 1]

    for out, outer, inner, third in ((rightward, 7, 6, 5), (leftward, 0, 1, 2)):
        lead = [leading(nodes[0, p], nodes[1, p], nodes[2, p]) for p in (outer, inner, third)]
        cubes = cubics(nodes, inner)
        out[0] = nodes[0, inner] + mob[inner] * laplace(lead[1], lead[0], lead[2]) + rea[inner] * leading(*cubes)
        cubes = cubics(nodes, outer)
        out[1] = nodes[0, outer] + mob[outer] * laplace(lead[0], lead[1]) + rea[outer] * leading(*cubes)
        out[4] = lead[0]
        trail = [trailing(nodes[0, p], nodes[1, p], nodes[2, p]) for p in (outer, inner)]
        out[2] = mob[outer] * laplace(trail[0], trail[1]) + rea[outer] * trailing(*cubes)
        out[5] = trail[0]
        out[3] = nodes[0, outer]
        out[6] = mob[outer]
        out[7] = rea[outer]
    mix[...] = 0.5 * nodes[0, 0] + 0.25 * nodes[0, 1]
    leftward[9, pl.ds(half, half), :] = reduced(mix)
    rightward[9, pl.ds(half, half), :] = jnp.zeros_like(own[0, 0])


def local_kernel(nodes, mob, rea, v1, step, first, lead, trail, start):
    for array in (lead, trail, start):
        for i in (0, 9):
            array[i] = jnp.zeros_like(array[i])

    @pl.loop(0, 8)
    def _(i):
        states = nodes[0, i], nodes[1, i], nodes[2, i]
        lead[i + 1] = leading(*states)
        trail[i + 1] = trailing(*states)
        start[i + 1] = states[0]

    @pl.loop(0, 8)
    def _(i):
        cubes = cubics(nodes, i)
        m = mob[i]
        r = rea[i]
        v1[i] = nodes[0, i] + m * laplace(lead[i + 1], lead[i], lead[i + 2]) + r * leading(*cubes)
        step[i] = m * laplace(trail[i + 1], trail[i], trail[i + 2]) + r * trailing(*cubes)
        first[i] = m * laplace(start[i + 1], start[i], start[i + 2]) + r * cubes[0]


def reduced(mix):
    half = mix.shape[0] // 2
    even = mix[pl.ds(0, half, stride=2), :]
    odd = mix[pl.ds(1, half, stride=2), :]
    return 0.5 * even + 0.25 * (odd + roll(odd, 1, 0))


def widen(d, wide, j):
    half = d.shape[0]
    wide[j, pl.ds(0, half, stride=2), :] = d
    wide[j, pl.ds(1, half, stride=2), :] = 0.5 * (d + roll(d, -1, 0))


def half_force(mid, low, high, mob, rea):
    planar = low + high + roll(mid, 1, 0) + roll(mid, -1, 0)
    vertical = roll(mid, 1, 1) + roll(mid, -1, 1)
    return mob * (planar + 4.0 * vertical - 12.0 * mid) + rea * cubic(mid)


def fine_kernel(
    nodes, mob, rea, left, right, to_right, to_left, own, v1_own, step_own, first_own,
    b1, b2, q, start, coarse, share, outer, rightward, leftward,
    mw, rw, v1, v2, step, first, f1, jj, mix,
):
    half = mob.shape[1] // 2

    @pl.loop(0, 8)
    def _(i):
        mw[i + 1] = mob[i]
        rw[i + 1] = rea[i]
        v1[i + 2] = v1_own[i]
        step[i + 1] = step_own[i]
        first[i] = first_own[i]

    for got, sent, place, far_place, beyond, plane in ((left, to_left, 1, 0, 0, 0), (right, to_right, 10, 11, 9, 7)):
        mw[beyond] = got[6]
        rw[beyond] = got[7]
        v1[far_place] = got[0]
        v1[place] = got[1] + got[6] * sent[4]
        step[beyond] = got[2] + got[6] * sent[5]
        v1[plane + 2] = v1_own[plane] + mob[plane] * got[4]
        step[plane + 1] = step_own[plane] + mob[plane] * got[5]
        first[plane] = first_own[plane] + mob[plane] * got[3]

    @pl.loop(0, 10, unroll=2)
    def _(i):
        a = v1[i + 1]
        force = mw[i] * laplace(a, v1[i], v1[i + 2]) + rw[i] * cubic(a)
        f1[i] = force
        v2[i] = a + (substep * force + step[i])

    @pl.loop(0, 8, unroll=2)
    def _(i):
        a = v2[i + 1]
        force = mob[i] * laplace(a, v2[i], v2[i + 2]) + rea[i] * cubic(a)
        second = middle * f1[i + 1]
        jj[0, i] = edge * first[i] + second + far * force
        jj[1, i] = far * first[i] + second + edge * force

    for j in range(4):
        before = nodes[0, 2 * j - 1] if j > 0 else left[3]
        mix[0] = 0.5 * nodes[0, 2 * j] + 0.25 * (nodes[0, 2 * j + 1] + before)
        mix[1] = 0.5 * v1[2 * j + 2] + 0.25 * (v1[2 * j + 3] + v1[2 * j + 1])
        mix[2] = 0.5 * v2[2 * j + 1] + 0.25 * (v2[2 * j + 2] + v2[2 * j])
        for m in range(2):
            mix[3 + m] = 0.5 * jj[m, 2 * j] + 0.25 * jj[m, 2 * j + 1]
            if j > 0:
                mix[3 + m] = mix[3 + m] + 0.25 * jj[m, 2 * j - 1]
        start[j] = reduced(mix.at[0])
        for m in range(2):
            coarse[m, j] = reduced(mix.at[1 + m])
            q[4 * m + j] = reduced(mix.at[3 + m])
    mix[0] = nodes[0, 7]
    start[4] = right[9, pl.ds(half, half), :] + 0.25 * reduced(mix.at[0])
    for m in range(2):
        mix[1 + m] = jj[m, 7]
        share[m] = 0.25 * reduced(mix.at[1 + m])

    outer[0] = 0.125 * right[6, pl.ds(0, half, stride=2), :]
    outer[1] = 0.5 * right[7, pl.ds(0, half, stride=2), :]
    for j in range(3):
        for side, got in enumerate((left, right)):
            outer[2 + 3 * side + j] = got[8 + j // 2, pl.ds(j % 2 * half, half), :]

    empty = jnp.zeros_like(share[0])
    for j in range(4):
        low = start[j - 1] if j > 0 else empty
        q[j] = q[j] - half_force(start[j], low, start[j + 1], own[0, j], own[1, j])
        low = coarse[0, j - 1] if j > 0 else empty
        high = coarse[0, j + 1] if j < 3 else empty
        q[4 + j] = q[4 + j] - half_force(coarse[0, j], low, high, own[0, j], own[1, j])

    for i in range(3):
        rightward[i] = q[1 + i]
        leftward[4 + i] = q[4 + i]
    for i in range(2):
        rightward[3 + i] = q[6 + i]
        rightward[10 + i] = share[i]
        leftward[11 + i] = coarse[i, 0]
    rightward[9] = coarse[0, 3]
    for i in range(4):
        rightward[5 + i] = start[i]
        leftward[i] = q[i]
        leftward[7 + i] = start[1 + i]

    for m, v, shift, b in ((0, v1, 2, b1), (1, v2, 1, b2)):
        for j in range(4):
            widen(coarse[m, j], mix, j)
        mix[4] = jnp.zeros_like(mix[4])
        for j in range(4):
            low = mix[j]
            b[2 * j] = v[2 * j + shift] - low
            b[2 * j + 1] = v[2 * j + 1 + shift] - 0.5 * (low + mix[j + 1])


def pack_kernel(q, start, c1, share, own, outer, from_left, from_right, window):
    window[0] = from_left[0]
    window[1] = from_left[1]
    window[2] = from_left[2]
    window[3] = q[0] + from_left[10] - own[0, 0] * from_left[8]
    for i in range(1, 4):
        window[3 + i] = q[i]
        window[7 + i] = from_right[i]
    window[7] = from_right[0] + share[0] - outer[0] * start[3]
    window[11] = from_left[3]
    window[12] = from_left[4]
    window[13] = q[4] + from_left[11] - own[0, 0] * from_left[9]
    window[14] = q[5]
    window[15] = q[6]
    window[16] = q[7] - own[0, 3] * from_right[11]
    window[17] = from_right[4] + share[1] - outer[0] * c1[3]
    window[18] = from_right[5]
    window[19] = from_right[6]
    for i in range(4):
        window[20 + i] = from_left[5 + i]
        window[29 + i] = from_right[7 + i]
    for i in range(5):
        window[24 + i] = start[i]
    for i in range(2):
        window[33 + i] = from_right[11 + i]
    for i in range(6):
        window[35 + i] = outer[2 + i]
    window[41] = c1[0]


def order(first, second, own, outer, out, mw, rw):
    for k, (source, coefficient) in enumerate(((first, mw), (second, rw))):
        for i in range(3):
            coefficient[i] = source[35 + i]
            coefficient[8 + i] = source[38 + i]
        for i in range(4):
            coefficient[3 + i] = own[k, i]
        coefficient[7] = outer[k]
    for i in range(20):
        out[i] = first[i]
    out[12] = first[12] - mw[2] * first[41]
    for i in range(7):
        out[20 + i] = second[2 + i]
    for i in range(5):
        out[27 + i] = second[13 + i]
    for i in range(2):
        out[32 + i] = first[33 + i]
        out[34 + i] = second[33 + i]
    for i in range(13):
        out[36 + i] = first[20 + i]


def sweep(x0, q, mw, rw, last, levels, x1, x2, x3):
    def level(source, target, count, terms, shift):
        for i in range(count):
            mid = source[i + 1]
            force = half_force(mid, source[i], source[i + 2], mw[i + shift], rw[i + shift])
            target[i] = mid + force + q[terms + i]

    level(x0, x1, 11, 0, 0)
    level(x1, x2, 9, 11, 1)
    level(x2, x3, 7, 20, 2)
    level(x3, last, 5, 27, 3)
    last[5] = q[35]
    if levels is not None:
        for i in range(4):
            levels[0, i] = x0[i + 4]
            levels[1, i] = x1[i + 3]
            levels[2, i] = x2[i + 2]
            levels[3, i] = x3[i + 1]
            levels[4, i] = last[i]
        levels[1, 4] = x1[7] - q[32]
        levels[2, 4] = x2[6] - q[33]
        levels[3, 4] = x3[5] - q[34]
        levels[4, 4] = last[4] - q[35]


def first_kernel(flags, mine, other, own, outer, last, ordered, mw, rw, x1, x2, x3):
    pl.when(flags[0] == 0)(lambda: order(mine, other, own, outer, ordered, mw, rw))
    pl.when(flags[0] != 0)(lambda: order(other, mine, own, outer, ordered, mw, rw))
    sweep(ordered.at[pl.ds(36, 13)], ordered, mw, rw, last, None, x1, x2, x3)


def turn_kernel(final, flags, ordered, mw, rw, mid, low, high, last, *refs):
    levels = refs[0] if final else None
    x0, x1, x2, x3 = refs[-4:]

    @pl.when(flags[1] == 0)
    def _():
        for i in range(13):
            x0[i] = ordered[36 + i]

    @pl.when(flags[1] != 0)
    def _():
        for i in range(4):
            x0[i] = low[i]
            x0[9 + i] = high[i]
        for i in range(5):
            x0[4 + i] = mid[i]

    sweep(x0, ordered, mw, rw, last, levels, x1, x2, x3)
    if final:
        levels[0, 4] = mid[4] - mid[5]


def final_kernel(flags, start, b1, b2, b_before, levels, out, wide):
    core = flags[0]
    for m, b in ((0, b_before), (1, b1), (2, b2)):

        def corrected(m=m, b=b):
            for j in range(5):
                widen(levels[2 * core + m, j], wide, j)
            for j in range(4):
                low = wide[j]
                out[0, m, 2 * j] = b[2 * j] + low
                out[0, m, 2 * j + 1] = b[2 * j + 1] + 0.5 * (low + wide[j + 1])

        if m == 0:
            pl.when(flags[2] != 0)(corrected)

            @pl.when(flags[2] == 0)
            def _():
                for i in range(8):
                    out[0, 0, i] = start[i]

        else:
            corrected()


def body(nodes, mobility, reaction):
    states = nodes[0]
    _, blocks, ny, nz = states.shape
    hy = ny // 2
    plane = (ny, nz)
    small = (hy, nz)
    slice_index = lax.axis_index("tm")
    flags = jnp.stack([slice_index % 2, slice_index // 2, slice_index]).astype(jnp.int32)

    own, to_right, to_left = call(
        edge_kernel, [(2, 4) + small, (10,) + plane, (10,) + plane], [plane], flags, states, mobility, reaction, scalars=1
    )
    left = ring(to_right, "space", 1)
    right = ring(to_left, "space", -1)
    v1, step, first = call(
        local_kernel, [(8,) + plane] * 3, [(10,) + plane] * 3, states, mobility, reaction, flops=10**7
    )
    b1, b2, q, start, coarse, share, outer, to_right, to_left = call(
        fine_kernel,
        [(8,) + plane, (8,) + plane, (8,) + small, (5,) + small, (2, 4) + small, (2,) + small, (8,) + small, (12,) + small,
         (13,) + small],
        [(10,) + plane, (10,) + plane, (12,) + plane, (10,) + plane, (10,) + plane, (8,) + plane, (10,) + plane,
         (2, 8) + plane, (5,) + plane],
        states, mobility, reaction, left, right, to_right, to_left, own, v1, step, first, flops=2 * 10**7, limit=16,
    )
    q_left = ring(to_right, "space", 1)
    q_right = ring(to_left, "space", -1)
    b_before = ring(b2, "tm", 1)
    (mine,) = call(pack_kernel, [(42,) + small], [], q, start, coarse[0], share, own, outer, q_left, q_right)
    other = swapped(mine)
    levels_shape = [(11,) + small, (9,) + small, (7,) + small]
    last, ordered, mw, rw = call(
        first_kernel, [(6,) + small, (49,) + small, (11,) + small, (11,) + small], levels_shape,
        flags, mine, other, own, outer, scalars=1,
    )
    turns = lax.axis_size("tm") // 2
    for turn in range(1, turns):
        final = turn == turns - 1
        mid = ring(last, "tm", 2)
        if turn == 1:
            mid, b_before = together(mid, b_before)
        low = ring(mid[0:4], "space", 1)
        high = ring(mid[1:5], "space", -1)
        last, *levels = call(
            functools.partial(turn_kernel, final), [(6,) + small] + [(5, 5) + small] * final, [(13,) + small] + levels_shape,
            flags, ordered, mw, rw, mid, low, high, scalars=1,
        )
    (out,) = call(
        final_kernel, [(1, 3, 8) + plane], [(5,) + plane], flags, states[0], b1, b2, b_before, levels[0], scalars=1,
    )
    return out


def solution(mesh):
    return jax.shard_map(
        body,
        mesh=mesh,
        in_specs=(
            P("tm", None, "space", None, None),
            P("space", None, None),
            P("space", None, None),
        ),
        out_specs=P("tm", None, "space", None, None),
        check_vma=False,
    )
```

time: 142 us -> 129 us (0.908)
  waiting for transfers between devices: 89 us -> 81.7 us
  starting transfers between devices: 33 us -> 30.2 us
  Pallas kernels: 16.1 us -> 13.7 us
    ppermute x14, waiting for transfers between devices: 86.7 us -> 79 us  [ring(): lax.ppermute(values, axis, [(i, (i + distance) % count) for i in range(co...]
    ppermute x14, starting transfers between devices: 33 us -> 30.1 us  [ring(): lax.ppermute(values, axis, [(i, (i + distance) % count) for i in range(co...]
    pallas_call x9, Pallas kernels: 16.1 us -> 13.7 us  [call(): pl.pallas_call(kernel, out_shape=[jax.ShapeDtypeStruct(s, jnp.float32) fo...]
    unnamed x14 -> x12, local copies, waits for them, and re-layouts: 2.1 us -> 3.5 us
where the time goes in v3:
time: 129 us
  waiting for transfers between devices  81.7 us (63%)
  starting transfers between devices  30.2 us (23%)
  Pallas kernels  13.7 us (11%)
  local copies, waits for them, and re-layouts  3.6 us (3%)
    ppermute x14, waiting for transfers between devices, ring(): lax.ppermute(values, axis, [(i, (i + distance) % count) for i in range(co...  79 us
    ppermute x14, starting transfers between devices, ring(): lax.ppermute(values, axis, [(i, (i + distance) % count) for i in range(co...  30.1 us
    pallas_call x9, Pallas kernels, call(): pl.pallas_call(kernel, out_shape=[jax.ShapeDtypeStruct(s, jnp.float32) fo...  13.7 us
    unnamed x12, local copies, waits for them, and re-layouts  3.5 us
    ppermute x1, waiting for transfers between devices, swapped(): return lax.ppermute(values, 'tm', [(i, i ^ 1) for i in range(count)])  2.62 us
  transfers between devices with their start and end apart: 15, of which 15 were waited for; matrix products, arithmetic and copies ran while one was open for 0% of the time, Pallas kernels for 2%

profile of v3, /device:TPU:30, one launch (start us, length us, event | category | flops | bytes accessed | tf_op | source)
XLA Modules:
  0.0 129.3 jit_solution(8730603427453705960)
XLA Ops:
  4.7 1.6 %collective-permute-start = (f32[10,128,128]{2,1,0:T(8,128)S(1)}, f32[10,128,128]{2,1,0:T(8,128)S(1)}, u32[]{:S(2)}, u32[]{:S(2)}) collective-permute-start(f32[10,128,128]{2,1,0:T(8,128)S(1)} %get-tuple-element.27.to_right), channel_id=1, source_target_pairs={{0,1},{1,2},{2,3},{3,4},{4,5},{5,6},{6,7},{7,8},{8,9},{9,10},{10,1... | collective-permute-start | bytes 1966088 | tf_op jit(solution)/shard_map/ppermute | solution.py:33
  6.8 1.7 %shard_map.38 = (f32[8,128,128]{2,1,0:T(8,128)S(1)}, f32[8,128,128]{2,1,0:T(8,128)S(1)}, f32[8,128,128]{2,1,0:T(8,128)S(1)}) custom-call(f32[3,8,128,128]{3,2,1,0:T(8,128)S(1)} %bitcast.9, f32[8,128,128]{2,1,0:T(8,128)S(1)} %copy-done.3, f32[8,128,128]{2,1,0:T(8,128)S(1)} %copy-done.5), custom_call_target="tpu_custom_call" | custom-call | flops 10000000 | bytes 4194304 | tf_op jit(solution)/shard_map/pallas_call | solution.py:47
  8.5 12.7 %collective-permute-done.left = f32[10,128,128]{2,1,0:T(8,128)S(1)} collective-permute-done((f32[10,128,128]{2,1,0:T(8,128)S(1)}, f32[10,128,128]{2,1,0:T(8,128)S(1)}, u32[]{:S(2)}, u32[]{:S(2)}) %collective-permute-start) | collective-permute-done | bytes 655392 | tf_op jit(solution)/shard_map/ppermute | solution.py:33
  21.2 5.4 %collective-permute-done.1.right = f32[10,128,128]{2,1,0:T(8,128)S(1)} collective-permute-done((f32[10,128,128]{2,1,0:T(8,128)S(1)}, f32[10,128,128]{2,1,0:T(8,128)S(1)}, u32[]{:S(2)}, u32[]{:S(2)}) %collective-permute-start.1) | collective-permute-done | bytes 655392 | tf_op jit(solution)/shard_map/ppermute | solution.py:33
  26.7 2.5 %shard_map.39 = (f32[8,128,128]{2,1,0:T(8,128)S(1)}, f32[8,128,128]{2,1,0:T(8,128)S(1)}, f32[8,64,128]{2,1,0:T(8,128)S(1)}, f32[5,64,128]{2,1,0:T(8,128)S(1)}, f...) custom-call(f32[3,8,128,128]{3,2,1,0:T(8,128)S(1)} %bitcast.10, ...), custom_call_target="tpu_custom_call" | custom-call | flops 20000000 | bytes 9961472 | tf_op jit(solution)/shard_map/pallas_call | solution.py:47
  29.2 6.2 %collective-permute-start.2 = (f32[12,64,128]{2,1,0:T(8,128)S(1)}, f32[12,64,128]{2,1,0:T(8,128)S(1)}, u32[]{:S(2)}, u32[]{:S(2)}) collective-permute-start(f32[12,64,128]{2,1,0:T(8,128)S(1)} %get-tuple-element.40), channel_id=1, source_target_pairs={{0,1},{1,2},{2,3},{3,4},{4,5},{5,6},{6,7},{7,8},{8,9},{9,10},{10,1... | collective-permute-start | bytes 1179656 | tf_op jit(solution)/shard_map/ppermute | solution.py:33
  35.5 6.9 %collective-permute-done.2.from_left = f32[12,64,128]{2,1,0:T(8,128)S(1)} collective-permute-done((f32[12,64,128]{2,1,0:T(8,128)S(1)}, f32[12,64,128]{2,1,0:T(8,128)S(1)}, u32[]{:S(2)}, u32[]{:S(2)}) %collective-permute-start.2) | collective-permute-done | bytes 393248 | tf_op jit(solution)/shard_map/ppermute | solution.py:33
  44.5 2.6 %collective-permute-done.4.other = f32[42,64,128]{2,1,0:T(8,128)S(1)} collective-permute-done((f32[42,64,128]{2,1,0:T(8,128)S(1)}, f32[42,64,128]{2,1,0:T(8,128)S(1)}, u32[]{:S(2)}, u32[]{:S(2)}) %collective-permute-start.4) | collective-permute-done | bytes 1376288 | tf_op jit(solution)/shard_map/ppermute | solution.py:42
  47.1 1.5 %shard_map.41 = (f32[6,64,128]{2,1,0:T(8,128)S(1)}, f32[49,64,128]{2,1,0:T(8,128)S(1)}, f32[11,64,128]{2,1,0:T(8,128)S(1)}, f32[11,64,128]{2,1,0:T(8,128)S(1)}) custom-call(s32[3]{0:T(128)S(1)} %pad_add_fusion.flags, f32[42,64,128]{2,1,0:T(8,128)S(1)} %shard_map.40.mine, f32[42,64,128]{2,1,0:T(8,128)S(1)} %collective-permute-done.4.other, ...), custom_call_target="tpu_custom_call" | custom-call | flops 1000000 | bytes 5799948 | tf_op jit(solution)/shard_map/pallas_call | solution.py:47
  48.7 3.3 %collective-permute-start.5 = (f32[6,64,128]{2,1,0:T(8,128)S(1)}, f32[6,64,128]{2,1,0:T(8,128)S(1)}, u32[]{:S(2)}, u32[]{:S(2)}) collective-permute-start(f32[6,64,128]{2,1,0:T(8,128)S(1)} %get-tuple-element.42), channel_id=1, source_target_pairs={{0,64},{32,96},{64,128},{96,160},{128,192},{160,224},{192,0},{224,... | collective-permute-start | bytes 589832 | tf_op jit(solution)/shard_map/ppermute | solution.py:33
  52.0 9.5 %collective-permute-done.6.b_before = f32[8,128,128]{2,1,0:T(8,128)S(1)} collective-permute-done((f32[8,128,128]{2,1,0:T(8,128)S(1)}, f32[8,128,128]{2,1,0:T(8,128)S(1)}, u32[]{:S(2)}, u32[]{:S(2)}) %collective-permute-start.6) | collective-permute-done | bytes 524320 | tf_op jit(solution)/shard_map/ppermute | solution.py:33
  61.8 11.9 %collective-permute-start.7 = (f32[4,64,128]{2,1,0:T(8,128)S(1)}, f32[4,64,128]{2,1,0:T(8,128)S(1)}, u32[]{:S(2)}, u32[]{:S(2)}) collective-permute-start(f32[4,64,128]{2,1,0:T(8,128)S(1)} %get-tuple-element.54), channel_id=1, source_target_pairs={{0,1},{1,2},{2,3},{3,4},{4,5},{5,6},{6,7},{7,8},{8,9},{9,10},{10,1... | collective-permute-start | bytes 393224 | tf_op jit(solution)/shard_map/ppermute | solution.py:33
  73.7 2.9 %collective-permute-done.7.low = f32[4,64,128]{2,1,0:T(8,128)S(1)} collective-permute-done((f32[4,64,128]{2,1,0:T(8,128)S(1)}, f32[4,64,128]{2,1,0:T(8,128)S(1)}, u32[]{:S(2)}, u32[]{:S(2)}) %collective-permute-start.7) | collective-permute-done | bytes 131104 | tf_op jit(solution)/shard_map/ppermute | solution.py:33
  76.6 7.0 %collective-permute-done.8.high = f32[4,64,128]{2,1,0:T(8,128)S(1)} collective-permute-done((f32[4,64,128]{2,1,0:T(8,128)S(1)}, f32[4,64,128]{2,1,0:T(8,128)S(1)}, u32[]{:S(2)}, u32[]{:S(2)}) %collective-permute-start.8) | collective-permute-done | bytes 131104 | tf_op jit(solution)/shard_map/ppermute | solution.py:33
  85.7 9.3 %collective-permute-done.9.mid = f32[6,64,128]{2,1,0:T(8,128)S(1)} collective-permute-done((f32[6,64,128]{2,1,0:T(8,128)S(1)}, f32[6,64,128]{2,1,0:T(8,128)S(1)}, u32[]{:S(2)}, u32[]{:S(2)}) %collective-permute-start.9) | collective-permute-done | bytes 196640 | tf_op jit(solution)/shard_map/ppermute | solution.py:33
  95.3 2.0 %collective-permute-start.11 = (f32[4,64,128]{2,1,0:T(8,128)S(1)}, f32[4,64,128]{2,1,0:T(8,128)S(1)}, u32[]{:S(2)}, u32[]{:S(2)}) collective-permute-start(f32[4,64,128]{2,1,0:T(8,128)S(1)} %get-tuple-element.51), channel_id=1, source_target_pairs={{0,31},{1,0},{2,1},{3,2},{4,3},{5,4},{6,5},{7,6},{8,7},{9,8},{10,9... | collective-permute-start | bytes 393224 | tf_op jit(solution)/shard_map/ppermute | solution.py:33
  97.3 3.0 %collective-permute-done.10.low = f32[4,64,128]{2,1,0:T(8,128)S(1)} collective-permute-done((f32[4,64,128]{2,1,0:T(8,128)S(1)}, f32[4,64,128]{2,1,0:T(8,128)S(1)}, u32[]{:S(2)}, u32[]{:S(2)}) %collective-permute-start.10) | collective-permute-done | bytes 131104 | tf_op jit(solution)/shard_map/ppermute | solution.py:33
  100.3 4.3 %collective-permute-done.11.high = f32[4,64,128]{2,1,0:T(8,128)S(1)} collective-permute-done((f32[4,64,128]{2,1,0:T(8,128)S(1)}, f32[4,64,128]{2,1,0:T(8,128)S(1)}, u32[]{:S(2)}, u32[]{:S(2)}) %collective-permute-start.11) | collective-permute-done | bytes 131104 | tf_op jit(solution)/shard_map/ppermute | solution.py:33
  107.0 7.0 %collective-permute-done.12.mid = f32[6,64,128]{2,1,0:T(8,128)S(1)} collective-permute-done((f32[6,64,128]{2,1,0:T(8,128)S(1)}, f32[6,64,128]{2,1,0:T(8,128)S(1)}, u32[]{:S(2)}, u32[]{:S(2)}) %collective-permute-start.12) | collective-permute-done | bytes 196640 | tf_op jit(solution)/shard_map/ppermute | solution.py:33
  114.0 2.1 %collective-permute-start.13 = (f32[4,64,128]{2,1,0:T(8,128)S(1)}, f32[4,64,128]{2,1,0:T(8,128)S(1)}, u32[]{:S(2)}, u32[]{:S(2)}) collective-permute-start(f32[4,64,128]{2,1,0:T(8,128)S(1)} %get-tuple-element.50), channel_id=1, source_target_pairs={{0,1},{1,2},{2,3},{3,4},{4,5},{5,6},{6,7},{7,8},{8,9},{9,10},{10,1... | collective-permute-start | bytes 393224 | tf_op jit(solution)/shard_map/ppermute | solution.py:33
  116.2 2.9 %collective-permute-done.13.low = f32[4,64,128]{2,1,0:T(8,128)S(1)} collective-permute-done((f32[4,64,128]{2,1,0:T(8,128)S(1)}, f32[4,64,128]{2,1,0:T(8,128)S(1)}, u32[]{:S(2)}, u32[]{:S(2)}) %collective-permute-start.13) | collective-permute-done | bytes 131104 | tf_op jit(solution)/shard_map/ppermute | solution.py:33
  119.1 6.2 %collective-permute-done.14.high = f32[4,64,128]{2,1,0:T(8,128)S(1)} collective-permute-done((f32[4,64,128]{2,1,0:T(8,128)S(1)}, f32[4,64,128]{2,1,0:T(8,128)S(1)}, u32[]{:S(2)}, u32[]{:S(2)}) %collective-permute-start.14) | collective-permute-done | bytes 131104 | tf_op jit(solution)/shard_map/ppermute | solution.py:33
  125.3 2.1 %shard_map.44 = (f32[6,64,128]{2,1,0:T(8,128)}, f32[5,5,64,128]{3,2,1,0:T(8,128)S(1)}) custom-call(s32[3]{0:T(128)S(1)} %pad_add_fusion.flags, f32[49,64,128]{2,1,0:T(8,128)S(1)} %get-tuple-element.44.ordered, f32[11,64,128]{2,1,0:T(8,128)S(1)} %get-tuple-element.45.mw, f32[11,64,128]{2,1,0:T(8,128)S(1)} %get-tuple-element.46.rw, ...), custom_call_target="tpu_custom_call" | custom-call | flops 1000000 | bytes 3801100 | tf_op jit(solution)/shard_map/pallas_call | solution.py:47
  127.4 1.9 %shard_map.45 = f32[1,3,8,128,128]{4,3,2,1,0:T(8,128)} custom-call(s32[3]{0:T(128)S(1)} %pad_add_fusion.flags, f32[8,128,128]{2,1,0:T(8,128)S(1)} %slice_bitcast_fusion.start, f32[8,128,128]{2,1,0:T(8,128)S(1)} %get-tuple-element.33.b1, f32[8,128,128]{2,1,0:T(8,128)S(1)} %get-tuple-element.34.b2, f32[8,128,128]{2,1,0:T(8,128)S(1)} %collective-permute-done.6.b_before, ...), custom_call_target="tpu_custom_call" | custom-call | flops 1000000 | bytes 4489228 | tf_op jit(solution)/shard_map/pallas_call | solution.py:47
  (33 shorter events, 12.5 us)
Async XLA Ops:
  0.1 1.4 %copy-start = (f32[1,3,8,128,128]{4,3,2,1,0:T(8,128)S(1)}, f32[1,3,8,128,128]{4,3,2,1,0:T(8,128)}, u32[]{:S(2)}) copy-start(f32[1,3,8,128,128]{4,3,2,1,0:T(8,128)} %param.3) | copy-start | bytes 4718596
  1.5 1.0 copy-start.2
  2.5 1.0 copy-start.4
  3.6 3.2 %copy-start.1 = (f32[1,3,8,128,128]{4,3,2,1,0:T(8,128)S(1)}, f32[1,3,8,128,128]{4,3,2,1,0:T(8,128)}, u32[]{:S(2)}) copy-start(f32[1,3,8,128,128]{4,3,2,1,0:T(8,128)} %param.3) | copy-start | bytes 4718596
  3.6 3.2 %copy-start.3 = (f32[8,128,128]{2,1,0:T(8,128)S(1)}, f32[8,128,128]{2,1,0:T(8,128)}, u32[]{:S(2)}) copy-start(f32[8,128,128]{2,1,0:T(8,128)} %mob.5) | copy-start | bytes 1572868
  3.6 3.2 %copy-start.5 = (f32[8,128,128]{2,1,0:T(8,128)S(1)}, f32[8,128,128]{2,1,0:T(8,128)}, u32[]{:S(2)}) copy-start(f32[8,128,128]{2,1,0:T(8,128)} %rea.5) | copy-start | bytes 1572868
  4.7 16.5 %collective-permute-start = (f32[10,128,128]{2,1,0:T(8,128)S(1)}, f32[10,128,128]{2,1,0:T(8,128)S(1)}, u32[]{:S(2)}, u32[]{:S(2)}) collective-permute-start(f32[10,128,128]{2,1,0:T(8,128)S(1)} %get-tuple-element.27.to_right), channel_id=1, source_target_pairs={{0,1},{1,2},{2,3},{3,4},{4,5},{5,6},{6,7},{7,8},{8,9},{9,10},{10,1... | collective-permute-start | bytes 1966088 | tf_op jit(solution)/shard_map/ppermute | solution.py:33
  6.2 20.4 %collective-permute-start.1 = (f32[10,128,128]{2,1,0:T(8,128)S(1)}, f32[10,128,128]{2,1,0:T(8,128)S(1)}, u32[]{:S(2)}, u32[]{:S(2)}) collective-permute-start(f32[10,128,128]{2,1,0:T(8,128)S(1)} %get-tuple-element.28.to_left), channel_id=1, source_target_pairs={{0,31},{1,0},{2,1},{3,2},{4,3},{5,4},{6,5},{7,6},{8,7},{9,8},{10,9... | collective-permute-start | bytes 1966088 | tf_op jit(solution)/shard_map/ppermute | solution.py:33
  29.2 14.7 %collective-permute-start.3 = (f32[13,64,128]{2,1,0:T(8,128)S(1)}, f32[13,64,128]{2,1,0:T(8,128)S(1)}, u32[]{:S(2)}, u32[]{:S(2)}) collective-permute-start(f32[13,64,128]{2,1,0:T(8,128)S(1)} %get-tuple-element.41), channel_id=1, source_target_pairs={{0,31},{1,0},{2,1},{3,2},{4,3},{5,4},{6,5},{7,6},{8,7},{9,8},{10,9... | collective-permute-start | bytes 1277960 | tf_op jit(solution)/shard_map/ppermute | solution.py:33
  29.2 13.1 %collective-permute-start.2 = (f32[12,64,128]{2,1,0:T(8,128)S(1)}, f32[12,64,128]{2,1,0:T(8,128)S(1)}, u32[]{:S(2)}, u32[]{:S(2)}) collective-permute-start(f32[12,64,128]{2,1,0:T(8,128)S(1)} %get-tuple-element.40), channel_id=1, source_target_pairs={{0,1},{1,2},{2,3},{3,4},{4,5},{5,6},{6,7},{7,8},{8,9},{9,10},{10,1... | collective-permute-start | bytes 1179656 | tf_op jit(solution)/shard_map/ppermute | solution.py:33
  43.9 3.2 %collective-permute-start.4 = (f32[42,64,128]{2,1,0:T(8,128)S(1)}, f32[42,64,128]{2,1,0:T(8,128)S(1)}, u32[]{:S(2)}, u32[]{:S(2)}) collective-permute-start(f32[42,64,128]{2,1,0:T(8,128)S(1)} %shard_map.40.mine), channel_id=1, source_target_pairs={{0,32},{32,0},{64,96},{96,64},{128,160},{160,128},{192,224},{224,1... | collective-permute-start | bytes 4128776 | tf_op jit(solution)/shard_map/ppermute | solution.py:42
  44.0 17.5 %collective-permute-start.6 = (f32[8,128,128]{2,1,0:T(8,128)S(1)}, f32[8,128,128]{2,1,0:T(8,128)S(1)}, u32[]{:S(2)}, u32[]{:S(2)}) collective-permute-start(f32[8,128,128]{2,1,0:T(8,128)S(1)} %get-tuple-element.34.b2), channel_id=1, source_target_pairs={{0,32},{32,64},{64,96},{96,128},{128,160},{160,192},{192,224},{224... | collective-permute-start | bytes 1572872 | tf_op jit(solution)/shard_map/ppermute | solution.py:33
  48.7 13.2 %collective-permute-start.5 = (f32[6,64,128]{2,1,0:T(8,128)S(1)}, f32[6,64,128]{2,1,0:T(8,128)S(1)}, u32[]{:S(2)}, u32[]{:S(2)}) collective-permute-start(f32[6,64,128]{2,1,0:T(8,128)S(1)} %get-tuple-element.42), channel_id=1, source_target_pairs={{0,64},{32,96},{64,128},{96,160},{128,192},{160,224},{192,0},{224,... | collective-permute-start | bytes 589832 | tf_op jit(solution)/shard_map/ppermute | solution.py:33
  61.8 14.8 %collective-permute-start.7 = (f32[4,64,128]{2,1,0:T(8,128)S(1)}, f32[4,64,128]{2,1,0:T(8,128)S(1)}, u32[]{:S(2)}, u32[]{:S(2)}) collective-permute-start(f32[4,64,128]{2,1,0:T(8,128)S(1)} %get-tuple-element.54), channel_id=1, source_target_pairs={{0,1},{1,2},{2,3},{3,4},{4,5},{5,6},{6,7},{7,8},{8,9},{9,10},{10,1... | collective-permute-start | bytes 393224 | tf_op jit(solution)/shard_map/ppermute | solution.py:33
  73.7 10.0 %collective-permute-start.8 = (f32[4,64,128]{2,1,0:T(8,128)S(1)}, f32[4,64,128]{2,1,0:T(8,128)S(1)}, u32[]{:S(2)}, u32[]{:S(2)}) collective-permute-start(f32[4,64,128]{2,1,0:T(8,128)S(1)} %get-tuple-element.53), channel_id=1, source_target_pairs={{0,31},{1,0},{2,1},{3,2},{4,3},{5,4},{6,5},{7,6},{8,7},{9,8},{10,9... | collective-permute-start | bytes 393224 | tf_op jit(solution)/shard_map/ppermute | solution.py:33
  85.1 9.9 %collective-permute-start.9 = (f32[6,64,128]{2,1,0:T(8,128)S(1)}, f32[6,64,128]{2,1,0:T(8,128)S(1)}, u32[]{:S(2)}, u32[]{:S(2)}) collective-permute-start(f32[6,64,128]{2,1,0:T(8,128)S(1)} %shard_map.42), channel_id=1, source_target_pairs={{0,64},{32,96},{64,128},{96,160},{128,192},{160,224},{192,0},{224,... | collective-permute-start | bytes 589832 | tf_op jit(solution)/shard_map/ppermute | solution.py:33
  95.0 5.3 %collective-permute-start.10 = (f32[4,64,128]{2,1,0:T(8,128)S(1)}, f32[4,64,128]{2,1,0:T(8,128)S(1)}, u32[]{:S(2)}, u32[]{:S(2)}) collective-permute-start(f32[4,64,128]{2,1,0:T(8,128)S(1)} %get-tuple-element.52), channel_id=1, source_target_pairs={{0,1},{1,2},{2,3},{3,4},{4,5},{5,6},{6,7},{7,8},{8,9},{9,10},{10,1... | collective-permute-start | bytes 393224 | tf_op jit(solution)/shard_map/ppermute | solution.py:33
  95.3 9.3 %collective-permute-start.11 = (f32[4,64,128]{2,1,0:T(8,128)S(1)}, f32[4,64,128]{2,1,0:T(8,128)S(1)}, u32[]{:S(2)}, u32[]{:S(2)}) collective-permute-start(f32[4,64,128]{2,1,0:T(8,128)S(1)} %get-tuple-element.51), channel_id=1, source_target_pairs={{0,31},{1,0},{2,1},{3,2},{4,3},{5,4},{6,5},{7,6},{8,7},{9,8},{10,9... | collective-permute-start | bytes 393224 | tf_op jit(solution)/shard_map/ppermute | solution.py:33
  106.0 8.0 %collective-permute-start.12 = (f32[6,64,128]{2,1,0:T(8,128)S(1)}, f32[6,64,128]{2,1,0:T(8,128)S(1)}, u32[]{:S(2)}, u32[]{:S(2)}) collective-permute-start(f32[6,64,128]{2,1,0:T(8,128)S(1)} %shard_map.43), channel_id=1, source_target_pairs={{0,64},{32,96},{64,128},{96,160},{128,192},{160,224},{192,0},{224,... | collective-permute-start | bytes 589832 | tf_op jit(solution)/shard_map/ppermute | solution.py:33
  114.0 5.0 %collective-permute-start.13 = (f32[4,64,128]{2,1,0:T(8,128)S(1)}, f32[4,64,128]{2,1,0:T(8,128)S(1)}, u32[]{:S(2)}, u32[]{:S(2)}) collective-permute-start(f32[4,64,128]{2,1,0:T(8,128)S(1)} %get-tuple-element.50), channel_id=1, source_target_pairs={{0,1},{1,2},{2,3},{3,4},{4,5},{5,6},{6,7},{7,8},{8,9},{9,10},{10,1... | collective-permute-start | bytes 393224 | tf_op jit(solution)/shard_map/ppermute | solution.py:33
  116.1 9.2 %collective-permute-start.14 = (f32[4,64,128]{2,1,0:T(8,128)S(1)}, f32[4,64,128]{2,1,0:T(8,128)S(1)}, u32[]{:S(2)}, u32[]{:S(2)}) collective-permute-start(f32[4,64,128]{2,1,0:T(8,128)S(1)} %get-tuple-element.49), channel_id=1, source_target_pairs={{0,31},{1,0},{2,1},{3,2},{4,3},{5,4},{6,5},{7,6},{8,7},{9,8},{10,9... | collective-permute-start | bytes 393224 | tf_op jit(solution)/shard_map/ppermute | solution.py:33

commit v4 on v3

--- a/solution.py
+++ b/solution.py
@@ -76,8 +76,17 @@
     return [cubic(nodes[m, plane]) for m in range(3)]
 
 
-def edge_kernel(flags, nodes, mob, rea, own, rightward, leftward, mix):
+def edge_kernel(flags, nodes_hbm, mob_hbm, rea_hbm, own, rightward, leftward, mix, nodes, mob, rea, sems):
     half = mob.shape[1] // 2
+    copies = [pltpu.make_async_copy(mob_hbm, mob, sems.at[0]), pltpu.make_async_copy(rea_hbm, rea, sems.at[1])]
+    for m in range(3):
+        for k, first in enumerate((5, 0)):
+            part = pl.ds(first, 3)
+            copies.append(pltpu.make_async_copy(nodes_hbm.at[m, part], nodes.at[m, part], sems.at[2 + 2 * m + k]))
+    for copy in copies:
+        copy.start()
+    for copy in copies[:2]:
+        copy.wait()
     for k, (source, scale) in enumerate(((mob, 0.125), (rea, 0.5))):
         for j in range(4):
             own[k, j] = scale * source[2 * j, pl.ds(0, half, stride=2), :]
@@ -89,6 +98,9 @@
             for j in range(3):
                 for out in (rightward, leftward):
                     out[8 + j // 2, pl.ds(j % 2 * half, half), :] = own[core, j + 1]
+
+    for copy in copies[2:]:
+        copy.wait()
 
     for out, outer, inner, third in ((rightward, 7, 6, 5), (leftward, 0, 1, 2)):
         lead = [leading(nodes[0, p], nodes[1, p], nodes[2, p]) for p in (outer, inner, third)]
@@ -308,7 +320,8 @@
     level(x1, x2, 9, 11, 1)
     level(x2, x3, 7, 20, 2)
     level(x3, last, 5, 27, 3)
-    last[5] = q[35]
+    if last.shape[0] > 5:
+        last[5] = q[35]
     if levels is not None:
         for i in range(4):
             levels[0, i] = x0[i + 4]
@@ -383,9 +396,16 @@
     slice_index = lax.axis_index("tm")
     flags = jnp.stack([slice_index % 2, slice_index // 2, slice_index]).astype(jnp.int32)
 
-    own, to_right, to_left = call(
-        edge_kernel, [(2, 4) + small, (10,) + plane, (10,) + plane], [plane], flags, states, mobility, reaction, scalars=1
-    )
+    own, to_right, to_left = pl.pallas_call(
+        edge_kernel,
+        out_shape=[jax.ShapeDtypeStruct(s, jnp.float32) for s in ((2, 4) + small, (10,) + plane, (10,) + plane)],
+        in_specs=[pl.BlockSpec(memory_space=pltpu.SMEM)] + [pl.BlockSpec(memory_space=pltpu.HBM)] * 3,
+        out_specs=[pl.BlockSpec(memory_space=pltpu.VMEM)] * 3,
+        scratch_shapes=[pltpu.VMEM(s, jnp.float32) for s in (plane, (3, 8) + plane, (8,) + plane, (8,) + plane)]
+        + [pltpu.SemaphoreType.DMA((8,))],
+        compiler_params=pltpu.CompilerParams(vmem_limit_bytes=8 * 1024 * 1024),
+        cost_estimate=cost(10**6, 4 * 10**6),
+    )(flags, *(pltpu.with_memory_space_constraint(a, pltpu.HBM) for a in (states, mobility, reaction)))
     left = ring(to_right, "space", 1)
     right = ring(to_left, "space", -1)
     v1, step, first = call(
@@ -406,19 +426,19 @@
     other = swapped(mine)
     levels_shape = [(11,) + small, (9,) + small, (7,) + small]
     last, ordered, mw, rw = call(
-        first_kernel, [(6,) + small, (49,) + small, (11,) + small, (11,) + small], levels_shape,
+        first_kernel, [(5,) + small, (49,) + small, (11,) + small, (11,) + small], levels_shape,
         flags, mine, other, own, outer, scalars=1,
     )
     turns = lax.axis_size("tm") // 2
     for turn in range(1, turns):
         final = turn == turns - 1
         mid = ring(last, "tm", 2)
-        if turn == 1:
-            mid, b_before = together(mid, b_before)
         low = ring(mid[0:4], "space", 1)
         high = ring(mid[1:5], "space", -1)
+        if turn == 1:
+            low, high, b_before = together(low, high, b_before)
         last, *levels = call(
-            functools.partial(turn_kernel, final), [(6,) + small] + [(5, 5) + small] * final, [(13,) + small] + levels_shape,
+            functools.partial(turn_kernel, final), [(6 if turn == turns - 2 else 5,) + small] + [(5, 5) + small] * final, [(13,) + small] + levels_shape,
             flags, ordered, mw, rw, mid, low, high, scalars=1,
         )
     (out,) = call(

time: 129 us -> 125 us (0.969)
  waiting for transfers between devices: 81.7 us -> 78.2 us
  local copies, waits for them, and re-layouts: 3.6 us -> 0.11 us
  Pallas kernels: 13.7 us -> 15.3 us
    ppermute x14, waiting for transfers between devices: 79 us -> 75.1 us  [ring(): lax.ppermute(values, axis, [(i, (i + distance) % count) for i in range(co...]
    unnamed x12 -> x6, local copies, waits for them, and re-layouts: 3.5 us -> 0.01 us
    pallas_call x0 -> x1, Pallas kernels: none -> 2.77 us  [body(): pl.pallas_call(edge_kernel, out_shape=[jax.ShapeDtypeStruct(s, jnp.float3...]
    pallas_call x9 -> x8, Pallas kernels: 13.7 us -> 12.5 us  [call(): pl.pallas_call(kernel, out_shape=[jax.ShapeDtypeStruct(s, jnp.float32) fo...]
  transfers between devices with their start and end apart: 15 -> 15, of which waited for: 15 -> 14; matrix products, arithmetic and copies ran while one was open for 0% -> 0% of each run, Pallas kernels for 2% -> 1%
where the time goes in v4:
time: 125 us
  waiting for transfers between devices  78.2 us (63%)
  starting transfers between devices  30.8 us (25%)
  Pallas kernels  15.3 us (12%)
    ppermute x14, waiting for transfers between devices, ring(): lax.ppermute(values, axis, [(i, (i + distance) % count) for i in range(co...  75.1 us
    ppermute x14, starting transfers between devices, ring(): lax.ppermute(values, axis, [(i, (i + distance) % count) for i in range(co...  30.7 us
    pallas_call x8, Pallas kernels, call(): pl.pallas_call(kernel, out_shape=[jax.ShapeDtypeStruct(s, jnp.float32) fo...  12.5 us
    ppermute x1, waiting for transfers between devices, swapped(): return lax.ppermute(values, 'tm', [(i, i ^ 1) for i in range(count)])  3.12 us
    pallas_call x1, Pallas kernels, body(): pl.pallas_call(edge_kernel, out_shape=[jax.ShapeDtypeStruct(s, jnp.float3...  2.77 us
  transfers between devices with their start and end apart: 15, of which 14 were waited for; matrix products, arithmetic and copies ran while one was open for 0% of the time, Pallas kernels for 1%

profile of v4, /device:TPU:30, one launch (start us, length us, event | category | flops | bytes accessed | tf_op | source)
XLA Modules:
  0.0 124.6 jit_solution(3045378709915788350)
XLA Ops:
  0.1 2.8 %shard_map.37 = (f32[2,4,64,128]{3,2,1,0:T(8,128)S(1)}, f32[10,128,128]{2,1,0:T(8,128)S(1)}, f32[10,128,128]{2,1,0:T(8,128)S(1)}) custom-call(s32[3]{0:T(128)S(1)} %pad_add_fusion.flags, f32[3,8,128,128]{3,2,1,0:T(8,128)} %bitcast.8, f32[8,128,128]{2,1,0:T(8,128)} %mob.3, f32[8,128,128]{2,1,0:T(8,128)} %rea.3), custom_call_target="tpu_custom_call" | custom-call | flops 1000000 | bytes 4000000 | tf_op jit(solution)/shard_map/pallas_call | solution.py:399
  2.9 1.6 %collective-permute-start = (f32[10,128,128]{2,1,0:T(8,128)S(1)}, f32[10,128,128]{2,1,0:T(8,128)S(1)}, u32[]{:S(2)}, u32[]{:S(2)}) collective-permute-start(f32[10,128,128]{2,1,0:T(8,128)S(1)} %get-tuple-element.28.to_right), channel_id=1, source_target_pairs={{0,1},{1,2},{2,3},{3,4},{4,5},{5,6},{6,7},{7,8},{8,9},{9,10},{10,1... | collective-permute-start | bytes 1966088 | tf_op jit(solution)/shard_map/ppermute | solution.py:33
  5.0 1.7 %shard_map.38 = (f32[8,128,128]{2,1,0:T(8,128)S(1)}, f32[8,128,128]{2,1,0:T(8,128)S(1)}, f32[8,128,128]{2,1,0:T(8,128)S(1)}) custom-call(f32[3,8,128,128]{3,2,1,0:T(8,128)S(1)} %bitcast.9, f32[8,128,128]{2,1,0:T(8,128)S(1)} %copy-done.1, f32[8,128,128]{2,1,0:T(8,128)S(1)} %copy-done.2), custom_call_target="tpu_custom_call" | custom-call | flops 10000000 | bytes 4194304 | tf_op jit(solution)/shard_map/pallas_call | solution.py:47
  6.7 12.7 %collective-permute-done.left = f32[10,128,128]{2,1,0:T(8,128)S(1)} collective-permute-done((f32[10,128,128]{2,1,0:T(8,128)S(1)}, f32[10,128,128]{2,1,0:T(8,128)S(1)}, u32[]{:S(2)}, u32[]{:S(2)}) %collective-permute-start) | collective-permute-done | bytes 655392 | tf_op jit(solution)/shard_map/ppermute | solution.py:33
  19.4 5.4 %collective-permute-done.1.right = f32[10,128,128]{2,1,0:T(8,128)S(1)} collective-permute-done((f32[10,128,128]{2,1,0:T(8,128)S(1)}, f32[10,128,128]{2,1,0:T(8,128)S(1)}, u32[]{:S(2)}, u32[]{:S(2)}) %collective-permute-start.1) | collective-permute-done | bytes 655392 | tf_op jit(solution)/shard_map/ppermute | solution.py:33
  24.9 2.5 %shard_map.39 = (f32[8,128,128]{2,1,0:T(8,128)S(1)}, f32[8,128,128]{2,1,0:T(8,128)S(1)}, f32[8,64,128]{2,1,0:T(8,128)S(1)}, f32[5,64,128]{2,1,0:T(8,128)S(1)}, f...) custom-call(f32[3,8,128,128]{3,2,1,0:T(8,128)S(1)} %bitcast.10, ...), custom_call_target="tpu_custom_call" | custom-call | flops 20000000 | bytes 9961472 | tf_op jit(solution)/shard_map/pallas_call | solution.py:47
  27.4 6.2 %collective-permute-start.2 = (f32[12,64,128]{2,1,0:T(8,128)S(1)}, f32[12,64,128]{2,1,0:T(8,128)S(1)}, u32[]{:S(2)}, u32[]{:S(2)}) collective-permute-start(f32[12,64,128]{2,1,0:T(8,128)S(1)} %get-tuple-element.41), channel_id=1, source_target_pairs={{0,1},{1,2},{2,3},{3,4},{4,5},{5,6},{6,7},{7,8},{8,9},{9,10},{10,1... | collective-permute-start | bytes 1179656 | tf_op jit(solution)/shard_map/ppermute | solution.py:33
  33.7 6.9 %collective-permute-done.2.from_left = f32[12,64,128]{2,1,0:T(8,128)S(1)} collective-permute-done((f32[12,64,128]{2,1,0:T(8,128)S(1)}, f32[12,64,128]{2,1,0:T(8,128)S(1)}, u32[]{:S(2)}, u32[]{:S(2)}) %collective-permute-start.2) | collective-permute-done | bytes 393248 | tf_op jit(solution)/shard_map/ppermute | solution.py:33
  42.2 3.1 %collective-permute-done.4.other = f32[42,64,128]{2,1,0:T(8,128)S(1)} collective-permute-done((f32[42,64,128]{2,1,0:T(8,128)S(1)}, f32[42,64,128]{2,1,0:T(8,128)S(1)}, u32[]{:S(2)}, u32[]{:S(2)}) %collective-permute-start.4) | collective-permute-done | bytes 1376288 | tf_op jit(solution)/shard_map/ppermute | solution.py:42
  45.4 1.5 %shard_map.41 = (f32[5,64,128]{2,1,0:T(8,128)S(1)}, f32[49,64,128]{2,1,0:T(8,128)S(1)}, f32[11,64,128]{2,1,0:T(8,128)S(1)}, f32[11,64,128]{2,1,0:T(8,128)S(1)}) custom-call(s32[3]{0:T(128)S(1)} %pad_add_fusion.flags, f32[42,64,128]{2,1,0:T(8,128)S(1)} %shard_map.40.mine, f32[42,64,128]{2,1,0:T(8,128)S(1)} %collective-permute-done.4.other, ...), custom_call_target="tpu_custom_call" | custom-call | flops 1000000 | bytes 5767180 | tf_op jit(solution)/shard_map/pallas_call | solution.py:47
  46.9 3.3 %collective-permute-start.5 = (f32[5,64,128]{2,1,0:T(8,128)S(1)}, f32[5,64,128]{2,1,0:T(8,128)S(1)}, u32[]{:S(2)}, u32[]{:S(2)}) collective-permute-start(f32[5,64,128]{2,1,0:T(8,128)S(1)} %get-tuple-element.43), channel_id=1, source_target_pairs={{0,64},{32,96},{64,128},{96,160},{128,192},{160,224},{192,0},{224,... | collective-permute-start | bytes 491528 | tf_op jit(solution)/shard_map/ppermute | solution.py:33
  50.2 8.7 %collective-permute-done.5.mid = f32[5,64,128]{2,1,0:T(8,128)S(1)} collective-permute-done((f32[5,64,128]{2,1,0:T(8,128)S(1)}, f32[5,64,128]{2,1,0:T(8,128)S(1)}, u32[]{:S(2)}, u32[]{:S(2)}) %collective-permute-start.5) | collective-permute-done | bytes 163872 | tf_op jit(solution)/shard_map/ppermute | solution.py:33
  59.0 12.9 %collective-permute-start.6 = (f32[4,64,128]{2,1,0:T(8,128)S(1)}, f32[4,64,128]{2,1,0:T(8,128)S(1)}, u32[]{:S(2)}, u32[]{:S(2)}) collective-permute-start(f32[4,64,128]{2,1,0:T(8,128)S(1)} %get-tuple-element.56), channel_id=1, source_target_pairs={{0,1},{1,2},{2,3},{3,4},{4,5},{5,6},{6,7},{7,8},{8,9},{9,10},{10,1... | collective-permute-start | bytes 393224 | tf_op jit(solution)/shard_map/ppermute | solution.py:33
  71.9 2.5 %collective-permute-done.6.low = f32[4,64,128]{2,1,0:T(8,128)S(1)} collective-permute-done((f32[4,64,128]{2,1,0:T(8,128)S(1)}, f32[4,64,128]{2,1,0:T(8,128)S(1)}, u32[]{:S(2)}, u32[]{:S(2)}) %collective-permute-start.6) | collective-permute-done | bytes 131104 | tf_op jit(solution)/shard_map/ppermute | solution.py:33
  74.4 6.7 %collective-permute-done.7.high = f32[4,64,128]{2,1,0:T(8,128)S(1)} collective-permute-done((f32[4,64,128]{2,1,0:T(8,128)S(1)}, f32[4,64,128]{2,1,0:T(8,128)S(1)}, u32[]{:S(2)}, u32[]{:S(2)}) %collective-permute-start.7) | collective-permute-done | bytes 131104 | tf_op jit(solution)/shard_map/ppermute | solution.py:33
  83.2 7.5 %collective-permute-done.9.mid = f32[5,64,128]{2,1,0:T(8,128)S(1)} collective-permute-done((f32[5,64,128]{2,1,0:T(8,128)S(1)}, f32[5,64,128]{2,1,0:T(8,128)S(1)}, u32[]{:S(2)}, u32[]{:S(2)}) %collective-permute-start.9) | collective-permute-done | bytes 163872 | tf_op jit(solution)/shard_map/ppermute | solution.py:33
  91.5 1.5 %collective-permute-start.11 = (f32[4,64,128]{2,1,0:T(8,128)S(1)}, f32[4,64,128]{2,1,0:T(8,128)S(1)}, u32[]{:S(2)}, u32[]{:S(2)}) collective-permute-start(f32[4,64,128]{2,1,0:T(8,128)S(1)} %get-tuple-element.53), channel_id=1, source_target_pairs={{0,31},{1,0},{2,1},{3,2},{4,3},{5,4},{6,5},{7,6},{8,7},{9,8},{10,9... | collective-permute-start | bytes 393224 | tf_op jit(solution)/shard_map/ppermute | solution.py:33
  93.0 2.9 %collective-permute-done.10.low = f32[4,64,128]{2,1,0:T(8,128)S(1)} collective-permute-done((f32[4,64,128]{2,1,0:T(8,128)S(1)}, f32[4,64,128]{2,1,0:T(8,128)S(1)}, u32[]{:S(2)}, u32[]{:S(2)}) %collective-permute-start.10) | collective-permute-done | bytes 131104 | tf_op jit(solution)/shard_map/ppermute | solution.py:33
  96.0 4.7 %collective-permute-done.11.high = f32[4,64,128]{2,1,0:T(8,128)S(1)} collective-permute-done((f32[4,64,128]{2,1,0:T(8,128)S(1)}, f32[4,64,128]{2,1,0:T(8,128)S(1)}, u32[]{:S(2)}, u32[]{:S(2)}) %collective-permute-start.11) | collective-permute-done | bytes 131104 | tf_op jit(solution)/shard_map/ppermute | solution.py:33
  103.0 7.1 %collective-permute-done.12.mid = f32[6,64,128]{2,1,0:T(8,128)S(1)} collective-permute-done((f32[6,64,128]{2,1,0:T(8,128)S(1)}, f32[6,64,128]{2,1,0:T(8,128)S(1)}, u32[]{:S(2)}, u32[]{:S(2)}) %collective-permute-start.12) | collective-permute-done | bytes 196640 | tf_op jit(solution)/shard_map/ppermute | solution.py:33
  112.2 2.9 %collective-permute-done.13.low = f32[4,64,128]{2,1,0:T(8,128)S(1)} collective-permute-done((f32[4,64,128]{2,1,0:T(8,128)S(1)}, f32[4,64,128]{2,1,0:T(8,128)S(1)}, u32[]{:S(2)}, u32[]{:S(2)}) %collective-permute-start.13) | collective-permute-done | bytes 131104 | tf_op jit(solution)/shard_map/ppermute | solution.py:33
  115.1 5.6 %collective-permute-done.14.high = f32[4,64,128]{2,1,0:T(8,128)S(1)} collective-permute-done((f32[4,64,128]{2,1,0:T(8,128)S(1)}, f32[4,64,128]{2,1,0:T(8,128)S(1)}, u32[]{:S(2)}, u32[]{:S(2)}) %collective-permute-start.14) | collective-permute-done | bytes 131104 | tf_op jit(solution)/shard_map/ppermute | solution.py:33
  120.7 2.1 %shard_map.44 = (f32[5,64,128]{2,1,0:T(8,128)}, f32[5,5,64,128]{3,2,1,0:T(8,128)S(1)}) custom-call(s32[3]{0:T(128)S(1)} %pad_add_fusion.flags, f32[49,64,128]{2,1,0:T(8,128)S(1)} %get-tuple-element.45.ordered, f32[11,64,128]{2,1,0:T(8,128)S(1)} %get-tuple-element.46.mw, f32[11,64,128]{2,1,0:T(8,128)S(1)} %get-tuple-element.47.rw, ...), custom_call_target="tpu_custom_call" | custom-call | flops 1000000 | bytes 3768332 | tf_op jit(solution)/shard_map/pallas_call | solution.py:47
  122.8 1.9 %shard_map.45 = f32[1,3,8,128,128]{4,3,2,1,0:T(8,128)} custom-call(s32[3]{0:T(128)S(1)} %pad_add_fusion.flags, f32[8,128,128]{2,1,0:T(8,128)S(1)} %slice_bitcast_fusion.start, f32[8,128,128]{2,1,0:T(8,128)S(1)} %get-tuple-element.34.b1, f32[8,128,128]{2,1,0:T(8,128)S(1)} %get-tuple-element.35.b2, f32[8,128,128]{2,1,0:T(8,128)S(1)} %collective-permute-done.8.b_before, ...), custom_call_target="tpu_custom_call" | custom-call | flops 1000000 | bytes 4489228 | tf_op jit(solution)/shard_map/pallas_call | solution.py:47
  (27 shorter events, 9.7 us)
Async XLA Ops:
  0.0 5.0 %copy-start = (f32[1,3,8,128,128]{4,3,2,1,0:T(8,128)S(1)}, f32[1,3,8,128,128]{4,3,2,1,0:T(8,128)}, u32[]{:S(2)}) copy-start(f32[1,3,8,128,128]{4,3,2,1,0:T(8,128)} %param.3) | copy-start | bytes 4718596
  0.0 5.0 %copy-start.1 = (f32[8,128,128]{2,1,0:T(8,128)S(1)}, f32[8,128,128]{2,1,0:T(8,128)}, u32[]{:S(2)}) copy-start(f32[8,128,128]{2,1,0:T(8,128)} %mob.3) | copy-start | bytes 1572868
  0.0 5.0 %copy-start.2 = (f32[8,128,128]{2,1,0:T(8,128)S(1)}, f32[8,128,128]{2,1,0:T(8,128)}, u32[]{:S(2)}) copy-start(f32[8,128,128]{2,1,0:T(8,128)} %rea.3) | copy-start | bytes 1572868
  2.9 16.6 %collective-permute-start = (f32[10,128,128]{2,1,0:T(8,128)S(1)}, f32[10,128,128]{2,1,0:T(8,128)S(1)}, u32[]{:S(2)}, u32[]{:S(2)}) collective-permute-start(f32[10,128,128]{2,1,0:T(8,128)S(1)} %get-tuple-element.28.to_right), channel_id=1, source_target_pairs={{0,1},{1,2},{2,3},{3,4},{4,5},{5,6},{6,7},{7,8},{8,9},{9,10},{10,1... | collective-permute-start | bytes 1966088 | tf_op jit(solution)/shard_map/ppermute | solution.py:33
  4.5 20.4 %collective-permute-start.1 = (f32[10,128,128]{2,1,0:T(8,128)S(1)}, f32[10,128,128]{2,1,0:T(8,128)S(1)}, u32[]{:S(2)}, u32[]{:S(2)}) collective-permute-start(f32[10,128,128]{2,1,0:T(8,128)S(1)} %get-tuple-element.29.to_left), channel_id=1, source_target_pairs={{0,31},{1,0},{2,1},{3,2},{4,3},{5,4},{6,5},{7,6},{8,7},{9,8},{10,9... | collective-permute-start | bytes 1966088 | tf_op jit(solution)/shard_map/ppermute | solution.py:33
  27.4 14.7 %collective-permute-start.3 = (f32[13,64,128]{2,1,0:T(8,128)S(1)}, f32[13,64,128]{2,1,0:T(8,128)S(1)}, u32[]{:S(2)}, u32[]{:S(2)}) collective-permute-start(f32[13,64,128]{2,1,0:T(8,128)S(1)} %get-tuple-element.42), channel_id=1, source_target_pairs={{0,31},{1,0},{2,1},{3,2},{4,3},{5,4},{6,5},{7,6},{8,7},{9,8},{10,9... | collective-permute-start | bytes 1277960 | tf_op jit(solution)/shard_map/ppermute | solution.py:33
  27.4 13.1 %collective-permute-start.2 = (f32[12,64,128]{2,1,0:T(8,128)S(1)}, f32[12,64,128]{2,1,0:T(8,128)S(1)}, u32[]{:S(2)}, u32[]{:S(2)}) collective-permute-start(f32[12,64,128]{2,1,0:T(8,128)S(1)} %get-tuple-element.41), channel_id=1, source_target_pairs={{0,1},{1,2},{2,3},{3,4},{4,5},{5,6},{6,7},{7,8},{8,9},{9,10},{10,1... | collective-permute-start | bytes 1179656 | tf_op jit(solution)/shard_map/ppermute | solution.py:33
  42.1 3.2 %collective-permute-start.4 = (f32[42,64,128]{2,1,0:T(8,128)S(1)}, f32[42,64,128]{2,1,0:T(8,128)S(1)}, u32[]{:S(2)}, u32[]{:S(2)}) collective-permute-start(f32[42,64,128]{2,1,0:T(8,128)S(1)} %shard_map.40.mine), channel_id=1, source_target_pairs={{0,32},{32,0},{64,96},{96,64},{128,160},{160,128},{192,224},{224,1... | collective-permute-start | bytes 4128776 | tf_op jit(solution)/shard_map/ppermute | solution.py:42
  46.9 12.1 %collective-permute-start.5 = (f32[5,64,128]{2,1,0:T(8,128)S(1)}, f32[5,64,128]{2,1,0:T(8,128)S(1)}, u32[]{:S(2)}, u32[]{:S(2)}) collective-permute-start(f32[5,64,128]{2,1,0:T(8,128)S(1)} %get-tuple-element.43), channel_id=1, source_target_pairs={{0,64},{32,96},{64,128},{96,160},{128,192},{160,224},{192,0},{224,... | collective-permute-start | bytes 491528 | tf_op jit(solution)/shard_map/ppermute | solution.py:33
  50.2 21.7 %collective-permute-start.8 = (f32[8,128,128]{2,1,0:T(8,128)S(1)}, f32[8,128,128]{2,1,0:T(8,128)S(1)}, u32[]{:S(2)}, u32[]{:S(2)}) collective-permute-start(f32[8,128,128]{2,1,0:T(8,128)S(1)} %get-tuple-element.35.b2), channel_id=1, source_target_pairs={{0,32},{32,64},{64,96},{96,128},{128,160},{160,192},{192,224},{224... | collective-permute-start | bytes 1572872 | tf_op jit(solution)/shard_map/ppermute | solution.py:33
  59.0 15.5 %collective-permute-start.6 = (f32[4,64,128]{2,1,0:T(8,128)S(1)}, f32[4,64,128]{2,1,0:T(8,128)S(1)}, u32[]{:S(2)}, u32[]{:S(2)}) collective-permute-start(f32[4,64,128]{2,1,0:T(8,128)S(1)} %get-tuple-element.56), channel_id=1, source_target_pairs={{0,1},{1,2},{2,3},{3,4},{4,5},{5,6},{6,7},{7,8},{8,9},{9,10},{10,1... | collective-permute-start | bytes 393224 | tf_op jit(solution)/shard_map/ppermute | solution.py:33
  71.9 9.2 %collective-permute-start.7 = (f32[4,64,128]{2,1,0:T(8,128)S(1)}, f32[4,64,128]{2,1,0:T(8,128)S(1)}, u32[]{:S(2)}, u32[]{:S(2)}) collective-permute-start(f32[4,64,128]{2,1,0:T(8,128)S(1)} %get-tuple-element.55), channel_id=1, source_target_pairs={{0,31},{1,0},{2,1},{3,2},{4,3},{5,4},{6,5},{7,6},{8,7},{9,8},{10,9... | collective-permute-start | bytes 393224 | tf_op jit(solution)/shard_map/ppermute | solution.py:33
  82.5 8.2 %collective-permute-start.9 = (f32[5,64,128]{2,1,0:T(8,128)S(1)}, f32[5,64,128]{2,1,0:T(8,128)S(1)}, u32[]{:S(2)}, u32[]{:S(2)}) collective-permute-start(f32[5,64,128]{2,1,0:T(8,128)S(1)} %shard_map.42), channel_id=1, source_target_pairs={{0,64},{32,96},{64,128},{96,160},{128,192},{160,224},{192,0},{224,... | collective-permute-start | bytes 491528 | tf_op jit(solution)/shard_map/ppermute | solution.py:33
  90.7 5.2 %collective-permute-start.10 = (f32[4,64,128]{2,1,0:T(8,128)S(1)}, f32[4,64,128]{2,1,0:T(8,128)S(1)}, u32[]{:S(2)}, u32[]{:S(2)}) collective-permute-start(f32[4,64,128]{2,1,0:T(8,128)S(1)} %get-tuple-element.54), channel_id=1, source_target_pairs={{0,1},{1,2},{2,3},{3,4},{4,5},{5,6},{6,7},{7,8},{8,9},{9,10},{10,1... | collective-permute-start | bytes 393224 | tf_op jit(solution)/shard_map/ppermute | solution.py:33
  91.5 9.2 %collective-permute-start.11 = (f32[4,64,128]{2,1,0:T(8,128)S(1)}, f32[4,64,128]{2,1,0:T(8,128)S(1)}, u32[]{:S(2)}, u32[]{:S(2)}) collective-permute-start(f32[4,64,128]{2,1,0:T(8,128)S(1)} %get-tuple-element.53), channel_id=1, source_target_pairs={{0,31},{1,0},{2,1},{3,2},{4,3},{5,4},{6,5},{7,6},{8,7},{9,8},{10,9... | collective-permute-start | bytes 393224 | tf_op jit(solution)/shard_map/ppermute | solution.py:33
  102.1 8.0 %collective-permute-start.12 = (f32[6,64,128]{2,1,0:T(8,128)S(1)}, f32[6,64,128]{2,1,0:T(8,128)S(1)}, u32[]{:S(2)}, u32[]{:S(2)}) collective-permute-start(f32[6,64,128]{2,1,0:T(8,128)S(1)} %shard_map.43), channel_id=1, source_target_pairs={{0,64},{32,96},{64,128},{96,160},{128,192},{160,224},{192,0},{224,... | collective-permute-start | bytes 589832 | tf_op jit(solution)/shard_map/ppermute | solution.py:33
  110.1 5.0 %collective-permute-start.13 = (f32[4,64,128]{2,1,0:T(8,128)S(1)}, f32[4,64,128]{2,1,0:T(8,128)S(1)}, u32[]{:S(2)}, u32[]{:S(2)}) collective-permute-start(f32[4,64,128]{2,1,0:T(8,128)S(1)} %get-tuple-element.52), channel_id=1, source_target_pairs={{0,1},{1,2},{2,3},{3,4},{4,5},{5,6},{6,7},{7,8},{8,9},{9,10},{10,1... | collective-permute-start | bytes 393224 | tf_op jit(solution)/shard_map/ppermute | solution.py:33
  111.5 9.2 %collective-permute-start.14 = (f32[4,64,128]{2,1,0:T(8,128)S(1)}, f32[4,64,128]{2,1,0:T(8,128)S(1)}, u32[]{:S(2)}, u32[]{:S(2)}) collective-permute-start(f32[4,64,128]{2,1,0:T(8,128)S(1)} %get-tuple-element.51), channel_id=1, source_target_pairs={{0,31},{1,0},{2,1},{3,2},{4,3},{5,4},{6,5},{7,6},{8,7},{9,8},{10,9... | collective-permute-start | bytes 393224 | tf_op jit(solution)/shard_map/ppermute | solution.py:33

commit v5 on v4

--- a/solution.py
+++ b/solution.py
@@ -35,6 +35,10 @@
 
 def together(*values):
     return lax.optimization_barrier(values)
+
+
+def hop(values, turn):
+    return lax.ppermute(values, "tm", [(2 * turn - 2 + core, 2 * turn + core) for core in range(2)])
 
 
 def swapped(values):
@@ -162,8 +166,8 @@
 
 
 def fine_kernel(
-    nodes, mob, rea, left, right, to_right, to_left, own, v1_own, step_own, first_own,
-    b1, b2, q, start, coarse, share, outer, rightward, leftward,
+    flags, nodes, mob, rea, left, right, to_right, to_left, own, v1_own, step_own, first_own,
+    v1_out, v2_out, q, start, coarse, share, outer, rightward, leftward,
     mw, rw, v1, v2, step, first, f1, jj, mix,
 ):
     half = mob.shape[1] // 2
@@ -198,6 +202,8 @@
         a = v2[i + 1]
         force = mob[i] * laplace(a, v2[i], v2[i + 2]) + rea[i] * cubic(a)
         second = middle * f1[i + 1]
+        v1_out[i] = v1[i + 2]
+        v2_out[i] = a
         jj[0, i] = edge * first[i] + second + far * force
         jj[1, i] = far * first[i] + second + edge * force
 
@@ -227,9 +233,19 @@
             outer[2 + 3 * side + j] = got[8 + j // 2, pl.ds(j % 2 * half, half), :]
 
     empty = jnp.zeros_like(share[0])
+
+    @pl.when(flags[2] == 0)
+    def _():
+        for j in range(4):
+            q[j] = q[j] + start[j]
+
+    @pl.when(flags[2] != 0)
+    def _():
+        for j in range(4):
+            low = start[j - 1] if j > 0 else empty
+            q[j] = q[j] - half_force(start[j], low, start[j + 1], own[0, j], own[1, j])
+
     for j in range(4):
-        low = start[j - 1] if j > 0 else empty
-        q[j] = q[j] - half_force(start[j], low, start[j + 1], own[0, j], own[1, j])
         low = coarse[0, j - 1] if j > 0 else empty
         high = coarse[0, j + 1] if j < 3 else empty
         q[4 + j] = q[4 + j] - half_force(coarse[0, j], low, high, own[0, j], own[1, j])
@@ -239,74 +255,65 @@
         leftward[4 + i] = q[4 + i]
     for i in range(2):
         rightward[3 + i] = q[6 + i]
-        rightward[10 + i] = share[i]
-        leftward[11 + i] = coarse[i, 0]
-    rightward[9] = coarse[0, 3]
+        rightward[7 + i] = share[i]
+        leftward[7 + i] = coarse[i, 0]
+    rightward[5] = start[3]
+    rightward[6] = coarse[0, 3]
     for i in range(4):
-        rightward[5 + i] = start[i]
         leftward[i] = q[i]
-        leftward[7 + i] = start[1 + i]
-
-    for m, v, shift, b in ((0, v1, 2, b1), (1, v2, 1, b2)):
+
+
+def base_kernel(v1, v2, coarse, from_left, from_right, b1, b2, mix):
+    del from_left
+    for m, v, b in ((0, v1, b1), (1, v2, b2)):
         for j in range(4):
             widen(coarse[m, j], mix, j)
-        mix[4] = jnp.zeros_like(mix[4])
+        widen(from_right[7 + m], mix, 4)
         for j in range(4):
             low = mix[j]
-            b[2 * j] = v[2 * j + shift] - low
-            b[2 * j + 1] = v[2 * j + 1 + shift] - 0.5 * (low + mix[j + 1])
-
-
-def pack_kernel(q, start, c1, share, own, outer, from_left, from_right, window):
+            b[2 * j] = v[2 * j] - low
+            b[2 * j + 1] = v[2 * j + 1] - 0.5 * (low + mix[j + 1])
+
+
+def pack_kernel(flags, q, start, c1, share, own, outer, from_left, from_right, window):
+    keep = jnp.where(flags[2] == 0, 0.0, 1.0)
     window[0] = from_left[0]
     window[1] = from_left[1]
     window[2] = from_left[2]
-    window[3] = q[0] + from_left[10] - own[0, 0] * from_left[8]
+    window[3] = q[0] + from_left[7] - keep * own[0, 0] * from_left[5]
     for i in range(1, 4):
         window[3 + i] = q[i]
         window[7 + i] = from_right[i]
-    window[7] = from_right[0] + share[0] - outer[0] * start[3]
+    window[7] = from_right[0] + share[0] - keep * outer[0] * start[3]
     window[11] = from_left[3]
     window[12] = from_left[4]
-    window[13] = q[4] + from_left[11] - own[0, 0] * from_left[9]
+    window[13] = q[4] + from_left[8] - own[0, 0] * from_left[6]
     window[14] = q[5]
     window[15] = q[6]
-    window[16] = q[7] - own[0, 3] * from_right[11]
+    window[16] = q[7] - own[0, 3] * from_right[7]
     window[17] = from_right[4] + share[1] - outer[0] * c1[3]
     window[18] = from_right[5]
     window[19] = from_right[6]
-    for i in range(4):
-        window[20 + i] = from_left[5 + i]
-        window[29 + i] = from_right[7 + i]
-    for i in range(5):
-        window[24 + i] = start[i]
-    for i in range(2):
-        window[33 + i] = from_right[11 + i]
     for i in range(6):
-        window[35 + i] = outer[2 + i]
-    window[41] = c1[0]
+        window[20 + i] = outer[2 + i]
+    window[26] = c1[0]
 
 
 def order(first, second, own, outer, out, mw, rw):
     for k, (source, coefficient) in enumerate(((first, mw), (second, rw))):
         for i in range(3):
-            coefficient[i] = source[35 + i]
-            coefficient[8 + i] = source[38 + i]
+            coefficient[i] = source[20 + i]
+            coefficient[8 + i] = source[23 + i]
         for i in range(4):
             coefficient[3 + i] = own[k, i]
         coefficient[7] = outer[k]
     for i in range(20):
         out[i] = first[i]
-    out[12] = first[12] - mw[2] * first[41]
+    out[12] = first[12] - mw[2] * first[26]
     for i in range(7):
         out[20 + i] = second[2 + i]
     for i in range(5):
         out[27 + i] = second[13 + i]
-    for i in range(2):
-        out[32 + i] = first[33 + i]
-        out[34 + i] = second[33 + i]
-    for i in range(13):
-        out[36 + i] = first[20 + i]
 
 
 def sweep(x0, q, mw, rw, last, levels, x1, x2, x3):
@@ -316,41 +323,39 @@
             force = half_force(mid, source[i], source[i + 2], mw[i + shift], rw[i + shift])
             target[i] = mid + force + q[terms + i]
 
-    level(x0, x1, 11, 0, 0)
+    if x0 is not None:
+        level(x0, x1, 11, 0, 0)
     level(x1, x2, 9, 11, 1)
     level(x2, x3, 7, 20, 2)
     level(x3, last, 5, 27, 3)
-    if last.shape[0] > 5:
-        last[5] = q[35]
     if levels is not None:
-        for i in range(4):
+        for i in range(5):
             levels[0, i] = x0[i + 4]
             levels[1, i] = x1[i + 3]
             levels[2, i] = x2[i + 2]
             levels[3, i] = x3[i + 1]
             levels[4, i] = last[i]
-        levels[1, 4] = x1[7] - q[32]
-        levels[2, 4] = x2[6] - q[33]
-        levels[3, 4] = x3[5] - q[34]
-        levels[4, 4] = last[4] - q[35]
-
-
-def first_kernel(flags, mine, other, own, outer, last, ordered, mw, rw, x1, x2, x3):
+
+
+def first_kernel(flags, mine, other, own, outer, last, ordered, mw, rw, x2, x3):
     pl.when(flags[0] == 0)(lambda: order(mine, other, own, outer, ordered, mw, rw))
     pl.when(flags[0] != 0)(lambda: order(other, mine, own, outer, ordered, mw, rw))
-    sweep(ordered.at[pl.ds(36, 13)], ordered, mw, rw, last, None, x1, x2, x3)
-
-
-def turn_kernel(final, flags, ordered, mw, rw, mid, low, high, last, *refs):
-    levels = refs[0] if final else None
-    x0, x1, x2, x3 = refs[-4:]
-
-    @pl.when(flags[1] == 0)
+    sweep(None, ordered, mw, rw, last, None, ordered.at[pl.ds(0, 11)], x2, x3)
+
+
+def turn_kernel(turn, final, flags, ordered, mw, rw, mid, low, high, *refs):
+    if turn > 1:
+        kept, *refs = refs
+    last, x0 = refs[:2]
+    levels = refs[2] if final else None
+    x1, x2, x3 = refs[-3:]
+
+    @pl.when(flags[1] != turn)
     def _():
         for i in range(13):
-            x0[i] = ordered[36 + i]
-
-    @pl.when(flags[1] != 0)
+            x0[i] = kept[i] if turn > 1 else jnp.zeros_like(x0[i])
+
+    @pl.when(flags[1] == turn)
     def _():
         for i in range(4):
             x0[i] = low[i]
@@ -359,8 +364,6 @@
             x0[4 + i] = mid[i]
 
     sweep(x0, ordered, mw, rw, last, levels, x1, x2, x3)
-    if final:
-        levels[0, 4] = mid[4] - mid[5]
 
 
 def final_kernel(flags, start, b1, b2, b_before, levels, out, wide):
@@ -411,35 +414,41 @@
     v1, step, first = call(
         local_kernel, [(8,) + plane] * 3, [(10,) + plane] * 3, states, mobility, reaction, flops=10**7
     )
-    b1, b2, q, start, coarse, share, outer, to_right, to_left = call(
+    v1, v2, q, start, coarse, share, outer, to_right, to_left = call(
         fine_kernel,
-        [(8,) + plane, (8,) + plane, (8,) + small, (5,) + small, (2, 4) + small, (2,) + small, (8,) + small, (12,) + small,
-         (13,) + small],
+        [(8,) + plane, (8,) + plane, (8,) + small, (5,) + small, (2, 4) + small, (2,) + small, (8,) + small, (9,) + small,
+         (9,) + small],
         [(10,) + plane, (10,) + plane, (12,) + plane, (10,) + plane, (10,) + plane, (8,) + plane, (10,) + plane,
          (2, 8) + plane, (5,) + plane],
-        states, mobility, reaction, left, right, to_right, to_left, own, v1, step, first, flops=2 * 10**7, limit=16,
+        flags, states, mobility, reaction, left, right, to_right, to_left, own, v1, step, first,
+        flops=2 * 10**7, limit=16, scalars=1,
     )
     q_left = ring(to_right, "space", 1)
     q_right = ring(to_left, "space", -1)
+    b1, b2 = call(base_kernel, [(8,) + plane, (8,) + plane], [(5,) + plane], v1, v2, coarse, q_left, q_right)
     b_before = ring(b2, "tm", 1)
-    (mine,) = call(pack_kernel, [(42,) + small], [], q, start, coarse[0], share, own, outer, q_left, q_right)
+    (mine,) = call(
+        pack_kernel, [(27,) + small], [], flags, q, start, coarse[0], share, own, outer, q_left, q_right, scalars=1
+    )
     other = swapped(mine)
     levels_shape = [(11,) + small, (9,) + small, (7,) + small]
     last, ordered, mw, rw = call(
-        first_kernel, [(5,) + small, (49,) + small, (11,) + small, (11,) + small], levels_shape,
+        first_kernel, [(5,) + small, (32,) + small, (11,) + small, (11,) + small], levels_shape[1:],
         flags, mine, other, own, outer, scalars=1,
     )
     turns = lax.axis_size("tm") // 2
     for turn in range(1, turns):
         final = turn == turns - 1
-        mid = ring(last, "tm", 2)
+        mid = hop(last, turn)
         low = ring(mid[0:4], "space", 1)
         high = ring(mid[1:5], "space", -1)
         if turn == 1:
             low, high, b_before = together(low, high, b_before)
-        last, *levels = call(
-            functools.partial(turn_kernel, final), [(6 if turn == turns - 2 else 5,) + small] + [(5, 5) + small] * final, [(13,) + small] + levels_shape,
-            flags, ordered, mw, rw, mid, low, high, scalars=1,
+        last, kept, *levels = call(
+            functools.partial(turn_kernel, turn, final),
+            [(5,) + small, (13,) + small] + [(5, 5) + small] * final,
+            levels_shape,
+            flags, ordered, mw, rw, mid, low, high, *([kept] if turn > 1 else []), scalars=1,
         )
     (out,) = call(
         final_kernel, [(1, 3, 8) + plane], [(5,) + plane], flags, states[0], b1, b2, b_before, levels[0], scalars=1,

time: 125 us -> 114 us (0.912)
  the two profiles are of different devices: /device:TPU:30 before, /device:TPU:254 now
where the time goes in v5:
time: 114 us
  waiting for transfers between devices  83.4 us (73%)
  Pallas kernels  16.3 us (14%)
  starting transfers between devices  13.4 us (12%)
    ppermute x11, waiting for transfers between devices, ring(): lax.ppermute(values, axis, [(i, (i + distance) % count) for i in range(co...  55.3 us
    ppermute x3, waiting for transfers between devices, hop(): lax.ppermute(values, 'tm', [(2 * turn - 2 + core, 2 * turn + core) for co...  25.7 us
    pallas_call x9, Pallas kernels, call(): pl.pallas_call(kernel, out_shape=[jax.ShapeDtypeStruct(s, jnp.float32) fo...  13.6 us
    ppermute x11, starting transfers between devices, ring(): lax.ppermute(values, axis, [(i, (i + distance) % count) for i in range(co...  10.7 us
    pallas_call x1, Pallas kernels, body(): pl.pallas_call(edge_kernel, out_shape=[jax.ShapeDtypeStruct(s, jnp.float3...  2.78 us
    ppermute x3, starting transfers between devices, hop(): lax.ppermute(values, 'tm', [(2 * turn - 2 + core, 2 * turn + core) for co...  2.63 us
    ppermute x1, waiting for transfers between devices, swapped(): return lax.ppermute(values, 'tm', [(i, i ^ 1) for i in range(count)])  2.41 us
  transfers between devices with their start and end apart: 15, of which 12 were waited for; matrix products, arithmetic and copies ran while one was open for 0% of the time, Pallas kernels for 2%

profile of v5, /device:TPU:254, one launch (start us, length us, event | category | flops | bytes accessed | tf_op | source)
XLA Modules:
  0.0 113.5 jit_solution(4412262588174313670)
XLA Ops:
  0.1 2.8 %shard_map.37 = (f32[2,4,64,128]{3,2,1,0:T(8,128)S(1)}, f32[10,128,128]{2,1,0:T(8,128)S(1)}, f32[10,128,128]{2,1,0:T(8,128)S(1)}) custom-call(s32[3]{0:T(128)S(1)} %pad_add_fusion.flags, f32[3,8,128,128]{3,2,1,0:T(8,128)} %bitcast.8, f32[8,128,128]{2,1,0:T(8,128)} %mob.3, f32[8,128,128]{2,1,0:T(8,128)} %rea.3), custom_call_target="tpu_custom_call" | custom-call | flops 1000000 | bytes 4000000 | tf_op jit(solution)/shard_map/pallas_call | solution.py:402
  3.6 1.4 %collective-permute-start.1 = (f32[10,128,128]{2,1,0:T(8,128)S(1)}, f32[10,128,128]{2,1,0:T(8,128)S(1)}, u32[]{:S(2)}, u32[]{:S(2)}) collective-permute-start(f32[10,128,128]{2,1,0:T(8,128)S(1)} %get-tuple-element.35.to_left), channel_id=1, source_target_pairs={{0,31},{1,0},{2,1},{3,2},{4,3},{5,4},{6,5},{7,6},{8,7},{9,8},{10,9... | collective-permute-start | bytes 1966088 | tf_op jit(solution)/shard_map/ppermute | solution.py:33
  5.0 1.7 %shard_map.38 = (f32[8,128,128]{2,1,0:T(8,128)S(1)}, f32[8,128,128]{2,1,0:T(8,128)S(1)}, f32[8,128,128]{2,1,0:T(8,128)S(1)}) custom-call(f32[3,8,128,128]{3,2,1,0:T(8,128)S(1)} %bitcast.9, f32[8,128,128]{2,1,0:T(8,128)S(1)} %copy-done.1, f32[8,128,128]{2,1,0:T(8,128)S(1)} %copy-done.2), custom_call_target="tpu_custom_call" | custom-call | flops 10000000 | bytes 4194304 | tf_op jit(solution)/shard_map/pallas_call | solution.py:51
  6.7 12.7 %collective-permute-done.left = f32[10,128,128]{2,1,0:T(8,128)S(1)} collective-permute-done((f32[10,128,128]{2,1,0:T(8,128)S(1)}, f32[10,128,128]{2,1,0:T(8,128)S(1)}, u32[]{:S(2)}, u32[]{:S(2)}) %collective-permute-start) | collective-permute-done | bytes 655392 | tf_op jit(solution)/shard_map/ppermute | solution.py:33
  19.4 4.5 %collective-permute-done.1.right = f32[10,128,128]{2,1,0:T(8,128)S(1)} collective-permute-done((f32[10,128,128]{2,1,0:T(8,128)S(1)}, f32[10,128,128]{2,1,0:T(8,128)S(1)}, u32[]{:S(2)}, u32[]{:S(2)}) %collective-permute-start.1) | collective-permute-done | bytes 655392 | tf_op jit(solution)/shard_map/ppermute | solution.py:33
  24.0 2.9 %shard_map.39 = (f32[8,128,128]{2,1,0:T(8,128)S(1)}, f32[8,128,128]{2,1,0:T(8,128)S(1)}, f32[8,64,128]{2,1,0:T(8,128)S(1)}, f32[5,64,128]{2,1,0:T(8,128)S(1)}, f...) custom-call(s32[3]{0:T(128)S(1)} %pad_add_fusion.flags, ...), custom_call_target="tpu_custom_call" | custom-call | flops 20000000 | bytes 9732108 | tf_op jit(solution)/shard_map/pallas_call | solution.py:51
  27.3 1.7 %collective-permute-start.3 = (f32[9,64,128]{2,1,0:T(8,128)S(1)}, f32[9,64,128]{2,1,0:T(8,128)S(1)}, u32[]{:S(2)}, u32[]{:S(2)}) collective-permute-start(f32[9,64,128]{2,1,0:T(8,128)S(1)} %get-tuple-element.44), channel_id=1, source_target_pairs={{0,31},{1,0},{2,1},{3,2},{4,3},{5,4},{6,5},{7,6},{8,7},{9,8},{10,9... | collective-permute-start | bytes 884744 | tf_op jit(solution)/shard_map/ppermute | solution.py:33
  29.0 5.5 %collective-permute-done.2.from_left = f32[9,64,128]{2,1,0:T(8,128)S(1)} collective-permute-done((f32[9,64,128]{2,1,0:T(8,128)S(1)}, f32[9,64,128]{2,1,0:T(8,128)S(1)}, u32[]{:S(2)}, u32[]{:S(2)}) %collective-permute-start.2) | collective-permute-done | bytes 294944 | tf_op jit(solution)/shard_map/ppermute | solution.py:33
  34.5 4.5 %collective-permute-done.3.from_right = f32[9,64,128]{2,1,0:T(8,128)S(1)} collective-permute-done((f32[9,64,128]{2,1,0:T(8,128)S(1)}, f32[9,64,128]{2,1,0:T(8,128)S(1)}, u32[]{:S(2)}, u32[]{:S(2)}) %collective-permute-start.3) | collective-permute-done | bytes 294944 | tf_op jit(solution)/shard_map/ppermute | solution.py:33
  39.8 2.4 %collective-permute-done.4.other = f32[27,64,128]{2,1,0:T(8,128)S(1)} collective-permute-done((f32[27,64,128]{2,1,0:T(8,128)S(1)}, f32[27,64,128]{2,1,0:T(8,128)S(1)}, u32[]{:S(2)}, u32[]{:S(2)}) %collective-permute-start.4) | collective-permute-done | bytes 884768 | tf_op jit(solution)/shard_map/ppermute | solution.py:46
  44.9 1.7 %collective-permute-start.7 = (f32[4,64,128]{2,1,0:T(8,128)S(1)}, f32[4,64,128]{2,1,0:T(8,128)S(1)}, u32[]{:S(2)}, u32[]{:S(2)}) collective-permute-start(f32[4,64,128]{2,1,0:T(8,128)S(1)} %get-tuple-element.67), channel_id=1, source_target_pairs={{0,31},{1,0},{2,1},{3,2},{4,3},{5,4},{6,5},{7,6},{8,7},{9,8},{10,9... | collective-permute-start | bytes 393224 | tf_op jit(solution)/shard_map/ppermute | solution.py:33
  46.6 13.0 %collective-permute-done.8.b_before = f32[8,128,128]{2,1,0:T(8,128)S(1)} collective-permute-done((f32[8,128,128]{2,1,0:T(8,128)S(1)}, f32[8,128,128]{2,1,0:T(8,128)S(1)}, u32[]{:S(2)}, u32[]{:S(2)}) %collective-permute-start.8) | collective-permute-done | bytes 524320 | tf_op jit(solution)/shard_map/ppermute | solution.py:33
  60.0 1.4 %shard_map.43 = (f32[5,64,128]{2,1,0:T(8,128)S(1)}, f32[13,64,128]{2,1,0:T(8,128)S(1)}) custom-call(s32[3]{0:T(128)S(1)} %pad_add_fusion.flags, f32[32,64,128]{2,1,0:T(8,128)S(1)} %get-tuple-element.53.ordered, f32[11,64,128]{2,1,0:T(8,128)S(1)} %get-tuple-element.54.mw, f32[11,64,128]{2,1,0:T(8,128)S(1)} %get-tuple-element.55.rw, ...), custom_call_target="tpu_custom_call" | custom-call | flops 1000000 | bytes 2785292 | tf_op jit(solution)/shard_map/pallas_call | solution.py:51
  62.2 2.0 %collective-permute-start.11 = (f32[4,64,128]{2,1,0:T(8,128)S(1)}, f32[4,64,128]{2,1,0:T(8,128)S(1)}, u32[]{:S(2)}, u32[]{:S(2)}) collective-permute-start(f32[4,64,128]{2,1,0:T(8,128)S(1)} %get-tuple-element.65), channel_id=1, source_target_pairs={{0,31},{1,0},{2,1},{3,2},{4,3},{5,4},{6,5},{7,6},{8,7},{9,8},{10,9... | collective-permute-start | bytes 393224 | tf_op jit(solution)/shard_map/ppermute | solution.py:33
  64.2 3.1 %collective-permute-done.10.low = f32[4,64,128]{2,1,0:T(8,128)S(1)} collective-permute-done((f32[4,64,128]{2,1,0:T(8,128)S(1)}, f32[4,64,128]{2,1,0:T(8,128)S(1)}, u32[]{:S(2)}, u32[]{:S(2)}) %collective-permute-start.10) | collective-permute-done | bytes 131104 | tf_op jit(solution)/shard_map/ppermute | solution.py:33
  67.3 4.3 %collective-permute-done.11.high = f32[4,64,128]{2,1,0:T(8,128)S(1)} collective-permute-done((f32[4,64,128]{2,1,0:T(8,128)S(1)}, f32[4,64,128]{2,1,0:T(8,128)S(1)}, u32[]{:S(2)}, u32[]{:S(2)}) %collective-permute-start.11) | collective-permute-done | bytes 131104 | tf_op jit(solution)/shard_map/ppermute | solution.py:33
  71.6 1.6 %shard_map.44 = (f32[5,64,128]{2,1,0:T(8,128)S(1)}, f32[13,64,128]{2,1,0:T(8,128)S(1)}) custom-call(s32[3]{0:T(128)S(1)} %pad_add_fusion.flags, f32[32,64,128]{2,1,0:T(8,128)S(1)} %get-tuple-element.53.ordered, f32[11,64,128]{2,1,0:T(8,128)S(1)} %get-tuple-element.54.mw, f32[11,64,128]{2,1,0:T(8,128)S(1)} %get-tuple-element.55.rw, ...), custom_call_target="tpu_custom_call" | custom-call | flops 1000000 | bytes 3211276 | tf_op jit(solution)/shard_map/pallas_call | solution.py:51
  73.2 1.3 %collective-permute-start.12 = (f32[5,64,128]{2,1,0:T(8,128)S(1)}, f32[5,64,128]{2,1,0:T(8,128)S(1)}, u32[]{:S(2)}, u32[]{:S(2)}) collective-permute-start(f32[5,64,128]{2,1,0:T(8,128)S(1)} %get-tuple-element.60), channel_id=1, source_target_pairs={{128,192},{160,224},{129,193},{161,225},{130,194},{162,226},{131,1... | collective-permute-start | bytes 491528 | tf_op jit(solution)/shard_map/ppermute | solution.py:41
  74.5 25.6 %collective-permute-done.12.mid = f32[5,64,128]{2,1,0:T(8,128)S(1)} collective-permute-done((f32[5,64,128]{2,1,0:T(8,128)S(1)}, f32[5,64,128]{2,1,0:T(8,128)S(1)}, u32[]{:S(2)}, u32[]{:S(2)}) %collective-permute-start.12) | collective-permute-done | bytes 163872 | tf_op jit(solution)/shard_map/ppermute | solution.py:41
  100.3 2.0 %collective-permute-start.14 = (f32[4,64,128]{2,1,0:T(8,128)S(1)}, f32[4,64,128]{2,1,0:T(8,128)S(1)}, u32[]{:S(2)}, u32[]{:S(2)}) collective-permute-start(f32[4,64,128]{2,1,0:T(8,128)S(1)} %get-tuple-element.63), channel_id=1, source_target_pairs={{0,31},{1,0},{2,1},{3,2},{4,3},{5,4},{6,5},{7,6},{8,7},{9,8},{10,9... | collective-permute-start | bytes 393224 | tf_op jit(solution)/shard_map/ppermute | solution.py:33
  102.3 2.9 %collective-permute-done.13.low = f32[4,64,128]{2,1,0:T(8,128)S(1)} collective-permute-done((f32[4,64,128]{2,1,0:T(8,128)S(1)}, f32[4,64,128]{2,1,0:T(8,128)S(1)}, u32[]{:S(2)}, u32[]{:S(2)}) %collective-permute-start.13) | collective-permute-done | bytes 131104 | tf_op jit(solution)/shard_map/ppermute | solution.py:33
  105.2 4.3 %collective-permute-done.14.high = f32[4,64,128]{2,1,0:T(8,128)S(1)} collective-permute-done((f32[4,64,128]{2,1,0:T(8,128)S(1)}, f32[4,64,128]{2,1,0:T(8,128)S(1)}, u32[]{:S(2)}, u32[]{:S(2)}) %collective-permute-start.14) | collective-permute-done | bytes 131104 | tf_op jit(solution)/shard_map/ppermute | solution.py:33
  109.5 2.1 %shard_map.45 = (f32[5,64,128]{2,1,0:T(8,128)}, f32[13,64,128]{2,1,0:T(8,128)}, f32[5,5,64,128]{3,2,1,0:T(8,128)S(1)}) custom-call(s32[3]{0:T(128)S(1)} %pad_add_fusion.flags, f32[32,64,128]{2,1,0:T(8,128)S(1)} %get-tuple-element.53.ordered, f32[11,64,128]{2,1,0:T(8,128)S(1)} %get-tuple-element.54.mw, f32[11,64,128]{2,1,0:T(8,128)S(1)} %get-tuple-element.55.rw, ...), custom_call_target="tpu_custom_call" | custom-call | flops 1000000 | bytes 4030476 | tf_op jit(solution)/shard_map/pallas_call | solution.py:51
  111.6 1.9 %shard_map.46 = f32[1,3,8,128,128]{4,3,2,1,0:T(8,128)} custom-call(s32[3]{0:T(128)S(1)} %pad_add_fusion.flags, f32[8,128,128]{2,1,0:T(8,128)S(1)} %slice_bitcast_fusion.start, f32[8,128,128]{2,1,0:T(8,128)S(1)} %get-tuple-element.45.b1, f32[8,128,128]{2,1,0:T(8,128)S(1)} %get-tuple-element.46.b2, f32[8,128,128]{2,1,0:T(8,128)S(1)} %collective-permute-done.8.b_before, ...), custom_call_target="tpu_custom_call" | custom-call | flops 1000000 | bytes 4489228 | tf_op jit(solution)/shard_map/pallas_call | solution.py:51
  (28 shorter events, 5.8 us)
Async XLA Ops:
  0.0 5.0 %copy-start = (f32[1,3,8,128,128]{4,3,2,1,0:T(8,128)S(1)}, f32[1,3,8,128,128]{4,3,2,1,0:T(8,128)}, u32[]{:S(2)}) copy-start(f32[1,3,8,128,128]{4,3,2,1,0:T(8,128)} %param.3) | copy-start | bytes 4718596
  0.0 5.0 %copy-start.1 = (f32[8,128,128]{2,1,0:T(8,128)S(1)}, f32[8,128,128]{2,1,0:T(8,128)}, u32[]{:S(2)}) copy-start(f32[8,128,128]{2,1,0:T(8,128)} %mob.3) | copy-start | bytes 1572868
  0.0 5.0 %copy-start.2 = (f32[8,128,128]{2,1,0:T(8,128)S(1)}, f32[8,128,128]{2,1,0:T(8,128)}, u32[]{:S(2)}) copy-start(f32[8,128,128]{2,1,0:T(8,128)} %rea.3) | copy-start | bytes 1572868
  2.9 16.5 %collective-permute-start = (f32[10,128,128]{2,1,0:T(8,128)S(1)}, f32[10,128,128]{2,1,0:T(8,128)S(1)}, u32[]{:S(2)}, u32[]{:S(2)}) collective-permute-start(f32[10,128,128]{2,1,0:T(8,128)S(1)} %get-tuple-element.34.to_right), channel_id=1, source_target_pairs={{0,1},{1,2},{2,3},{3,4},{4,5},{5,6},{6,7},{7,8},{8,9},{9,10},{10,1... | collective-permute-start | bytes 1966088 | tf_op jit(solution)/shard_map/ppermute | solution.py:33
  3.6 20.4 %collective-permute-start.1 = (f32[10,128,128]{2,1,0:T(8,128)S(1)}, f32[10,128,128]{2,1,0:T(8,128)S(1)}, u32[]{:S(2)}, u32[]{:S(2)}) collective-permute-start(f32[10,128,128]{2,1,0:T(8,128)S(1)} %get-tuple-element.35.to_left), channel_id=1, source_target_pairs={{0,31},{1,0},{2,1},{3,2},{4,3},{5,4},{6,5},{7,6},{8,7},{9,8},{10,9... | collective-permute-start | bytes 1966088 | tf_op jit(solution)/shard_map/ppermute | solution.py:33
  26.9 7.6 %collective-permute-start.2 = (f32[9,64,128]{2,1,0:T(8,128)S(1)}, f32[9,64,128]{2,1,0:T(8,128)S(1)}, u32[]{:S(2)}, u32[]{:S(2)}) collective-permute-start(f32[9,64,128]{2,1,0:T(8,128)S(1)} %get-tuple-element.43), channel_id=1, source_target_pairs={{0,1},{1,2},{2,3},{3,4},{4,5},{5,6},{6,7},{7,8},{8,9},{9,10},{10,1... | collective-permute-start | bytes 884744 | tf_op jit(solution)/shard_map/ppermute | solution.py:33
  27.3 11.8 %collective-permute-start.3 = (f32[9,64,128]{2,1,0:T(8,128)S(1)}, f32[9,64,128]{2,1,0:T(8,128)S(1)}, u32[]{:S(2)}, u32[]{:S(2)}) collective-permute-start(f32[9,64,128]{2,1,0:T(8,128)S(1)} %get-tuple-element.44), channel_id=1, source_target_pairs={{0,31},{1,0},{2,1},{3,2},{4,3},{5,4},{6,5},{7,6},{8,7},{9,8},{10,9... | collective-permute-start | bytes 884744 | tf_op jit(solution)/shard_map/ppermute | solution.py:33
  39.7 2.5 %collective-permute-start.4 = (f32[27,64,128]{2,1,0:T(8,128)S(1)}, f32[27,64,128]{2,1,0:T(8,128)S(1)}, u32[]{:S(2)}, u32[]{:S(2)}) collective-permute-start(f32[27,64,128]{2,1,0:T(8,128)S(1)} %shard_map.41.mine), channel_id=1, source_target_pairs={{0,32},{32,0},{64,96},{96,64},{128,160},{160,128},{192,224},{224,1... | collective-permute-start | bytes 2654216 | tf_op jit(solution)/shard_map/ppermute | solution.py:46
  43.4 1.1 collective-permute-start.5
  44.3 15.3 %collective-permute-start.8 = (f32[8,128,128]{2,1,0:T(8,128)S(1)}, f32[8,128,128]{2,1,0:T(8,128)S(1)}, u32[]{:S(2)}, u32[]{:S(2)}) collective-permute-start(f32[8,128,128]{2,1,0:T(8,128)S(1)} %get-tuple-element.46.b2), channel_id=1, source_target_pairs={{0,32},{32,64},{64,96},{96,128},{128,160},{160,192},{192,224},{224... | collective-permute-start | bytes 1572872 | tf_op jit(solution)/shard_map/ppermute | solution.py:33
  44.5 15.1 %collective-permute-start.6 = (f32[4,64,128]{2,1,0:T(8,128)S(1)}, f32[4,64,128]{2,1,0:T(8,128)S(1)}, u32[]{:S(2)}, u32[]{:S(2)}) collective-permute-start(f32[4,64,128]{2,1,0:T(8,128)S(1)} %get-tuple-element.68), channel_id=1, source_target_pairs={{0,1},{1,2},{2,3},{3,4},{4,5},{5,6},{6,7},{7,8},{8,9},{9,10},{10,1... | collective-permute-start | bytes 393224 | tf_op jit(solution)/shard_map/ppermute | solution.py:33
  44.9 15.1 %collective-permute-start.7 = (f32[4,64,128]{2,1,0:T(8,128)S(1)}, f32[4,64,128]{2,1,0:T(8,128)S(1)}, u32[]{:S(2)}, u32[]{:S(2)}) collective-permute-start(f32[4,64,128]{2,1,0:T(8,128)S(1)} %get-tuple-element.67), channel_id=1, source_target_pairs={{0,31},{1,0},{2,1},{3,2},{4,3},{5,4},{6,5},{7,6},{8,7},{9,8},{10,9... | collective-permute-start | bytes 393224 | tf_op jit(solution)/shard_map/ppermute | solution.py:33
  61.4 0.7 collective-permute-start.9
  62.1 5.2 %collective-permute-start.10 = (f32[4,64,128]{2,1,0:T(8,128)S(1)}, f32[4,64,128]{2,1,0:T(8,128)S(1)}, u32[]{:S(2)}, u32[]{:S(2)}) collective-permute-start(f32[4,64,128]{2,1,0:T(8,128)S(1)} %get-tuple-element.66), channel_id=1, source_target_pairs={{0,1},{1,2},{2,3},{3,4},{4,5},{5,6},{6,7},{7,8},{8,9},{9,10},{10,1... | collective-permute-start | bytes 393224 | tf_op jit(solution)/shard_map/ppermute | solution.py:33
  62.2 9.4 %collective-permute-start.11 = (f32[4,64,128]{2,1,0:T(8,128)S(1)}, f32[4,64,128]{2,1,0:T(8,128)S(1)}, u32[]{:S(2)}, u32[]{:S(2)}) collective-permute-start(f32[4,64,128]{2,1,0:T(8,128)S(1)} %get-tuple-element.65), channel_id=1, source_target_pairs={{0,31},{1,0},{2,1},{3,2},{4,3},{5,4},{6,5},{7,6},{8,7},{9,8},{10,9... | collective-permute-start | bytes 393224 | tf_op jit(solution)/shard_map/ppermute | solution.py:33
  73.2 26.9 %collective-permute-start.12 = (f32[5,64,128]{2,1,0:T(8,128)S(1)}, f32[5,64,128]{2,1,0:T(8,128)S(1)}, u32[]{:S(2)}, u32[]{:S(2)}) collective-permute-start(f32[5,64,128]{2,1,0:T(8,128)S(1)} %get-tuple-element.60), channel_id=1, source_target_pairs={{128,192},{160,224},{129,193},{161,225},{130,194},{162,226},{131,1... | collective-permute-start | bytes 491528 | tf_op jit(solution)/shard_map/ppermute | solution.py:41
  100.2 5.0 %collective-permute-start.13 = (f32[4,64,128]{2,1,0:T(8,128)S(1)}, f32[4,64,128]{2,1,0:T(8,128)S(1)}, u32[]{:S(2)}, u32[]{:S(2)}) collective-permute-start(f32[4,64,128]{2,1,0:T(8,128)S(1)} %get-tuple-element.64), channel_id=1, source_target_pairs={{0,1},{1,2},{2,3},{3,4},{4,5},{5,6},{6,7},{7,8},{8,9},{9,10},{10,1... | collective-permute-start | bytes 393224 | tf_op jit(solution)/shard_map/ppermute | solution.py:33
  100.3 9.3 %collective-permute-start.14 = (f32[4,64,128]{2,1,0:T(8,128)S(1)}, f32[4,64,128]{2,1,0:T(8,128)S(1)}, u32[]{:S(2)}, u32[]{:S(2)}) collective-permute-start(f32[4,64,128]{2,1,0:T(8,128)S(1)} %get-tuple-element.63), channel_id=1, source_target_pairs={{0,31},{1,0},{2,1},{3,2},{4,3},{5,4},{6,5},{7,6},{8,7},{9,8},{10,9... | collective-permute-start | bytes 393224 | tf_op jit(solution)/shard_map/ppermute | solution.py:33

commit v6 on v5

--- a/solution.py
+++ b/solution.py
@@ -366,28 +366,28 @@
     sweep(x0, ordered, mw, rw, last, levels, x1, x2, x3)
 
 
-def final_kernel(flags, start, b1, b2, b_before, levels, out, wide):
+def final_kernel(flags, start, b1, b2, b_before, b_late, b_later, levels, out, wide):
     core = flags[0]
-    for m, b in ((0, b_before), (1, b1), (2, b2)):
-
-        def corrected(m=m, b=b):
-            for j in range(5):
-                widen(levels[2 * core + m, j], wide, j)
-            for j in range(4):
-                low = wide[j]
-                out[0, m, 2 * j] = b[2 * j] + low
-                out[0, m, 2 * j + 1] = b[2 * j + 1] + 0.5 * (low + wide[j + 1])
-
-        if m == 0:
-            pl.when(flags[2] != 0)(corrected)
-
-            @pl.when(flags[2] == 0)
-            def _():
-                for i in range(8):
-                    out[0, 0, i] = start[i]
-
-        else:
-            corrected()
+
+    def corrected(m, b):
+        for j in range(5):
+            widen(levels[2 * core + m, j], wide, j)
+        for j in range(4):
+            low = wide[j]
+            out[0, m, 2 * j] = b[2 * j] + low
+            out[0, m, 2 * j + 1] = b[2 * j + 1] + 0.5 * (low + wide[j + 1])
+
+    corrected(1, b1)
+    corrected(2, b2)
+
+    @pl.when(flags[2] == 0)
+    def _():
+        for i in range(8):
+            out[0, 0, i] = start[i]
+
+    pl.when(flags[2] == 2)(lambda: corrected(0, b_late))
+    pl.when(flags[2] == 4)(lambda: corrected(0, b_later))
+    pl.when((flags[2] != 0) & (flags[2] != 2) & (flags[2] != 4))(lambda: corrected(0, b_before))
 
 
 def body(nodes, mobility, reaction):
@@ -426,7 +426,8 @@
     q_left = ring(to_right, "space", 1)
     q_right = ring(to_left, "space", -1)
     b1, b2 = call(base_kernel, [(8,) + plane, (8,) + plane], [(5,) + plane], v1, v2, coarse, q_left, q_right)
-    b_before = ring(b2, "tm", 1)
+    count = lax.axis_size("tm")
+    b_before = lax.ppermute(b2, "tm", [(i, i + 1) for i in range(count - 1) if i not in (1, 3)])
     (mine,) = call(
         pack_kernel, [(27,) + small], [], flags, q, start, coarse[0], share, own, outer, q_left, q_right, scalars=1
     )
@@ -439,7 +440,15 @@
     turns = lax.axis_size("tm") // 2
     for turn in range(1, turns):
         final = turn == turns - 1
+        if turn == 2:
+            last, b_later = together(last, b_later)
+        if turn == 3:
+            last, sent = together(last, b2)
+            b_late = lax.ppermute(sent, "tm", [(1, 2)])
         mid = hop(last, turn)
+        if turn == 1:
+            mid, sent = together(mid, b2)
+            b_later = lax.ppermute(sent, "tm", [(3, 4)])
         low = ring(mid[0:4], "space", 1)
         high = ring(mid[1:5], "space", -1)
         if turn == 1:
@@ -451,7 +460,7 @@
             flags, ordered, mw, rw, mid, low, high, *([kept] if turn > 1 else []), scalars=1,
         )
     (out,) = call(
-        final_kernel, [(1, 3, 8) + plane], [(5,) + plane], flags, states[0], b1, b2, b_before, levels[0], scalars=1,
+        final_kernel, [(1, 3, 8) + plane], [(5,) + plane], flags, states[0], b1, b2, b_before, b_late, b_later, levels[0], scalars=1,
     )
     return out
 

time: 114 us -> 111 us (0.974)
  the two profiles are of different devices: /device:TPU:254 before, /device:TPU:33 now
where the time goes in v6:
time: 111 us
  starting transfers between devices  57 us (51%)
  waiting for transfers between devices  37.7 us (34%)
  Pallas kernels  16.2 us (15%)
    ppermute x10, waiting for transfers between devices, ring(): lax.ppermute(values, axis, [(i, (i + distance) % count) for i in range(co...  30.2 us
    ppermute x10, starting transfers between devices, ring(): lax.ppermute(values, axis, [(i, (i + distance) % count) for i in range(co...  29.2 us
    ppermute x1, starting transfers between devices, body(): b_late = lax.ppermute(sent, 'tm', [(1, 2)])  17.1 us
    pallas_call x9, Pallas kernels, call(): pl.pallas_call(kernel, out_shape=[jax.ShapeDtypeStruct(s, jnp.float32) fo...  13.4 us
    ppermute x3, starting transfers between devices, hop(): lax.ppermute(values, 'tm', [(2 * turn - 2 + core, 2 * turn + core) for co...  6.25 us
    ppermute x3, waiting for transfers between devices, hop(): lax.ppermute(values, 'tm', [(2 * turn - 2 + core, 2 * turn + core) for co...  5.5 us
    pallas_call x1, Pallas kernels, body(): pl.pallas_call(edge_kernel, out_shape=[jax.ShapeDtypeStruct(s, jnp.float3...  2.78 us
    ppermute x1, starting transfers between devices, swapped(): return lax.ppermute(values, 'tm', [(i, i ^ 1) for i in range(count)])  2.43 us
  transfers between devices with their start and end apart: 17, of which 7 were waited for; matrix products, arithmetic and copies ran while one was open for 0% of the time, Pallas kernels for 5%

profile of v6, /device:TPU:33, one launch (start us, length us, event | category | flops | bytes accessed | tf_op | source)
XLA Modules:
  0.0 111.3 jit_solution(8282818457710258867)
XLA Ops:
  0.1 2.8 %shard_map.37 = (f32[2,4,64,128]{3,2,1,0:T(8,128)S(1)}, f32[10,128,128]{2,1,0:T(8,128)S(1)}, f32[10,128,128]{2,1,0:T(8,128)S(1)}) custom-call(s32[3]{0:T(128)S(1)} %pad_add_fusion.flags, f32[3,8,128,128]{3,2,1,0:T(8,128)} %bitcast.8, f32[8,128,128]{2,1,0:T(8,128)} %mob.3, f32[8,128,128]{2,1,0:T(8,128)} %rea.3), custom_call_target="tpu_custom_call" | custom-call | flops 1000000 | bytes 4000000 | tf_op jit(solution)/shard_map/pallas_call | solution.py:402
  2.9 1.4 %collective-permute-start = (f32[10,128,128]{2,1,0:T(8,128)S(1)}, f32[10,128,128]{2,1,0:T(8,128)S(1)}, u32[]{:S(2)}, u32[]{:S(2)}) collective-permute-start(f32[10,128,128]{2,1,0:T(8,128)S(1)} %get-tuple-element.40.to_right), channel_id=1, source_target_pairs={{0,1},{1,2},{2,3},{3,4},{4,5},{5,6},{6,7},{7,8},{8,9},{9,10},{10,1... | collective-permute-start | bytes 1966088 | tf_op jit(solution)/shard_map/ppermute | solution.py:33
  4.3 4.4 %collective-permute-start.1 = (f32[10,128,128]{2,1,0:T(8,128)S(1)}, f32[10,128,128]{2,1,0:T(8,128)S(1)}, u32[]{:S(2)}, u32[]{:S(2)}) collective-permute-start(f32[10,128,128]{2,1,0:T(8,128)S(1)} %get-tuple-element.41.to_left), channel_id=1, source_target_pairs={{0,31},{1,0},{2,1},{3,2},{4,3},{5,4},{6,5},{7,6},{8,7},{9,8},{10,9... | collective-permute-start | bytes 1966088 | tf_op jit(solution)/shard_map/ppermute | solution.py:33
  8.7 1.7 %shard_map.38 = (f32[8,128,128]{2,1,0:T(8,128)S(1)}, f32[8,128,128]{2,1,0:T(8,128)S(1)}, f32[8,128,128]{2,1,0:T(8,128)S(1)}) custom-call(f32[3,8,128,128]{3,2,1,0:T(8,128)S(1)} %bitcast.9, f32[8,128,128]{2,1,0:T(8,128)S(1)} %copy-done.1, f32[8,128,128]{2,1,0:T(8,128)S(1)} %copy-done.2), custom_call_target="tpu_custom_call" | custom-call | flops 10000000 | bytes 4194304 | tf_op jit(solution)/shard_map/pallas_call | solution.py:51
  10.4 12.4 %collective-permute-done.left = f32[10,128,128]{2,1,0:T(8,128)S(1)} collective-permute-done((f32[10,128,128]{2,1,0:T(8,128)S(1)}, f32[10,128,128]{2,1,0:T(8,128)S(1)}, u32[]{:S(2)}, u32[]{:S(2)}) %collective-permute-start) | collective-permute-done | bytes 655392 | tf_op jit(solution)/shard_map/ppermute | solution.py:33
  22.8 2.9 %shard_map.39 = (f32[8,128,128]{2,1,0:T(8,128)S(1)}, f32[8,128,128]{2,1,0:T(8,128)S(1)}, f32[8,64,128]{2,1,0:T(8,128)S(1)}, f32[5,64,128]{2,1,0:T(8,128)S(1)}, f...) custom-call(s32[3]{0:T(128)S(1)} %pad_add_fusion.flags, ...), custom_call_target="tpu_custom_call" | custom-call | flops 20000000 | bytes 9732108 | tf_op jit(solution)/shard_map/pallas_call | solution.py:51
  25.8 5.7 %collective-permute-start.3 = (f32[9,64,128]{2,1,0:T(8,128)S(1)}, f32[9,64,128]{2,1,0:T(8,128)S(1)}, u32[]{:S(2)}, u32[]{:S(2)}) collective-permute-start(f32[9,64,128]{2,1,0:T(8,128)S(1)} %get-tuple-element.50), channel_id=1, source_target_pairs={{0,31},{1,0},{2,1},{3,2},{4,3},{5,4},{6,5},{7,6},{8,7},{9,8},{10,9... | collective-permute-start | bytes 884744 | tf_op jit(solution)/shard_map/ppermute | solution.py:33
  31.5 5.6 %collective-permute-done.2.from_left = f32[9,64,128]{2,1,0:T(8,128)S(1)} collective-permute-done((f32[9,64,128]{2,1,0:T(8,128)S(1)}, f32[9,64,128]{2,1,0:T(8,128)S(1)}, u32[]{:S(2)}, u32[]{:S(2)}) %collective-permute-start.2) | collective-permute-done | bytes 294944 | tf_op jit(solution)/shard_map/ppermute | solution.py:33
  37.7 2.4 %collective-permute-start.4 = (f32[27,64,128]{2,1,0:T(8,128)S(1)}, f32[27,64,128]{2,1,0:T(8,128)S(1)}, u32[]{:S(2)}, u32[]{:S(2)}) collective-permute-start(f32[27,64,128]{2,1,0:T(8,128)S(1)} %shard_map.41.mine), channel_id=1, source_target_pairs={{0,32},{32,0},{64,96},{96,64},{128,160},{160,128},{192,224},{224,1... | collective-permute-start | bytes 2654216 | tf_op jit(solution)/shard_map/ppermute | solution.py:46
  40.2 2.1 %collective-permute-done.4.other = f32[27,64,128]{2,1,0:T(8,128)S(1)} collective-permute-done((f32[27,64,128]{2,1,0:T(8,128)S(1)}, f32[27,64,128]{2,1,0:T(8,128)S(1)}, u32[]{:S(2)}, u32[]{:S(2)}) %collective-permute-start.4) | collective-permute-done | bytes 884768 | tf_op jit(solution)/shard_map/ppermute | solution.py:46
  43.4 4.9 %collective-permute-start.5 = (f32[5,64,128]{2,1,0:T(8,128)S(1)}, f32[5,64,128]{2,1,0:T(8,128)S(1)}, u32[]{:S(2)}, u32[]{:S(2)}) collective-permute-start(f32[5,64,128]{2,1,0:T(8,128)S(1)} %get-tuple-element.57), channel_id=1, source_target_pairs={{0,64},{32,96},{1,65},{33,97},{2,66},{34,98},{3,67},{35,99},{4,68}... | collective-permute-start | bytes 491528 | tf_op jit(solution)/shard_map/ppermute | solution.py:41
  48.5 1.3 %collective-permute-start.8 = (f32[8,128,128]{2,1,0:T(8,128)S(1)}, f32[8,128,128]{2,1,0:T(8,128)S(1)}, u32[]{:S(2)}, u32[]{:S(2)}) collective-permute-start(f32[8,128,128]{2,1,0:T(8,128)S(1)} %get-tuple-element.70.b2), channel_id=1, source_target_pairs={{0,32},{64,96},{128,160},{160,192},{192,224},{1,33},{65,97},{129,1... | collective-permute-start | bytes 1572872 | tf_op jit(solution)/shard_map/ppermute | solution.py:430
  49.8 5.5 %collective-permute-done.5.mid = f32[5,64,128]{2,1,0:T(8,128)S(1)} collective-permute-done((f32[5,64,128]{2,1,0:T(8,128)S(1)}, f32[5,64,128]{2,1,0:T(8,128)S(1)}, u32[]{:S(2)}, u32[]{:S(2)}) %collective-permute-start.5) | collective-permute-done | bytes 163872 | tf_op jit(solution)/shard_map/ppermute | solution.py:41
  56.1 5.7 %collective-permute-start.7 = (f32[4,64,128]{2,1,0:T(8,128)S(1)}, f32[4,64,128]{2,1,0:T(8,128)S(1)}, u32[]{:S(2)}, u32[]{:S(2)}) collective-permute-start(f32[4,64,128]{2,1,0:T(8,128)S(1)} %get-tuple-element.79), channel_id=1, source_target_pairs={{0,31},{1,0},{2,1},{3,2},{4,3},{5,4},{6,5},{7,6},{8,7},{9,8},{10,9... | collective-permute-start | bytes 393224 | tf_op jit(solution)/shard_map/ppermute | solution.py:33
  61.8 2.3 %collective-permute-done.6.low = f32[4,64,128]{2,1,0:T(8,128)S(1)} collective-permute-done((f32[4,64,128]{2,1,0:T(8,128)S(1)}, f32[4,64,128]{2,1,0:T(8,128)S(1)}, u32[]{:S(2)}, u32[]{:S(2)}) %collective-permute-start.6) | collective-permute-done | bytes 131104 | tf_op jit(solution)/shard_map/ppermute | solution.py:33
  64.1 1.4 %shard_map.43 = (f32[5,64,128]{2,1,0:T(8,128)S(1)}, f32[13,64,128]{2,1,0:T(8,128)S(1)}) custom-call(s32[3]{0:T(128)S(1)} %pad_add_fusion.flags, f32[32,64,128]{2,1,0:T(8,128)S(1)} %get-tuple-element.60.ordered, f32[11,64,128]{2,1,0:T(8,128)S(1)} %get-tuple-element.61.mw, f32[11,64,128]{2,1,0:T(8,128)S(1)} %get-tuple-element.62.rw, ...), custom_call_target="tpu_custom_call" | custom-call | flops 1000000 | bytes 2785292 | tf_op jit(solution)/shard_map/pallas_call | solution.py:51
  66.3 5.8 %collective-permute-start.12 = (f32[4,64,128]{2,1,0:T(8,128)S(1)}, f32[4,64,128]{2,1,0:T(8,128)S(1)}, u32[]{:S(2)}, u32[]{:S(2)}) collective-permute-start(f32[4,64,128]{2,1,0:T(8,128)S(1)} %get-tuple-element.77), channel_id=1, source_target_pairs={{0,31},{1,0},{2,1},{3,2},{4,3},{5,4},{6,5},{7,6},{8,7},{9,8},{10,9... | collective-permute-start | bytes 393224 | tf_op jit(solution)/shard_map/ppermute | solution.py:33
  72.1 2.3 %collective-permute-done.11.low = f32[4,64,128]{2,1,0:T(8,128)S(1)} collective-permute-done((f32[4,64,128]{2,1,0:T(8,128)S(1)}, f32[4,64,128]{2,1,0:T(8,128)S(1)}, u32[]{:S(2)}, u32[]{:S(2)}) %collective-permute-start.11) | collective-permute-done | bytes 131104 | tf_op jit(solution)/shard_map/ppermute | solution.py:33
  74.4 1.4 %shard_map.44 = (f32[5,64,128]{2,1,0:T(8,128)S(1)}, f32[13,64,128]{2,1,0:T(8,128)S(1)}) custom-call(s32[3]{0:T(128)S(1)} %pad_add_fusion.flags, f32[32,64,128]{2,1,0:T(8,128)S(1)} %get-tuple-element.60.ordered, f32[11,64,128]{2,1,0:T(8,128)S(1)} %get-tuple-element.61.mw, f32[11,64,128]{2,1,0:T(8,128)S(1)} %get-tuple-element.62.rw, ...), custom_call_target="tpu_custom_call" | custom-call | flops 1000000 | bytes 3211276 | tf_op jit(solution)/shard_map/pallas_call | solution.py:51
  76.4 17.1 %collective-permute-start.13 = (f32[8,128,128]{2,1,0:T(8,128)S(1)}, f32[8,128,128]{2,1,0:T(8,128)S(1)}, u32[]{:S(2)}, u32[]{:S(2)}) collective-permute-start(f32[8,128,128]{2,1,0:T(8,128)S(1)} %get-tuple-element.70.b2), channel_id=1, source_target_pairs={{32,64},{33,65},{34,66},{35,67},{36,68},{37,69},{38,70},{39,71},{4... | collective-permute-start | bytes 1572872 | tf_op jit(solution)/shard_map/ppermute | solution.py:447
  93.7 6.0 %collective-permute-start.16 = (f32[4,64,128]{2,1,0:T(8,128)S(1)}, f32[4,64,128]{2,1,0:T(8,128)S(1)}, u32[]{:S(2)}, u32[]{:S(2)}) collective-permute-start(f32[4,64,128]{2,1,0:T(8,128)S(1)} %get-tuple-element.75), channel_id=1, source_target_pairs={{0,31},{1,0},{2,1},{3,2},{4,3},{5,4},{6,5},{7,6},{8,7},{9,8},{10,9... | collective-permute-start | bytes 393224 | tf_op jit(solution)/shard_map/ppermute | solution.py:33
  99.8 7.5 %collective-permute-done.15.low = f32[4,64,128]{2,1,0:T(8,128)S(1)} collective-permute-done((f32[4,64,128]{2,1,0:T(8,128)S(1)}, f32[4,64,128]{2,1,0:T(8,128)S(1)}, u32[]{:S(2)}, u32[]{:S(2)}) %collective-permute-start.15) | collective-permute-done | bytes 131104 | tf_op jit(solution)/shard_map/ppermute | solution.py:33
  107.3 2.1 %shard_map.45 = (f32[5,64,128]{2,1,0:T(8,128)}, f32[13,64,128]{2,1,0:T(8,128)}, f32[5,5,64,128]{3,2,1,0:T(8,128)S(1)}) custom-call(s32[3]{0:T(128)S(1)} %pad_add_fusion.flags, f32[32,64,128]{2,1,0:T(8,128)S(1)} %get-tuple-element.60.ordered, f32[11,64,128]{2,1,0:T(8,128)S(1)} %get-tuple-element.61.mw, f32[11,64,128]{2,1,0:T(8,128)S(1)} %get-tuple-element.62.rw, ...), custom_call_target="tpu_custom_call" | custom-call | flops 1000000 | bytes 4030476 | tf_op jit(solution)/shard_map/pallas_call | solution.py:51
  109.4 1.9 %shard_map.46 = f32[1,3,8,128,128]{4,3,2,1,0:T(8,128)} custom-call(s32[3]{0:T(128)S(1)} %pad_add_fusion.flags, f32[8,128,128]{2,1,0:T(8,128)S(1)} %slice_bitcast_fusion.start, f32[8,128,128]{2,1,0:T(8,128)S(1)} %get-tuple-element.51.b1, f32[8,128,128]{2,1,0:T(8,128)S(1)} %get-tuple-element.70.b2, f32[8,128,128]{2,1,0:T(8,128)S(1)} %collective-permute-done.8.b_before, ...), custom_call_target="tpu_custom_call" | custom-call | flops 1000000 | bytes 5537804 | tf_op jit(solution)/shard_map/pallas_call | solution.py:51
  (32 shorter events, 4.6 us)
Async XLA Ops:
  0.0 8.7 %copy-start = (f32[1,3,8,128,128]{4,3,2,1,0:T(8,128)S(1)}, f32[1,3,8,128,128]{4,3,2,1,0:T(8,128)}, u32[]{:S(2)}) copy-start(f32[1,3,8,128,128]{4,3,2,1,0:T(8,128)} %param.3) | copy-start | bytes 4718596
  0.0 8.7 %copy-start.1 = (f32[8,128,128]{2,1,0:T(8,128)S(1)}, f32[8,128,128]{2,1,0:T(8,128)}, u32[]{:S(2)}) copy-start(f32[8,128,128]{2,1,0:T(8,128)} %mob.3) | copy-start | bytes 1572868
  0.0 8.7 %copy-start.2 = (f32[8,128,128]{2,1,0:T(8,128)S(1)}, f32[8,128,128]{2,1,0:T(8,128)}, u32[]{:S(2)}) copy-start(f32[8,128,128]{2,1,0:T(8,128)} %rea.3) | copy-start | bytes 1572868
  2.9 19.9 %collective-permute-start = (f32[10,128,128]{2,1,0:T(8,128)S(1)}, f32[10,128,128]{2,1,0:T(8,128)S(1)}, u32[]{:S(2)}, u32[]{:S(2)}) collective-permute-start(f32[10,128,128]{2,1,0:T(8,128)S(1)} %get-tuple-element.40.to_right), channel_id=1, source_target_pairs={{0,1},{1,2},{2,3},{3,4},{4,5},{5,6},{6,7},{7,8},{8,9},{9,10},{10,1... | collective-permute-start | bytes 1966088 | tf_op jit(solution)/shard_map/ppermute | solution.py:33
  4.3 18.5 %collective-permute-start.1 = (f32[10,128,128]{2,1,0:T(8,128)S(1)}, f32[10,128,128]{2,1,0:T(8,128)S(1)}, u32[]{:S(2)}, u32[]{:S(2)}) collective-permute-start(f32[10,128,128]{2,1,0:T(8,128)S(1)} %get-tuple-element.41.to_left), channel_id=1, source_target_pairs={{0,31},{1,0},{2,1},{3,2},{4,3},{5,4},{6,5},{7,6},{8,7},{9,8},{10,9... | collective-permute-start | bytes 1966088 | tf_op jit(solution)/shard_map/ppermute | solution.py:33
  25.7 11.4 %collective-permute-start.2 = (f32[9,64,128]{2,1,0:T(8,128)S(1)}, f32[9,64,128]{2,1,0:T(8,128)S(1)}, u32[]{:S(2)}, u32[]{:S(2)}) collective-permute-start(f32[9,64,128]{2,1,0:T(8,128)S(1)} %get-tuple-element.49), channel_id=1, source_target_pairs={{0,1},{1,2},{2,3},{3,4},{4,5},{5,6},{6,7},{7,8},{8,9},{9,10},{10,1... | collective-permute-start | bytes 884744 | tf_op jit(solution)/shard_map/ppermute | solution.py:33
  25.8 11.3 %collective-permute-start.3 = (f32[9,64,128]{2,1,0:T(8,128)S(1)}, f32[9,64,128]{2,1,0:T(8,128)S(1)}, u32[]{:S(2)}, u32[]{:S(2)}) collective-permute-start(f32[9,64,128]{2,1,0:T(8,128)S(1)} %get-tuple-element.50), channel_id=1, source_target_pairs={{0,31},{1,0},{2,1},{3,2},{4,3},{5,4},{6,5},{7,6},{8,7},{9,8},{10,9... | collective-permute-start | bytes 884744 | tf_op jit(solution)/shard_map/ppermute | solution.py:33
  37.7 4.5 %collective-permute-start.4 = (f32[27,64,128]{2,1,0:T(8,128)S(1)}, f32[27,64,128]{2,1,0:T(8,128)S(1)}, u32[]{:S(2)}, u32[]{:S(2)}) collective-permute-start(f32[27,64,128]{2,1,0:T(8,128)S(1)} %shard_map.41.mine), channel_id=1, source_target_pairs={{0,32},{32,0},{64,96},{96,64},{128,160},{160,128},{192,224},{224,1... | collective-permute-start | bytes 2654216 | tf_op jit(solution)/shard_map/ppermute | solution.py:46
  43.4 11.9 %collective-permute-start.5 = (f32[5,64,128]{2,1,0:T(8,128)S(1)}, f32[5,64,128]{2,1,0:T(8,128)S(1)}, u32[]{:S(2)}, u32[]{:S(2)}) collective-permute-start(f32[5,64,128]{2,1,0:T(8,128)S(1)} %get-tuple-element.57), channel_id=1, source_target_pairs={{0,64},{32,96},{1,65},{33,97},{2,66},{34,98},{3,67},{35,99},{4,68}... | collective-permute-start | bytes 491528 | tf_op jit(solution)/shard_map/ppermute | solution.py:41
  48.5 13.3 %collective-permute-start.8 = (f32[8,128,128]{2,1,0:T(8,128)S(1)}, f32[8,128,128]{2,1,0:T(8,128)S(1)}, u32[]{:S(2)}, u32[]{:S(2)}) collective-permute-start(f32[8,128,128]{2,1,0:T(8,128)S(1)} %get-tuple-element.70.b2), channel_id=1, source_target_pairs={{0,32},{64,96},{128,160},{160,192},{192,224},{1,33},{65,97},{129,1... | collective-permute-start | bytes 1572872 | tf_op jit(solution)/shard_map/ppermute | solution.py:430
  55.3 10.2 %collective-permute-start.9 = (f32[8,128,128]{2,1,0:T(8,128)S(1)}, f32[8,128,128]{2,1,0:T(8,128)S(1)}, u32[]{:S(2)}, u32[]{:S(2)}) collective-permute-start(f32[8,128,128]{2,1,0:T(8,128)S(1)} %get-tuple-element.70.b2), channel_id=1, source_target_pairs={{96,128},{97,129},{98,130},{99,131},{100,132},{101,133},{102,134},... | collective-permute-start | bytes 1572872 | tf_op jit(solution)/shard_map/ppermute | solution.py:451
  56.0 8.1 %collective-permute-start.6 = (f32[4,64,128]{2,1,0:T(8,128)S(1)}, f32[4,64,128]{2,1,0:T(8,128)S(1)}, u32[]{:S(2)}, u32[]{:S(2)}) collective-permute-start(f32[4,64,128]{2,1,0:T(8,128)S(1)} %get-tuple-element.80), channel_id=1, source_target_pairs={{0,1},{1,2},{2,3},{3,4},{4,5},{5,6},{6,7},{7,8},{8,9},{9,10},{10,1... | collective-permute-start | bytes 393224 | tf_op jit(solution)/shard_map/ppermute | solution.py:33
  56.1 8.0 %collective-permute-start.7 = (f32[4,64,128]{2,1,0:T(8,128)S(1)}, f32[4,64,128]{2,1,0:T(8,128)S(1)}, u32[]{:S(2)}, u32[]{:S(2)}) collective-permute-start(f32[4,64,128]{2,1,0:T(8,128)S(1)} %get-tuple-element.79), channel_id=1, source_target_pairs={{0,31},{1,0},{2,1},{3,2},{4,3},{5,4},{6,5},{7,6},{8,7},{9,8},{10,9... | collective-permute-start | bytes 393224 | tf_op jit(solution)/shard_map/ppermute | solution.py:33
  65.5 0.7 collective-permute-start.10
  66.3 8.1 %collective-permute-start.11 = (f32[4,64,128]{2,1,0:T(8,128)S(1)}, f32[4,64,128]{2,1,0:T(8,128)S(1)}, u32[]{:S(2)}, u32[]{:S(2)}) collective-permute-start(f32[4,64,128]{2,1,0:T(8,128)S(1)} %get-tuple-element.78), channel_id=1, source_target_pairs={{0,1},{1,2},{2,3},{3,4},{4,5},{5,6},{6,7},{7,8},{8,9},{9,10},{10,1... | collective-permute-start | bytes 393224 | tf_op jit(solution)/shard_map/ppermute | solution.py:33
  66.3 8.0 %collective-permute-start.12 = (f32[4,64,128]{2,1,0:T(8,128)S(1)}, f32[4,64,128]{2,1,0:T(8,128)S(1)}, u32[]{:S(2)}, u32[]{:S(2)}) collective-permute-start(f32[4,64,128]{2,1,0:T(8,128)S(1)} %get-tuple-element.77), channel_id=1, source_target_pairs={{0,31},{1,0},{2,1},{3,2},{4,3},{5,4},{6,5},{7,6},{8,7},{9,8},{10,9... | collective-permute-start | bytes 393224 | tf_op jit(solution)/shard_map/ppermute | solution.py:33
  75.8 17.8 %collective-permute-start.14 = (f32[5,64,128]{2,1,0:T(8,128)S(1)}, f32[5,64,128]{2,1,0:T(8,128)S(1)}, u32[]{:S(2)}, u32[]{:S(2)}) collective-permute-start(f32[5,64,128]{2,1,0:T(8,128)S(1)} %get-tuple-element.72), channel_id=1, source_target_pairs={{128,192},{160,224},{129,193},{161,225},{130,194},{162,226},{131,1... | collective-permute-start | bytes 491528 | tf_op jit(solution)/shard_map/ppermute | solution.py:41
  76.4 32.9 %collective-permute-start.13 = (f32[8,128,128]{2,1,0:T(8,128)S(1)}, f32[8,128,128]{2,1,0:T(8,128)S(1)}, u32[]{:S(2)}, u32[]{:S(2)}) collective-permute-start(f32[8,128,128]{2,1,0:T(8,128)S(1)} %get-tuple-element.70.b2), channel_id=1, source_target_pairs={{32,64},{33,65},{34,66},{35,67},{36,68},{37,69},{38,70},{39,71},{4... | collective-permute-start | bytes 1572872 | tf_op jit(solution)/shard_map/ppermute | solution.py:447
  93.6 13.7 %collective-permute-start.15 = (f32[4,64,128]{2,1,0:T(8,128)S(1)}, f32[4,64,128]{2,1,0:T(8,128)S(1)}, u32[]{:S(2)}, u32[]{:S(2)}) collective-permute-start(f32[4,64,128]{2,1,0:T(8,128)S(1)} %get-tuple-element.76), channel_id=1, source_target_pairs={{0,1},{1,2},{2,3},{3,4},{4,5},{5,6},{6,7},{7,8},{8,9},{9,10},{10,1... | collective-permute-start | bytes 393224 | tf_op jit(solution)/shard_map/ppermute | solution.py:33
  93.7 13.6 %collective-permute-start.16 = (f32[4,64,128]{2,1,0:T(8,128)S(1)}, f32[4,64,128]{2,1,0:T(8,128)S(1)}, u32[]{:S(2)}, u32[]{:S(2)}) collective-permute-start(f32[4,64,128]{2,1,0:T(8,128)S(1)} %get-tuple-element.75), channel_id=1, source_target_pairs={{0,31},{1,0},{2,1},{3,2},{4,3},{5,4},{6,5},{7,6},{8,7},{9,8},{10,9... | collective-permute-start | bytes 393224 | tf_op jit(solution)/shard_map/ppermute | solution.py:33

commit v7 on v6

--- a/solution.py
+++ b/solution.py
@@ -366,7 +366,7 @@
     sweep(x0, ordered, mw, rw, last, levels, x1, x2, x3)
 
 
-def final_kernel(flags, start, b1, b2, b_before, b_late, b_later, levels, out, wide):
+def final_kernel(flags, start, b1, b2, b_before, b_late, b_later, levels, out_hbm, out, wide, sems):
     core = flags[0]
 
     def corrected(m, b):
@@ -374,20 +374,32 @@
             widen(levels[2 * core + m, j], wide, j)
         for j in range(4):
             low = wide[j]
-            out[0, m, 2 * j] = b[2 * j] + low
-            out[0, m, 2 * j + 1] = b[2 * j + 1] + 0.5 * (low + wide[j + 1])
-
+            out[m, 2 * j] = b[2 * j] + low
+            out[m, 2 * j + 1] = b[2 * j + 1] + 0.5 * (low + wide[j + 1])
+
+    copies = [pltpu.make_async_copy(out.at[m], out_hbm.at[0, m], sems.at[m]) for m in range(3)]
     corrected(1, b1)
+    copies[1].start()
     corrected(2, b2)
+    copies[2].start()
 
     @pl.when(flags[2] == 0)
     def _():
         for i in range(8):
-            out[0, 0, i] = start[i]
+            out[0, i] = start[i]
 
     pl.when(flags[2] == 2)(lambda: corrected(0, b_late))
     pl.when(flags[2] == 4)(lambda: corrected(0, b_later))
     pl.when((flags[2] != 0) & (flags[2] != 2) & (flags[2] != 4))(lambda: corrected(0, b_before))
+    copies[0].start()
+    for copy in copies:
+        copy.wait()
+
+
+def closing_kernel(turn, flags, ordered, mw, rw, mid, low, high, kept, *refs):
+    bases, (out_hbm, last, x0, levels, x1, x2, x3, out, wide, sems) = refs[:6], refs[6:]
+    turn_kernel(turn, True, flags, ordered, mw, rw, mid, low, high, kept, last, x0, levels, x1, x2, x3)
+    final_kernel(flags, *bases, levels, out_hbm, out, wide, sems)
 
 
 def body(nodes, mobility, reaction):
@@ -453,16 +465,21 @@
         high = ring(mid[1:5], "space", -1)
         if turn == 1:
             low, high, b_before = together(low, high, b_before)
-        last, kept, *levels = call(
-            functools.partial(turn_kernel, turn, final),
-            [(5,) + small, (13,) + small] + [(5, 5) + small] * final,
-            levels_shape,
-            flags, ordered, mw, rw, mid, low, high, *([kept] if turn > 1 else []), scalars=1,
-        )
-    (out,) = call(
-        final_kernel, [(1, 3, 8) + plane], [(5,) + plane], flags, states[0], b1, b2, b_before, b_late, b_later, levels[0], scalars=1,
-    )
-    return out
+        operands = (flags, ordered, mw, rw, mid, low, high) + ((kept,) if turn > 1 else ())
+        if not final:
+            last, kept = call(
+                functools.partial(turn_kernel, turn, False), [(5,) + small, (13,) + small], levels_shape, *operands, scalars=1
+            )
+    scratch = [(5,) + small, (13,) + small, (5, 5) + small] + levels_shape + [(3, 8) + plane, (5,) + plane]
+    return pl.pallas_call(
+        functools.partial(closing_kernel, turns - 1),
+        out_shape=jax.ShapeDtypeStruct((1, 3, 8) + plane, jnp.float32),
+        in_specs=[pl.BlockSpec(memory_space=pltpu.SMEM)] + [pl.BlockSpec(memory_space=pltpu.VMEM)] * 13,
+        out_specs=pl.BlockSpec(memory_space=pltpu.HBM),
+        scratch_shapes=[pltpu.VMEM(s, jnp.float32) for s in scratch] + [pltpu.SemaphoreType.DMA((3,))],
+        compiler_params=pltpu.CompilerParams(vmem_limit_bytes=12 * 1024 * 1024),
+        cost_estimate=cost(10**7, 8 * 10**6),
+    )(*operands, states[0], b1, b2, b_before, b_late, b_later)
 
 
 def solution(mesh):

time: 111 us -> 110 us (level)
  Pallas kernels: 16.2 us -> 14.9 us
    pallas_call x9 -> x7, Pallas kernels: 13.4 us -> 9.4 us  [call(): pl.pallas_call(kernel, out_shape=[jax.ShapeDtypeStruct(s, jnp.float32) fo...]
    pallas_call x0 -> x1, Pallas kernels: none -> 2.69 us  [body(): pl.pallas_call(functools.partial(closing_kernel, turns - 1), out_shape=ja...]
  transfers between devices with their start and end apart: 17 -> 17, of which waited for: 7 -> 7; matrix products, arithmetic and copies ran while one was open for 0% -> 0% of each run, Pallas kernels for 5% -> 3%
where the time goes in v7:
time: 110 us
  starting transfers between devices  57 us (52%)
  waiting for transfers between devices  37.7 us (34%)
  Pallas kernels  14.9 us (14%)
    ppermute x10, waiting for transfers between devices, ring(): lax.ppermute(values, axis, [(i, (i + distance) % count) for i in range(co...  30.2 us
    ppermute x10, starting transfers between devices, ring(): lax.ppermute(values, axis, [(i, (i + distance) % count) for i in range(co...  29.2 us
    ppermute x1, starting transfers between devices, body(): b_late = lax.ppermute(sent, 'tm', [(1, 2)])  17.1 us
    pallas_call x7, Pallas kernels, call(): pl.pallas_call(kernel, out_shape=[jax.ShapeDtypeStruct(s, jnp.float32) fo...  9.4 us
    ppermute x3, starting transfers between devices, hop(): lax.ppermute(values, 'tm', [(2 * turn - 2 + core, 2 * turn + core) for co...  6.25 us
    ppermute x3, waiting for transfers between devices, hop(): lax.ppermute(values, 'tm', [(2 * turn - 2 + core, 2 * turn + core) for co...  5.5 us
    pallas_call x1, Pallas kernels, body(): pl.pallas_call(edge_kernel, out_shape=[jax.ShapeDtypeStruct(s, jnp.float3...  2.78 us
    pallas_call x1, Pallas kernels, body(): pl.pallas_call(functools.partial(closing_kernel, turns - 1), out_shape=ja...  2.69 us
  transfers between devices with their start and end apart: 17, of which 7 were waited for; matrix products, arithmetic and copies ran while one was open for 0% of the time, Pallas kernels for 3%

profile of v7, /device:TPU:33, one launch (start us, length us, event | category | flops | bytes accessed | tf_op | source)
XLA Modules:
  0.0 110.2 jit_solution(2113328155639091541)
XLA Ops:
  0.1 2.8 %shard_map.37 = (f32[2,4,64,128]{3,2,1,0:T(8,128)S(1)}, f32[10,128,128]{2,1,0:T(8,128)S(1)}, f32[10,128,128]{2,1,0:T(8,128)S(1)}) custom-call(s32[3]{0:T(128)S(1)} %pad_add_fusion.flags, f32[3,8,128,128]{3,2,1,0:T(8,128)} %bitcast.8, f32[8,128,128]{2,1,0:T(8,128)} %mob.3, f32[8,128,128]{2,1,0:T(8,128)} %rea.3), custom_call_target="tpu_custom_call" | custom-call | flops 1000000 | bytes 4000000 | tf_op jit(solution)/shard_map/pallas_call | solution.py:414
  2.9 1.4 %collective-permute-start = (f32[10,128,128]{2,1,0:T(8,128)S(1)}, f32[10,128,128]{2,1,0:T(8,128)S(1)}, u32[]{:S(2)}, u32[]{:S(2)}) collective-permute-start(f32[10,128,128]{2,1,0:T(8,128)S(1)} %get-tuple-element.39.to_right), channel_id=1, source_target_pairs={{0,1},{1,2},{2,3},{3,4},{4,5},{5,6},{6,7},{7,8},{8,9},{9,10},{10,1... | collective-permute-start | bytes 1966088 | tf_op jit(solution)/shard_map/ppermute | solution.py:33
  4.3 4.4 %collective-permute-start.1 = (f32[10,128,128]{2,1,0:T(8,128)S(1)}, f32[10,128,128]{2,1,0:T(8,128)S(1)}, u32[]{:S(2)}, u32[]{:S(2)}) collective-permute-start(f32[10,128,128]{2,1,0:T(8,128)S(1)} %get-tuple-element.40.to_left), channel_id=1, source_target_pairs={{0,31},{1,0},{2,1},{3,2},{4,3},{5,4},{6,5},{7,6},{8,7},{9,8},{10,9... | collective-permute-start | bytes 1966088 | tf_op jit(solution)/shard_map/ppermute | solution.py:33
  8.7 1.7 %shard_map.38 = (f32[8,128,128]{2,1,0:T(8,128)S(1)}, f32[8,128,128]{2,1,0:T(8,128)S(1)}, f32[8,128,128]{2,1,0:T(8,128)S(1)}) custom-call(f32[3,8,128,128]{3,2,1,0:T(8,128)S(1)} %bitcast.9, f32[8,128,128]{2,1,0:T(8,128)S(1)} %copy-done.1, f32[8,128,128]{2,1,0:T(8,128)S(1)} %copy-done.2), custom_call_target="tpu_custom_call" | custom-call | flops 10000000 | bytes 4194304 | tf_op jit(solution)/shard_map/pallas_call | solution.py:51
  10.4 12.4 %collective-permute-done.left = f32[10,128,128]{2,1,0:T(8,128)S(1)} collective-permute-done((f32[10,128,128]{2,1,0:T(8,128)S(1)}, f32[10,128,128]{2,1,0:T(8,128)S(1)}, u32[]{:S(2)}, u32[]{:S(2)}) %collective-permute-start) | collective-permute-done | bytes 655392 | tf_op jit(solution)/shard_map/ppermute | solution.py:33
  22.8 2.9 %shard_map.39 = (f32[8,128,128]{2,1,0:T(8,128)S(1)}, f32[8,128,128]{2,1,0:T(8,128)S(1)}, f32[8,64,128]{2,1,0:T(8,128)S(1)}, f32[5,64,128]{2,1,0:T(8,128)S(1)}, f...) custom-call(s32[3]{0:T(128)S(1)} %pad_add_fusion.flags, ...), custom_call_target="tpu_custom_call" | custom-call | flops 20000000 | bytes 9732108 | tf_op jit(solution)/shard_map/pallas_call | solution.py:51
  25.8 5.7 %collective-permute-start.3 = (f32[9,64,128]{2,1,0:T(8,128)S(1)}, f32[9,64,128]{2,1,0:T(8,128)S(1)}, u32[]{:S(2)}, u32[]{:S(2)}) collective-permute-start(f32[9,64,128]{2,1,0:T(8,128)S(1)} %get-tuple-element.51), channel_id=1, source_target_pairs={{0,31},{1,0},{2,1},{3,2},{4,3},{5,4},{6,5},{7,6},{8,7},{9,8},{10,9... | collective-permute-start | bytes 884744 | tf_op jit(solution)/shard_map/ppermute | solution.py:33
  31.5 5.6 %collective-permute-done.2.from_left = f32[9,64,128]{2,1,0:T(8,128)S(1)} collective-permute-done((f32[9,64,128]{2,1,0:T(8,128)S(1)}, f32[9,64,128]{2,1,0:T(8,128)S(1)}, u32[]{:S(2)}, u32[]{:S(2)}) %collective-permute-start.2) | collective-permute-done | bytes 294944 | tf_op jit(solution)/shard_map/ppermute | solution.py:33
  37.7 2.4 %collective-permute-start.4 = (f32[27,64,128]{2,1,0:T(8,128)S(1)}, f32[27,64,128]{2,1,0:T(8,128)S(1)}, u32[]{:S(2)}, u32[]{:S(2)}) collective-permute-start(f32[27,64,128]{2,1,0:T(8,128)S(1)} %shard_map.40.mine), channel_id=1, source_target_pairs={{0,32},{32,0},{64,96},{96,64},{128,160},{160,128},{192,224},{224,1... | collective-permute-start | bytes 2654216 | tf_op jit(solution)/shard_map/ppermute | solution.py:46
  40.2 2.1 %collective-permute-done.4.other = f32[27,64,128]{2,1,0:T(8,128)S(1)} collective-permute-done((f32[27,64,128]{2,1,0:T(8,128)S(1)}, f32[27,64,128]{2,1,0:T(8,128)S(1)}, u32[]{:S(2)}, u32[]{:S(2)}) %collective-permute-start.4) | collective-permute-done | bytes 884768 | tf_op jit(solution)/shard_map/ppermute | solution.py:46
  42.2 1.2 %shard_map.41 = (f32[5,64,128]{2,1,0:T(8,128)S(1)}, f32[32,64,128]{2,1,0:T(8,128)S(1)}, f32[11,64,128]{2,1,0:T(8,128)S(1)}, f32[11,64,128]{2,1,0:T(8,128)S(1)}) custom-call(s32[3]{0:T(128)S(1)} %pad_add_fusion.flags, f32[27,64,128]{2,1,0:T(8,128)S(1)} %shard_map.40.mine, f32[27,64,128]{2,1,0:T(8,128)S(1)} %collective-permute-done.4.other, ...), custom_call_target="tpu_custom_call" | custom-call | flops 1000000 | bytes 4227084 | tf_op jit(solution)/shard_map/pallas_call | solution.py:51
  43.4 4.9 %collective-permute-start.5 = (f32[5,64,128]{2,1,0:T(8,128)S(1)}, f32[5,64,128]{2,1,0:T(8,128)S(1)}, u32[]{:S(2)}, u32[]{:S(2)}) collective-permute-start(f32[5,64,128]{2,1,0:T(8,128)S(1)} %get-tuple-element.55), channel_id=1, source_target_pairs={{0,64},{32,96},{1,65},{33,97},{2,66},{34,98},{3,67},{35,99},{4,68}... | collective-permute-start | bytes 491528 | tf_op jit(solution)/shard_map/ppermute | solution.py:41
  48.5 1.3 %collective-permute-start.8 = (f32[8,128,128]{2,1,0:T(8,128)S(1)}, f32[8,128,128]{2,1,0:T(8,128)S(1)}, u32[]{:S(2)}, u32[]{:S(2)}) collective-permute-start(f32[8,128,128]{2,1,0:T(8,128)S(1)} %get-tuple-element.71.refs_2_), channel_id=1, source_target_pairs={{0,32},{64,96},{128,160},{160,192},{192,224},{1,33},{65,97},{129,1... | collective-permute-start | bytes 1572872 | tf_op jit(solution)/shard_map/ppermute | solution.py:442
  49.8 5.5 %collective-permute-done.5.mid = f32[5,64,128]{2,1,0:T(8,128)S(1)} collective-permute-done((f32[5,64,128]{2,1,0:T(8,128)S(1)}, f32[5,64,128]{2,1,0:T(8,128)S(1)}, u32[]{:S(2)}, u32[]{:S(2)}) %collective-permute-start.5) | collective-permute-done | bytes 163872 | tf_op jit(solution)/shard_map/ppermute | solution.py:41
  56.1 5.7 %collective-permute-start.7 = (f32[4,64,128]{2,1,0:T(8,128)S(1)}, f32[4,64,128]{2,1,0:T(8,128)S(1)}, u32[]{:S(2)}, u32[]{:S(2)}) collective-permute-start(f32[4,64,128]{2,1,0:T(8,128)S(1)} %get-tuple-element.77), channel_id=1, source_target_pairs={{0,31},{1,0},{2,1},{3,2},{4,3},{5,4},{6,5},{7,6},{8,7},{9,8},{10,9... | collective-permute-start | bytes 393224 | tf_op jit(solution)/shard_map/ppermute | solution.py:33
  61.8 2.3 %collective-permute-done.6.low = f32[4,64,128]{2,1,0:T(8,128)S(1)} collective-permute-done((f32[4,64,128]{2,1,0:T(8,128)S(1)}, f32[4,64,128]{2,1,0:T(8,128)S(1)}, u32[]{:S(2)}, u32[]{:S(2)}) %collective-permute-start.6) | collective-permute-done | bytes 131104 | tf_op jit(solution)/shard_map/ppermute | solution.py:33
  64.1 1.4 %shard_map.43 = (f32[5,64,128]{2,1,0:T(8,128)S(1)}, f32[13,64,128]{2,1,0:T(8,128)S(1)}) custom-call(s32[3]{0:T(128)S(1)} %pad_add_fusion.flags, f32[32,64,128]{2,1,0:T(8,128)S(1)} %get-tuple-element.52.ordered, f32[11,64,128]{2,1,0:T(8,128)S(1)} %get-tuple-element.53.mw, f32[11,64,128]{2,1,0:T(8,128)S(1)} %get-tuple-element.54.rw, ...), custom_call_target="tpu_custom_call" | custom-call | flops 1000000 | bytes 2785292 | tf_op jit(solution)/shard_map/pallas_call | solution.py:51
  66.3 5.8 %collective-permute-start.12 = (f32[4,64,128]{2,1,0:T(8,128)S(1)}, f32[4,64,128]{2,1,0:T(8,128)S(1)}, u32[]{:S(2)}, u32[]{:S(2)}) collective-permute-start(f32[4,64,128]{2,1,0:T(8,128)S(1)} %get-tuple-element.75), channel_id=1, source_target_pairs={{0,31},{1,0},{2,1},{3,2},{4,3},{5,4},{6,5},{7,6},{8,7},{9,8},{10,9... | collective-permute-start | bytes 393224 | tf_op jit(solution)/shard_map/ppermute | solution.py:33
  72.1 2.3 %collective-permute-done.11.low = f32[4,64,128]{2,1,0:T(8,128)S(1)} collective-permute-done((f32[4,64,128]{2,1,0:T(8,128)S(1)}, f32[4,64,128]{2,1,0:T(8,128)S(1)}, u32[]{:S(2)}, u32[]{:S(2)}) %collective-permute-start.11) | collective-permute-done | bytes 131104 | tf_op jit(solution)/shard_map/ppermute | solution.py:33
  74.4 1.4 %shard_map.44 = (f32[5,64,128]{2,1,0:T(8,128)S(1)}, f32[13,64,128]{2,1,0:T(8,128)S(1)}) custom-call(s32[3]{0:T(128)S(1)} %pad_add_fusion.flags, f32[32,64,128]{2,1,0:T(8,128)S(1)} %get-tuple-element.52.ordered, f32[11,64,128]{2,1,0:T(8,128)S(1)} %get-tuple-element.53.mw, f32[11,64,128]{2,1,0:T(8,128)S(1)} %get-tuple-element.54.rw, ...), custom_call_target="tpu_custom_call" | custom-call | flops 1000000 | bytes 3211276 | tf_op jit(solution)/shard_map/pallas_call | solution.py:51
  76.4 17.1 %collective-permute-start.16 = (f32[8,128,128]{2,1,0:T(8,128)S(1)}, f32[8,128,128]{2,1,0:T(8,128)S(1)}, u32[]{:S(2)}, u32[]{:S(2)}) collective-permute-start(f32[8,128,128]{2,1,0:T(8,128)S(1)} %get-tuple-element.71.refs_2_), channel_id=1, source_target_pairs={{32,64},{33,65},{34,66},{35,67},{36,68},{37,69},{38,70},{39,71},{4... | collective-permute-start | bytes 1572872 | tf_op jit(solution)/shard_map/ppermute | solution.py:459
  93.7 6.0 %collective-permute-start.15 = (f32[4,64,128]{2,1,0:T(8,128)S(1)}, f32[4,64,128]{2,1,0:T(8,128)S(1)}, u32[]{:S(2)}, u32[]{:S(2)}) collective-permute-start(f32[4,64,128]{2,1,0:T(8,128)S(1)} %get-tuple-element.73), channel_id=1, source_target_pairs={{0,31},{1,0},{2,1},{3,2},{4,3},{5,4},{6,5},{7,6},{8,7},{9,8},{10,9... | collective-permute-start | bytes 393224 | tf_op jit(solution)/shard_map/ppermute | solution.py:33
  99.8 7.5 %collective-permute-done.14.low = f32[4,64,128]{2,1,0:T(8,128)S(1)} collective-permute-done((f32[4,64,128]{2,1,0:T(8,128)S(1)}, f32[4,64,128]{2,1,0:T(8,128)S(1)}, u32[]{:S(2)}, u32[]{:S(2)}) %collective-permute-start.14) | collective-permute-done | bytes 131104 | tf_op jit(solution)/shard_map/ppermute | solution.py:33
  107.3 2.7 %shard_map.45 = f32[1,3,8,128,128]{4,3,2,1,0:T(8,128)} custom-call(s32[3]{0:T(128)S(1)} %pad_add_fusion.flags, f32[32,64,128]{2,1,0:T(8,128)S(1)} %get-tuple-element.52.ordered, f32[11,64,128]{2,1,0:T(8,128)S(1)} %get-tuple-element.53.mw, f32[11,64,128]{2,1,0:T(8,128)S(1)} %get-tuple-element.54.rw, f32[5,64,128]{2,1,0:T(8,128)S(1)} %collective-permute-done.13.mid, ...), custom_call_target="tpu_custom_call" | custom-call | flops 10000000 | bytes 8000000 | tf_op jit(solution)/shard_map/pallas_call | solution.py:474
  (31 shorter events, 3.3 us)
Async XLA Ops:
  0.0 8.7 %copy-start = (f32[1,3,8,128,128]{4,3,2,1,0:T(8,128)S(1)}, f32[1,3,8,128,128]{4,3,2,1,0:T(8,128)}, u32[]{:S(2)}) copy-start(f32[1,3,8,128,128]{4,3,2,1,0:T(8,128)} %param.3) | copy-start | bytes 4718596
  0.0 8.7 %copy-start.1 = (f32[8,128,128]{2,1,0:T(8,128)S(1)}, f32[8,128,128]{2,1,0:T(8,128)}, u32[]{:S(2)}) copy-start(f32[8,128,128]{2,1,0:T(8,128)} %mob.3) | copy-start | bytes 1572868
  0.0 8.7 %copy-start.2 = (f32[8,128,128]{2,1,0:T(8,128)S(1)}, f32[8,128,128]{2,1,0:T(8,128)}, u32[]{:S(2)}) copy-start(f32[8,128,128]{2,1,0:T(8,128)} %rea.3) | copy-start | bytes 1572868
  2.9 19.9 %collective-permute-start = (f32[10,128,128]{2,1,0:T(8,128)S(1)}, f32[10,128,128]{2,1,0:T(8,128)S(1)}, u32[]{:S(2)}, u32[]{:S(2)}) collective-permute-start(f32[10,128,128]{2,1,0:T(8,128)S(1)} %get-tuple-element.39.to_right), channel_id=1, source_target_pairs={{0,1},{1,2},{2,3},{3,4},{4,5},{5,6},{6,7},{7,8},{8,9},{9,10},{10,1... | collective-permute-start | bytes 1966088 | tf_op jit(solution)/shard_map/ppermute | solution.py:33
  4.3 18.5 %collective-permute-start.1 = (f32[10,128,128]{2,1,0:T(8,128)S(1)}, f32[10,128,128]{2,1,0:T(8,128)S(1)}, u32[]{:S(2)}, u32[]{:S(2)}) collective-permute-start(f32[10,128,128]{2,1,0:T(8,128)S(1)} %get-tuple-element.40.to_left), channel_id=1, source_target_pairs={{0,31},{1,0},{2,1},{3,2},{4,3},{5,4},{6,5},{7,6},{8,7},{9,8},{10,9... | collective-permute-start | bytes 1966088 | tf_op jit(solution)/shard_map/ppermute | solution.py:33
  25.7 11.4 %collective-permute-start.2 = (f32[9,64,128]{2,1,0:T(8,128)S(1)}, f32[9,64,128]{2,1,0:T(8,128)S(1)}, u32[]{:S(2)}, u32[]{:S(2)}) collective-permute-start(f32[9,64,128]{2,1,0:T(8,128)S(1)} %get-tuple-element.50), channel_id=1, source_target_pairs={{0,1},{1,2},{2,3},{3,4},{4,5},{5,6},{6,7},{7,8},{8,9},{9,10},{10,1... | collective-permute-start | bytes 884744 | tf_op jit(solution)/shard_map/ppermute | solution.py:33
  25.8 11.3 %collective-permute-start.3 = (f32[9,64,128]{2,1,0:T(8,128)S(1)}, f32[9,64,128]{2,1,0:T(8,128)S(1)}, u32[]{:S(2)}, u32[]{:S(2)}) collective-permute-start(f32[9,64,128]{2,1,0:T(8,128)S(1)} %get-tuple-element.51), channel_id=1, source_target_pairs={{0,31},{1,0},{2,1},{3,2},{4,3},{5,4},{6,5},{7,6},{8,7},{9,8},{10,9... | collective-permute-start | bytes 884744 | tf_op jit(solution)/shard_map/ppermute | solution.py:33
  37.7 4.5 %collective-permute-start.4 = (f32[27,64,128]{2,1,0:T(8,128)S(1)}, f32[27,64,128]{2,1,0:T(8,128)S(1)}, u32[]{:S(2)}, u32[]{:S(2)}) collective-permute-start(f32[27,64,128]{2,1,0:T(8,128)S(1)} %shard_map.40.mine), channel_id=1, source_target_pairs={{0,32},{32,0},{64,96},{96,64},{128,160},{160,128},{192,224},{224,1... | collective-permute-start | bytes 2654216 | tf_op jit(solution)/shard_map/ppermute | solution.py:46
  43.4 11.9 %collective-permute-start.5 = (f32[5,64,128]{2,1,0:T(8,128)S(1)}, f32[5,64,128]{2,1,0:T(8,128)S(1)}, u32[]{:S(2)}, u32[]{:S(2)}) collective-permute-start(f32[5,64,128]{2,1,0:T(8,128)S(1)} %get-tuple-element.55), channel_id=1, source_target_pairs={{0,64},{32,96},{1,65},{33,97},{2,66},{34,98},{3,67},{35,99},{4,68}... | collective-permute-start | bytes 491528 | tf_op jit(solution)/shard_map/ppermute | solution.py:41
  48.5 13.3 %collective-permute-start.8 = (f32[8,128,128]{2,1,0:T(8,128)S(1)}, f32[8,128,128]{2,1,0:T(8,128)S(1)}, u32[]{:S(2)}, u32[]{:S(2)}) collective-permute-start(f32[8,128,128]{2,1,0:T(8,128)S(1)} %get-tuple-element.71.refs_2_), channel_id=1, source_target_pairs={{0,32},{64,96},{128,160},{160,192},{192,224},{1,33},{65,97},{129,1... | collective-permute-start | bytes 1572872 | tf_op jit(solution)/shard_map/ppermute | solution.py:442
  55.3 10.2 %collective-permute-start.9 = (f32[8,128,128]{2,1,0:T(8,128)S(1)}, f32[8,128,128]{2,1,0:T(8,128)S(1)}, u32[]{:S(2)}, u32[]{:S(2)}) collective-permute-start(f32[8,128,128]{2,1,0:T(8,128)S(1)} %get-tuple-element.71.refs_2_), channel_id=1, source_target_pairs={{96,128},{97,129},{98,130},{99,131},{100,132},{101,133},{102,134},... | collective-permute-start | bytes 1572872 | tf_op jit(solution)/shard_map/ppermute | solution.py:463
  56.0 8.1 %collective-permute-start.6 = (f32[4,64,128]{2,1,0:T(8,128)S(1)}, f32[4,64,128]{2,1,0:T(8,128)S(1)}, u32[]{:S(2)}, u32[]{:S(2)}) collective-permute-start(f32[4,64,128]{2,1,0:T(8,128)S(1)} %get-tuple-element.78), channel_id=1, source_target_pairs={{0,1},{1,2},{2,3},{3,4},{4,5},{5,6},{6,7},{7,8},{8,9},{9,10},{10,1... | collective-permute-start | bytes 393224 | tf_op jit(solution)/shard_map/ppermute | solution.py:33
  56.1 8.0 %collective-permute-start.7 = (f32[4,64,128]{2,1,0:T(8,128)S(1)}, f32[4,64,128]{2,1,0:T(8,128)S(1)}, u32[]{:S(2)}, u32[]{:S(2)}) collective-permute-start(f32[4,64,128]{2,1,0:T(8,128)S(1)} %get-tuple-element.77), channel_id=1, source_target_pairs={{0,31},{1,0},{2,1},{3,2},{4,3},{5,4},{6,5},{7,6},{8,7},{9,8},{10,9... | collective-permute-start | bytes 393224 | tf_op jit(solution)/shard_map/ppermute | solution.py:33
  65.5 0.7 collective-permute-start.10
  66.3 8.1 %collective-permute-start.11 = (f32[4,64,128]{2,1,0:T(8,128)S(1)}, f32[4,64,128]{2,1,0:T(8,128)S(1)}, u32[]{:S(2)}, u32[]{:S(2)}) collective-permute-start(f32[4,64,128]{2,1,0:T(8,128)S(1)} %get-tuple-element.76), channel_id=1, source_target_pairs={{0,1},{1,2},{2,3},{3,4},{4,5},{5,6},{6,7},{7,8},{8,9},{9,10},{10,1... | collective-permute-start | bytes 393224 | tf_op jit(solution)/shard_map/ppermute | solution.py:33
  66.3 8.0 %collective-permute-start.12 = (f32[4,64,128]{2,1,0:T(8,128)S(1)}, f32[4,64,128]{2,1,0:T(8,128)S(1)}, u32[]{:S(2)}, u32[]{:S(2)}) collective-permute-start(f32[4,64,128]{2,1,0:T(8,128)S(1)} %get-tuple-element.75), channel_id=1, source_target_pairs={{0,31},{1,0},{2,1},{3,2},{4,3},{5,4},{6,5},{7,6},{8,7},{9,8},{10,9... | collective-permute-start | bytes 393224 | tf_op jit(solution)/shard_map/ppermute | solution.py:33
  75.8 17.8 %collective-permute-start.13 = (f32[5,64,128]{2,1,0:T(8,128)S(1)}, f32[5,64,128]{2,1,0:T(8,128)S(1)}, u32[]{:S(2)}, u32[]{:S(2)}) collective-permute-start(f32[5,64,128]{2,1,0:T(8,128)S(1)} %get-tuple-element.67), channel_id=1, source_target_pairs={{128,192},{160,224},{129,193},{161,225},{130,194},{162,226},{131,1... | collective-permute-start | bytes 491528 | tf_op jit(solution)/shard_map/ppermute | solution.py:41
  76.4 30.9 %collective-permute-start.16 = (f32[8,128,128]{2,1,0:T(8,128)S(1)}, f32[8,128,128]{2,1,0:T(8,128)S(1)}, u32[]{:S(2)}, u32[]{:S(2)}) collective-permute-start(f32[8,128,128]{2,1,0:T(8,128)S(1)} %get-tuple-element.71.refs_2_), channel_id=1, source_target_pairs={{32,64},{33,65},{34,66},{35,67},{36,68},{37,69},{38,70},{39,71},{4... | collective-permute-start | bytes 1572872 | tf_op jit(solution)/shard_map/ppermute | solution.py:459
  93.6 13.7 %collective-permute-start.14 = (f32[4,64,128]{2,1,0:T(8,128)S(1)}, f32[4,64,128]{2,1,0:T(8,128)S(1)}, u32[]{:S(2)}, u32[]{:S(2)}) collective-permute-start(f32[4,64,128]{2,1,0:T(8,128)S(1)} %get-tuple-element.74), channel_id=1, source_target_pairs={{0,1},{1,2},{2,3},{3,4},{4,5},{5,6},{6,7},{7,8},{8,9},{9,10},{10,1... | collective-permute-start | bytes 393224 | tf_op jit(solution)/shard_map/ppermute | solution.py:33
  93.7 13.6 %collective-permute-start.15 = (f32[4,64,128]{2,1,0:T(8,128)S(1)}, f32[4,64,128]{2,1,0:T(8,128)S(1)}, u32[]{:S(2)}, u32[]{:S(2)}) collective-permute-start(f32[4,64,128]{2,1,0:T(8,128)S(1)} %get-tuple-element.73), channel_id=1, source_target_pairs={{0,31},{1,0},{2,1},{3,2},{4,3},{5,4},{6,5},{7,6},{8,7},{9,8},{10,9... | collective-permute-start | bytes 393224 | tf_op jit(solution)/shard_map/ppermute | solution.py:33

commit v8 on v7

--- a/solution.py
+++ b/solution.py
@@ -26,6 +26,11 @@
 
 def cost(flops, moved):
     return pl.CostEstimate(flops=flops, bytes_accessed=moved, transcendentals=0)
+
+
+def where():
+    index = lax.axis_index("tm")
+    return index & 1, index >> 1, index
 
 
 def ring(values, axis, distance):
@@ -80,7 +85,8 @@
     return [cubic(nodes[m, plane]) for m in range(3)]
 
 
-def edge_kernel(flags, nodes_hbm, mob_hbm, rea_hbm, own, rightward, leftward, mix, nodes, mob, rea, sems):
+def edge_kernel(nodes_hbm, mob_hbm, rea_hbm, own, rightward, leftward, mix, nodes, mob, rea, sems):
+    flags = where()
     half = mob.shape[1] // 2
     copies = [pltpu.make_async_copy(mob_hbm, mob, sems.at[0]), pltpu.make_async_copy(rea_hbm, rea, sems.at[1])]
     for m in range(3):
@@ -166,10 +172,11 @@
 
 
 def fine_kernel(
-    flags, nodes, mob, rea, left, right, to_right, to_left, own, v1_own, step_own, first_own,
+    nodes, mob, rea, left, right, to_right, to_left, own, v1_own, step_own, first_own,
     v1_out, v2_out, q, start, coarse, share, outer, rightward, leftward,
     mw, rw, v1, v2, step, first, f1, jj, mix,
 ):
+    flags = where()
     half = mob.shape[1] // 2
 
     @pl.loop(0, 8)
@@ -275,8 +282,8 @@
             b[2 * j + 1] = v[2 * j + 1] - 0.5 * (low + mix[j + 1])
 
 
-def pack_kernel(flags, q, start, c1, share, own, outer, from_left, from_right, window):
-    keep = jnp.where(flags[2] == 0, 0.0, 1.0)
+def pack_kernel(q, start, c1, share, own, outer, from_left, from_right, window):
+    keep = jnp.where(where()[2] == 0, 0.0, 1.0)
     window[0] = from_left[0]
     window[1] = from_left[1]
     window[2] = from_left[2]
@@ -337,13 +344,15 @@
             levels[4, i] = last[i]
 
 
-def first_kernel(flags, mine, other, own, outer, last, ordered, mw, rw, x2, x3):
+def first_kernel(mine, other, own, outer, last, ordered, mw, rw, x2, x3):
+    flags = where()
     pl.when(flags[0] == 0)(lambda: order(mine, other, own, outer, ordered, mw, rw))
     pl.when(flags[0] != 0)(lambda: order(other, mine, own, outer, ordered, mw, rw))
     sweep(None, ordered, mw, rw, last, None, ordered.at[pl.ds(0, 11)], x2, x3)
 
 
-def turn_kernel(turn, final, flags, ordered, mw, rw, mid, low, high, *refs):
+def turn_kernel(turn, final, ordered, mw, rw, mid, low, high, *refs):
+    flags = where()
     if turn > 1:
         kept, *refs = refs
     last, x0 = refs[:2]
@@ -366,8 +375,8 @@
     sweep(x0, ordered, mw, rw, last, levels, x1, x2, x3)
 
 
-def final_kernel(flags, start, b1, b2, b_before, b_late, b_later, levels, out_hbm, out, wide, sems):
-    core = flags[0]
+def final_kernel(start, b1, b2, b_before, b_late, b_later, levels, out_hbm, out, wide, sems):
+    core = where()[0]
 
     def corrected(m, b):
         for j in range(5):
@@ -377,6 +386,7 @@
             out[m, 2 * j] = b[2 * j] + low
             out[m, 2 * j + 1] = b[2 * j + 1] + 0.5 * (low + wide[j + 1])
 
+    flags = where()
     copies = [pltpu.make_async_copy(out.at[m], out_hbm.at[0, m], sems.at[m]) for m in range(3)]
     corrected(1, b1)
     copies[1].start()
@@ -396,10 +406,10 @@
         copy.wait()
 
 
-def closing_kernel(turn, flags, ordered, mw, rw, mid, low, high, kept, *refs):
+def closing_kernel(turn, ordered, mw, rw, mid, low, high, kept, *refs):
     bases, (out_hbm, last, x0, levels, x1, x2, x3, out, wide, sems) = refs[:6], refs[6:]
-    turn_kernel(turn, True, flags, ordered, mw, rw, mid, low, high, kept, last, x0, levels, x1, x2, x3)
-    final_kernel(flags, *bases, levels, out_hbm, out, wide, sems)
+    turn_kernel(turn, True, ordered, mw, rw, mid, low, high, kept, last, x0, levels, x1, x2, x3)
+    final_kernel(*bases, levels, out_hbm, out, wide, sems)
 
 
 def body(nodes, mobility, reaction):
@@ -408,19 +418,17 @@
     hy = ny // 2
     plane = (ny, nz)
     small = (hy, nz)
-    slice_index = lax.axis_index("tm")
-    flags = jnp.stack([slice_index % 2, slice_index // 2, slice_index]).astype(jnp.int32)
 
     own, to_right, to_left = pl.pallas_call(
         edge_kernel,
         out_shape=[jax.ShapeDtypeStruct(s, jnp.float32) for s in ((2, 4) + small, (10,) + plane, (10,) + plane)],
-        in_specs=[pl.BlockSpec(memory_space=pltpu.SMEM)] + [pl.BlockSpec(memory_space=pltpu.HBM)] * 3,
+        in_specs=[pl.BlockSpec(memory_space=pltpu.HBM)] * 3,
         out_specs=[pl.BlockSpec(memory_space=pltpu.VMEM)] * 3,
         scratch_shapes=[pltpu.VMEM(s, jnp.float32) for s in (plane, (3, 8) + plane, (8,) + plane, (8,) + plane)]
         + [pltpu.SemaphoreType.DMA((8,))],
         compiler_params=pltpu.CompilerParams(vmem_limit_bytes=8 * 1024 * 1024),
         cost_estimate=cost(10**6, 4 * 10**6),
-    )(flags, *(pltpu.with_memory_space_constraint(a, pltpu.HBM) for a in (states, mobility, reaction)))
+    )(*(pltpu.with_memory_space_constraint(a, pltpu.HBM) for a in (states, mobility, reaction)))
     left = ring(to_right, "space", 1)
     right = ring(to_left, "space", -1)
     v1, step, first = call(
@@ -432,8 +440,8 @@
          (9,) + small],
         [(10,) + plane, (10,) + plane, (12,) + plane, (10,) + plane, (10,) + plane, (8,) + plane, (10,) + plane,
          (2, 8) + plane, (5,) + plane],
-        flags, states, mobility, reaction, left, right, to_right, to_left, own, v1, step, first,
-        flops=2 * 10**7, limit=16, scalars=1,
+        states, mobility, reaction, left, right, to_right, to_left, own, v1, step, first,
+        flops=2 * 10**7, limit=16,
     )
     q_left = ring(to_right, "space", 1)
     q_right = ring(to_left, "space", -1)
@@ -441,13 +449,13 @@
     count = lax.axis_size("tm")
     b_before = lax.ppermute(b2, "tm", [(i, i + 1) for i in range(count - 1) if i not in (1, 3)])
     (mine,) = call(
-        pack_kernel, [(27,) + small], [], flags, q, start, coarse[0], share, own, outer, q_left, q_right, scalars=1
+        pack_kernel, [(27,) + small], [], q, start, coarse[0], share, own, outer, q_left, q_right
     )
     other = swapped(mine)
     levels_shape = [(11,) + small, (9,) + small, (7,) + small]
     last, ordered, mw, rw = call(
         first_kernel, [(5,) + small, (32,) + small, (11,) + small, (11,) + small], levels_shape[1:],
-        flags, mine, other, own, outer, scalars=1,
+        mine, other, own, outer,
     )
     turns = lax.axis_size("tm") // 2
     for turn in range(1, turns):
@@ -465,16 +473,16 @@
         high = ring(mid[1:5], "space", -1)
         if turn == 1:
             low, high, b_before = together(low, high, b_before)
-        operands = (flags, ordered, mw, rw, mid, low, high) + ((kept,) if turn > 1 else ())
+        operands = (ordered, mw, rw, mid, low, high) + ((kept,) if turn > 1 else ())
         if not final:
             last, kept = call(
-                functools.partial(turn_kernel, turn, False), [(5,) + small, (13,) + small], levels_shape, *operands, scalars=1
+                functools.partial(turn_kernel, turn, False), [(5,) + small, (13,) + small], levels_shape, *operands
             )
     scratch = [(5,) + small, (13,) + small, (5, 5) + small] + levels_shape + [(3, 8) + plane, (5,) + plane]
     return pl.pallas_call(
         functools.partial(closing_kernel, turns - 1),
         out_shape=jax.ShapeDtypeStruct((1, 3, 8) + plane, jnp.float32),
-        in_specs=[pl.BlockSpec(memory_space=pltpu.SMEM)] + [pl.BlockSpec(memory_space=pltpu.VMEM)] * 13,
+        in_specs=[pl.BlockSpec(memory_space=pltpu.VMEM)] * 13,
         out_specs=pl.BlockSpec(memory_space=pltpu.HBM),
         scratch_shapes=[pltpu.VMEM(s, jnp.float32) for s in scratch] + [pltpu.SemaphoreType.DMA((3,))],
         compiler_params=pltpu.CompilerParams(vmem_limit_bytes=12 * 1024 * 1024),

time: 110 us -> 106 us (0.964)
  Pallas kernels: 14.9 us -> 11 us
    pallas_call x7, Pallas kernels: 9.4 us -> 6.61 us  [call(): pl.pallas_call(kernel, out_shape=[jax.ShapeDtypeStruct(s, jnp.float32) fo...]
where the time goes in v8:
time: 106 us
  starting transfers between devices  57 us (54%)
  waiting for transfers between devices  37.7 us (36%)
  Pallas kernels  11 us (10%)
    ppermute x10, waiting for transfers between devices, ring(): lax.ppermute(values, axis, [(i, (i + distance) % count) for i in range(co...  30.2 us
    ppermute x10, starting transfers between devices, ring(): lax.ppermute(values, axis, [(i, (i + distance) % count) for i in range(co...  29.4 us
    ppermute x1, starting transfers between devices, body(): b_late = lax.ppermute(sent, 'tm', [(1, 2)])  16.9 us
    pallas_call x7, Pallas kernels, call(): pl.pallas_call(kernel, out_shape=[jax.ShapeDtypeStruct(s, jnp.float32) fo...  6.61 us
    ppermute x3, starting transfers between devices, hop(): lax.ppermute(values, 'tm', [(2 * turn - 2 + core, 2 * turn + core) for co...  6.25 us
    ppermute x3, waiting for transfers between devices, hop(): lax.ppermute(values, 'tm', [(2 * turn - 2 + core, 2 * turn + core) for co...  5.51 us
    ppermute x1, starting transfers between devices, swapped(): return lax.ppermute(values, 'tm', [(i, i ^ 1) for i in range(count)])  2.43 us
    pallas_call x1, Pallas kernels, body(): pl.pallas_call(edge_kernel, out_shape=[jax.ShapeDtypeStruct(s, jnp.float3...  2.24 us
  transfers between devices with their start and end apart: 17, of which 7 were waited for; matrix products, arithmetic and copies ran while one was open for 0% of the time, Pallas kernels for 3%

profile of v8, /device:TPU:33, one launch (start us, length us, event | category | flops | bytes accessed | tf_op | source)
XLA Modules:
  0.0 106.2 jit_solution(17497014745445726426)
XLA Ops:
  0.0 2.2 %shard_map.37 = (f32[2,4,64,128]{3,2,1,0:T(8,128)S(1)}, f32[10,128,128]{2,1,0:T(8,128)S(1)}, f32[10,128,128]{2,1,0:T(8,128)S(1)}) custom-call(f32[3,8,128,128]{3,2,1,0:T(8,128)} %bitcast.5, f32[8,128,128]{2,1,0:T(8,128)} %mob.3, f32[8,128,128]{2,1,0:T(8,128)} %rea.3), custom_call_target="tpu_custom_call" | custom-call | flops 1000000 | bytes 4000000 | tf_op jit(solution)/shard_map/pallas_call | solution.py:422
  2.3 1.4 %collective-permute-start = (f32[10,128,128]{2,1,0:T(8,128)S(1)}, f32[10,128,128]{2,1,0:T(8,128)S(1)}, u32[]{:S(2)}, u32[]{:S(2)}) collective-permute-start(f32[10,128,128]{2,1,0:T(8,128)S(1)} %get-tuple-element.39.to_right), channel_id=1, source_target_pairs={{0,1},{1,2},{2,3},{3,4},{4,5},{5,6},{6,7},{7,8},{8,9},{9,10},{10,1... | collective-permute-start | bytes 1966088 | tf_op jit(solution)/shard_map/ppermute | solution.py:38
  3.6 4.4 %collective-permute-start.1 = (f32[10,128,128]{2,1,0:T(8,128)S(1)}, f32[10,128,128]{2,1,0:T(8,128)S(1)}, u32[]{:S(2)}, u32[]{:S(2)}) collective-permute-start(f32[10,128,128]{2,1,0:T(8,128)S(1)} %get-tuple-element.40.to_left), channel_id=1, source_target_pairs={{0,31},{1,0},{2,1},{3,2},{4,3},{5,4},{6,5},{7,6},{8,7},{9,8},{10,9... | collective-permute-start | bytes 1966088 | tf_op jit(solution)/shard_map/ppermute | solution.py:38
  8.0 1.7 %shard_map.38 = (f32[8,128,128]{2,1,0:T(8,128)S(1)}, f32[8,128,128]{2,1,0:T(8,128)S(1)}, f32[8,128,128]{2,1,0:T(8,128)S(1)}) custom-call(f32[3,8,128,128]{3,2,1,0:T(8,128)S(1)} %bitcast.6, f32[8,128,128]{2,1,0:T(8,128)S(1)} %copy-done.1, f32[8,128,128]{2,1,0:T(8,128)S(1)} %copy-done.2), custom_call_target="tpu_custom_call" | custom-call | flops 10000000 | bytes 4194304 | tf_op jit(solution)/shard_map/pallas_call | solution.py:56
  9.8 12.4 %collective-permute-done.left = f32[10,128,128]{2,1,0:T(8,128)S(1)} collective-permute-done((f32[10,128,128]{2,1,0:T(8,128)S(1)}, f32[10,128,128]{2,1,0:T(8,128)S(1)}, u32[]{:S(2)}, u32[]{:S(2)}) %collective-permute-start) | collective-permute-done | bytes 655392 | tf_op jit(solution)/shard_map/ppermute | solution.py:38
  22.2 2.4 %shard_map.39 = (f32[8,128,128]{2,1,0:T(8,128)S(1)}, f32[8,128,128]{2,1,0:T(8,128)S(1)}, f32[8,64,128]{2,1,0:T(8,128)S(1)}, f32[5,64,128]{2,1,0:T(8,128)S(1)}, f...) custom-call(f32[3,8,128,128]{3,2,1,0:T(8,128)S(1)} %bitcast.7, ...), custom_call_target="tpu_custom_call" | custom-call | flops 20000000 | bytes 9732096 | tf_op jit(solution)/shard_map/pallas_call | solution.py:56
  24.6 5.7 %collective-permute-start.3 = (f32[9,64,128]{2,1,0:T(8,128)S(1)}, f32[9,64,128]{2,1,0:T(8,128)S(1)}, u32[]{:S(2)}, u32[]{:S(2)}) collective-permute-start(f32[9,64,128]{2,1,0:T(8,128)S(1)} %get-tuple-element.51), channel_id=1, source_target_pairs={{0,31},{1,0},{2,1},{3,2},{4,3},{5,4},{6,5},{7,6},{8,7},{9,8},{10,9... | collective-permute-start | bytes 884744 | tf_op jit(solution)/shard_map/ppermute | solution.py:38
  30.3 5.6 %collective-permute-done.2.from_left = f32[9,64,128]{2,1,0:T(8,128)S(1)} collective-permute-done((f32[9,64,128]{2,1,0:T(8,128)S(1)}, f32[9,64,128]{2,1,0:T(8,128)S(1)}, u32[]{:S(2)}, u32[]{:S(2)}) %collective-permute-start.2) | collective-permute-done | bytes 294944 | tf_op jit(solution)/shard_map/ppermute | solution.py:38
  36.0 2.4 %collective-permute-start.4 = (f32[27,64,128]{2,1,0:T(8,128)S(1)}, f32[27,64,128]{2,1,0:T(8,128)S(1)}, u32[]{:S(2)}, u32[]{:S(2)}) collective-permute-start(f32[27,64,128]{2,1,0:T(8,128)S(1)} %shard_map.40.mine), channel_id=1, source_target_pairs={{0,32},{32,0},{64,96},{96,64},{128,160},{160,128},{192,224},{224,1... | collective-permute-start | bytes 2654216 | tf_op jit(solution)/shard_map/ppermute | solution.py:51
  38.4 2.1 %collective-permute-done.4.other = f32[27,64,128]{2,1,0:T(8,128)S(1)} collective-permute-done((f32[27,64,128]{2,1,0:T(8,128)S(1)}, f32[27,64,128]{2,1,0:T(8,128)S(1)}, u32[]{:S(2)}, u32[]{:S(2)}) %collective-permute-start.4) | collective-permute-done | bytes 884768 | tf_op jit(solution)/shard_map/ppermute | solution.py:51
  41.1 4.9 %collective-permute-start.5 = (f32[5,64,128]{2,1,0:T(8,128)S(1)}, f32[5,64,128]{2,1,0:T(8,128)S(1)}, u32[]{:S(2)}, u32[]{:S(2)}) collective-permute-start(f32[5,64,128]{2,1,0:T(8,128)S(1)} %get-tuple-element.55), channel_id=1, source_target_pairs={{0,64},{32,96},{1,65},{33,97},{2,66},{34,98},{3,67},{35,99},{4,68}... | collective-permute-start | bytes 491528 | tf_op jit(solution)/shard_map/ppermute | solution.py:46
  46.2 1.3 %collective-permute-start.8 = (f32[8,128,128]{2,1,0:T(8,128)S(1)}, f32[8,128,128]{2,1,0:T(8,128)S(1)}, u32[]{:S(2)}, u32[]{:S(2)}) collective-permute-start(f32[8,128,128]{2,1,0:T(8,128)S(1)} %get-tuple-element.71.refs_2_), channel_id=1, source_target_pairs={{0,32},{64,96},{128,160},{160,192},{192,224},{1,33},{65,97},{129,1... | collective-permute-start | bytes 1572872 | tf_op jit(solution)/shard_map/ppermute | solution.py:450
  47.5 5.5 %collective-permute-done.5.mid = f32[5,64,128]{2,1,0:T(8,128)S(1)} collective-permute-done((f32[5,64,128]{2,1,0:T(8,128)S(1)}, f32[5,64,128]{2,1,0:T(8,128)S(1)}, u32[]{:S(2)}, u32[]{:S(2)}) %collective-permute-start.5) | collective-permute-done | bytes 163872 | tf_op jit(solution)/shard_map/ppermute | solution.py:46
  53.0 0.7 collective-permute-start.9
  53.8 5.7 %collective-permute-start.7 = (f32[4,64,128]{2,1,0:T(8,128)S(1)}, f32[4,64,128]{2,1,0:T(8,128)S(1)}, u32[]{:S(2)}, u32[]{:S(2)}) collective-permute-start(f32[4,64,128]{2,1,0:T(8,128)S(1)} %get-tuple-element.77), channel_id=1, source_target_pairs={{0,31},{1,0},{2,1},{3,2},{4,3},{5,4},{6,5},{7,6},{8,7},{9,8},{10,9... | collective-permute-start | bytes 393224 | tf_op jit(solution)/shard_map/ppermute | solution.py:38
  59.5 2.3 %collective-permute-done.6.low = f32[4,64,128]{2,1,0:T(8,128)S(1)} collective-permute-done((f32[4,64,128]{2,1,0:T(8,128)S(1)}, f32[4,64,128]{2,1,0:T(8,128)S(1)}, u32[]{:S(2)}, u32[]{:S(2)}) %collective-permute-start.6) | collective-permute-done | bytes 131104 | tf_op jit(solution)/shard_map/ppermute | solution.py:38
  61.8 0.8 shard_map.43
  63.5 5.8 %collective-permute-start.12 = (f32[4,64,128]{2,1,0:T(8,128)S(1)}, f32[4,64,128]{2,1,0:T(8,128)S(1)}, u32[]{:S(2)}, u32[]{:S(2)}) collective-permute-start(f32[4,64,128]{2,1,0:T(8,128)S(1)} %get-tuple-element.75), channel_id=1, source_target_pairs={{0,31},{1,0},{2,1},{3,2},{4,3},{5,4},{6,5},{7,6},{8,7},{9,8},{10,9... | collective-permute-start | bytes 393224 | tf_op jit(solution)/shard_map/ppermute | solution.py:38
  69.2 2.3 %collective-permute-done.11.low = f32[4,64,128]{2,1,0:T(8,128)S(1)} collective-permute-done((f32[4,64,128]{2,1,0:T(8,128)S(1)}, f32[4,64,128]{2,1,0:T(8,128)S(1)}, u32[]{:S(2)}, u32[]{:S(2)}) %collective-permute-start.11) | collective-permute-done | bytes 131104 | tf_op jit(solution)/shard_map/ppermute | solution.py:38
  71.5 0.8 shard_map.44
  73.0 16.9 %collective-permute-start.16 = (f32[8,128,128]{2,1,0:T(8,128)S(1)}, f32[8,128,128]{2,1,0:T(8,128)S(1)}, u32[]{:S(2)}, u32[]{:S(2)}) collective-permute-start(f32[8,128,128]{2,1,0:T(8,128)S(1)} %get-tuple-element.71.refs_2_), channel_id=1, source_target_pairs={{32,64},{33,65},{34,66},{35,67},{36,68},{37,69},{38,70},{39,71},{4... | collective-permute-start | bytes 1572872 | tf_op jit(solution)/shard_map/ppermute | solution.py:467
  90.3 6.0 %collective-permute-start.15 = (f32[4,64,128]{2,1,0:T(8,128)S(1)}, f32[4,64,128]{2,1,0:T(8,128)S(1)}, u32[]{:S(2)}, u32[]{:S(2)}) collective-permute-start(f32[4,64,128]{2,1,0:T(8,128)S(1)} %get-tuple-element.73), channel_id=1, source_target_pairs={{0,31},{1,0},{2,1},{3,2},{4,3},{5,4},{6,5},{7,6},{8,7},{9,8},{10,9... | collective-permute-start | bytes 393224 | tf_op jit(solution)/shard_map/ppermute | solution.py:38
  96.3 7.5 %collective-permute-done.14.low = f32[4,64,128]{2,1,0:T(8,128)S(1)} collective-permute-done((f32[4,64,128]{2,1,0:T(8,128)S(1)}, f32[4,64,128]{2,1,0:T(8,128)S(1)}, u32[]{:S(2)}, u32[]{:S(2)}) %collective-permute-start.14) | collective-permute-done | bytes 131104 | tf_op jit(solution)/shard_map/ppermute | solution.py:38
  103.9 2.1 %shard_map.45 = f32[1,3,8,128,128]{4,3,2,1,0:T(8,128)} custom-call(f32[32,64,128]{2,1,0:T(8,128)S(1)} %get-tuple-element.52.ordered, f32[11,64,128]{2,1,0:T(8,128)S(1)} %get-tuple-element.53.mw, f32[11,64,128]{2,1,0:T(8,128)S(1)} %get-tuple-element.54.rw, f32[5,64,128]{2,1,0:T(8,128)S(1)} %collective-permute-done.13.mid, ...), custom_call_target="tpu_custom_call" | custom-call | flops 10000000 | bytes 8000000 | tf_op jit(solution)/shard_map/pallas_call | solution.py:482
  (30 shorter events, 2.9 us)
Async XLA Ops:
  0.0 8.0 %copy-start = (f32[1,3,8,128,128]{4,3,2,1,0:T(8,128)S(1)}, f32[1,3,8,128,128]{4,3,2,1,0:T(8,128)}, u32[]{:S(2)}) copy-start(f32[1,3,8,128,128]{4,3,2,1,0:T(8,128)} %param.3) | copy-start | bytes 4718596
  0.0 8.0 %copy-start.1 = (f32[8,128,128]{2,1,0:T(8,128)S(1)}, f32[8,128,128]{2,1,0:T(8,128)}, u32[]{:S(2)}) copy-start(f32[8,128,128]{2,1,0:T(8,128)} %mob.3) | copy-start | bytes 1572868
  0.0 8.0 %copy-start.2 = (f32[8,128,128]{2,1,0:T(8,128)S(1)}, f32[8,128,128]{2,1,0:T(8,128)}, u32[]{:S(2)}) copy-start(f32[8,128,128]{2,1,0:T(8,128)} %rea.3) | copy-start | bytes 1572868
  2.3 19.9 %collective-permute-start = (f32[10,128,128]{2,1,0:T(8,128)S(1)}, f32[10,128,128]{2,1,0:T(8,128)S(1)}, u32[]{:S(2)}, u32[]{:S(2)}) collective-permute-start(f32[10,128,128]{2,1,0:T(8,128)S(1)} %get-tuple-element.39.to_right), channel_id=1, source_target_pairs={{0,1},{1,2},{2,3},{3,4},{4,5},{5,6},{6,7},{7,8},{8,9},{9,10},{10,1... | collective-permute-start | bytes 1966088 | tf_op jit(solution)/shard_map/ppermute | solution.py:38
  3.6 18.5 %collective-permute-start.1 = (f32[10,128,128]{2,1,0:T(8,128)S(1)}, f32[10,128,128]{2,1,0:T(8,128)S(1)}, u32[]{:S(2)}, u32[]{:S(2)}) collective-permute-start(f32[10,128,128]{2,1,0:T(8,128)S(1)} %get-tuple-element.40.to_left), channel_id=1, source_target_pairs={{0,31},{1,0},{2,1},{3,2},{4,3},{5,4},{6,5},{7,6},{8,7},{9,8},{10,9... | collective-permute-start | bytes 1966088 | tf_op jit(solution)/shard_map/ppermute | solution.py:38
  24.5 11.4 %collective-permute-start.2 = (f32[9,64,128]{2,1,0:T(8,128)S(1)}, f32[9,64,128]{2,1,0:T(8,128)S(1)}, u32[]{:S(2)}, u32[]{:S(2)}) collective-permute-start(f32[9,64,128]{2,1,0:T(8,128)S(1)} %get-tuple-element.50), channel_id=1, source_target_pairs={{0,1},{1,2},{2,3},{3,4},{4,5},{5,6},{6,7},{7,8},{8,9},{9,10},{10,1... | collective-permute-start | bytes 884744 | tf_op jit(solution)/shard_map/ppermute | solution.py:38
  24.6 11.3 %collective-permute-start.3 = (f32[9,64,128]{2,1,0:T(8,128)S(1)}, f32[9,64,128]{2,1,0:T(8,128)S(1)}, u32[]{:S(2)}, u32[]{:S(2)}) collective-permute-start(f32[9,64,128]{2,1,0:T(8,128)S(1)} %get-tuple-element.51), channel_id=1, source_target_pairs={{0,31},{1,0},{2,1},{3,2},{4,3},{5,4},{6,5},{7,6},{8,7},{9,8},{10,9... | collective-permute-start | bytes 884744 | tf_op jit(solution)/shard_map/ppermute | solution.py:38
  36.0 4.5 %collective-permute-start.4 = (f32[27,64,128]{2,1,0:T(8,128)S(1)}, f32[27,64,128]{2,1,0:T(8,128)S(1)}, u32[]{:S(2)}, u32[]{:S(2)}) collective-permute-start(f32[27,64,128]{2,1,0:T(8,128)S(1)} %shard_map.40.mine), channel_id=1, source_target_pairs={{0,32},{32,0},{64,96},{96,64},{128,160},{160,128},{192,224},{224,1... | collective-permute-start | bytes 2654216 | tf_op jit(solution)/shard_map/ppermute | solution.py:51
  41.1 11.9 %collective-permute-start.5 = (f32[5,64,128]{2,1,0:T(8,128)S(1)}, f32[5,64,128]{2,1,0:T(8,128)S(1)}, u32[]{:S(2)}, u32[]{:S(2)}) collective-permute-start(f32[5,64,128]{2,1,0:T(8,128)S(1)} %get-tuple-element.55), channel_id=1, source_target_pairs={{0,64},{32,96},{1,65},{33,97},{2,66},{34,98},{3,67},{35,99},{4,68}... | collective-permute-start | bytes 491528 | tf_op jit(solution)/shard_map/ppermute | solution.py:46
  46.2 13.3 %collective-permute-start.8 = (f32[8,128,128]{2,1,0:T(8,128)S(1)}, f32[8,128,128]{2,1,0:T(8,128)S(1)}, u32[]{:S(2)}, u32[]{:S(2)}) collective-permute-start(f32[8,128,128]{2,1,0:T(8,128)S(1)} %get-tuple-element.71.refs_2_), channel_id=1, source_target_pairs={{0,32},{64,96},{128,160},{160,192},{192,224},{1,33},{65,97},{129,1... | collective-permute-start | bytes 1572872 | tf_op jit(solution)/shard_map/ppermute | solution.py:450
  53.0 9.7 %collective-permute-start.9 = (f32[8,128,128]{2,1,0:T(8,128)S(1)}, f32[8,128,128]{2,1,0:T(8,128)S(1)}, u32[]{:S(2)}, u32[]{:S(2)}) collective-permute-start(f32[8,128,128]{2,1,0:T(8,128)S(1)} %get-tuple-element.71.refs_2_), channel_id=1, source_target_pairs={{96,128},{97,129},{98,130},{99,131},{100,132},{101,133},{102,134},... | collective-permute-start | bytes 1572872 | tf_op jit(solution)/shard_map/ppermute | solution.py:471
  53.7 8.1 %collective-permute-start.6 = (f32[4,64,128]{2,1,0:T(8,128)S(1)}, f32[4,64,128]{2,1,0:T(8,128)S(1)}, u32[]{:S(2)}, u32[]{:S(2)}) collective-permute-start(f32[4,64,128]{2,1,0:T(8,128)S(1)} %get-tuple-element.78), channel_id=1, source_target_pairs={{0,1},{1,2},{2,3},{3,4},{4,5},{5,6},{6,7},{7,8},{8,9},{9,10},{10,1... | collective-permute-start | bytes 393224 | tf_op jit(solution)/shard_map/ppermute | solution.py:38
  53.8 8.0 %collective-permute-start.7 = (f32[4,64,128]{2,1,0:T(8,128)S(1)}, f32[4,64,128]{2,1,0:T(8,128)S(1)}, u32[]{:S(2)}, u32[]{:S(2)}) collective-permute-start(f32[4,64,128]{2,1,0:T(8,128)S(1)} %get-tuple-element.77), channel_id=1, source_target_pairs={{0,31},{1,0},{2,1},{3,2},{4,3},{5,4},{6,5},{7,6},{8,7},{9,8},{10,9... | collective-permute-start | bytes 393224 | tf_op jit(solution)/shard_map/ppermute | solution.py:38
  62.7 0.7 collective-permute-start.10
  63.4 8.1 %collective-permute-start.11 = (f32[4,64,128]{2,1,0:T(8,128)S(1)}, f32[4,64,128]{2,1,0:T(8,128)S(1)}, u32[]{:S(2)}, u32[]{:S(2)}) collective-permute-start(f32[4,64,128]{2,1,0:T(8,128)S(1)} %get-tuple-element.76), channel_id=1, source_target_pairs={{0,1},{1,2},{2,3},{3,4},{4,5},{5,6},{6,7},{7,8},{8,9},{9,10},{10,1... | collective-permute-start | bytes 393224 | tf_op jit(solution)/shard_map/ppermute | solution.py:38
  63.5 8.0 %collective-permute-start.12 = (f32[4,64,128]{2,1,0:T(8,128)S(1)}, f32[4,64,128]{2,1,0:T(8,128)S(1)}, u32[]{:S(2)}, u32[]{:S(2)}) collective-permute-start(f32[4,64,128]{2,1,0:T(8,128)S(1)} %get-tuple-element.75), channel_id=1, source_target_pairs={{0,31},{1,0},{2,1},{3,2},{4,3},{5,4},{6,5},{7,6},{8,7},{9,8},{10,9... | collective-permute-start | bytes 393224 | tf_op jit(solution)/shard_map/ppermute | solution.py:38
  72.3 17.6 %collective-permute-start.13 = (f32[5,64,128]{2,1,0:T(8,128)S(1)}, f32[5,64,128]{2,1,0:T(8,128)S(1)}, u32[]{:S(2)}, u32[]{:S(2)}) collective-permute-start(f32[5,64,128]{2,1,0:T(8,128)S(1)} %get-tuple-element.67), channel_id=1, source_target_pairs={{128,192},{160,224},{129,193},{161,225},{130,194},{162,226},{131,1... | collective-permute-start | bytes 491528 | tf_op jit(solution)/shard_map/ppermute | solution.py:46
  73.0 30.9 %collective-permute-start.16 = (f32[8,128,128]{2,1,0:T(8,128)S(1)}, f32[8,128,128]{2,1,0:T(8,128)S(1)}, u32[]{:S(2)}, u32[]{:S(2)}) collective-permute-start(f32[8,128,128]{2,1,0:T(8,128)S(1)} %get-tuple-element.71.refs_2_), channel_id=1, source_target_pairs={{32,64},{33,65},{34,66},{35,67},{36,68},{37,69},{38,70},{39,71},{4... | collective-permute-start | bytes 1572872 | tf_op jit(solution)/shard_map/ppermute | solution.py:467
  90.0 13.9 %collective-permute-start.14 = (f32[4,64,128]{2,1,0:T(8,128)S(1)}, f32[4,64,128]{2,1,0:T(8,128)S(1)}, u32[]{:S(2)}, u32[]{:S(2)}) collective-permute-start(f32[4,64,128]{2,1,0:T(8,128)S(1)} %get-tuple-element.74), channel_id=1, source_target_pairs={{0,1},{1,2},{2,3},{3,4},{4,5},{5,6},{6,7},{7,8},{8,9},{9,10},{10,1... | collective-permute-start | bytes 393224 | tf_op jit(solution)/shard_map/ppermute | solution.py:38
  90.3 13.6 %collective-permute-start.15 = (f32[4,64,128]{2,1,0:T(8,128)S(1)}, f32[4,64,128]{2,1,0:T(8,128)S(1)}, u32[]{:S(2)}, u32[]{:S(2)}) collective-permute-start(f32[4,64,128]{2,1,0:T(8,128)S(1)} %get-tuple-element.73), channel_id=1, source_target_pairs={{0,31},{1,0},{2,1},{3,2},{4,3},{5,4},{6,5},{7,6},{8,7},{9,8},{10,9... | collective-permute-start | bytes 393224 | tf_op jit(solution)/shard_map/ppermute | solution.py:38

commit v9 on v8

--- a/solution.py
+++ b/solution.py
@@ -179,7 +179,7 @@
     flags = where()
     half = mob.shape[1] // 2
 
-    @pl.loop(0, 8)
+    @pl.loop(0, 8, unroll=4)
     def _(i):
         mw[i + 1] = mob[i]
         rw[i + 1] = rea[i]
@@ -197,14 +197,14 @@
         step[plane + 1] = step_own[plane] + mob[plane] * got[5]
         first[plane] = first_own[plane] + mob[plane] * got[3]
 
-    @pl.loop(0, 10, unroll=2)
+    @pl.loop(0, 10, unroll=5)
     def _(i):
         a = v1[i + 1]
         force = mw[i] * laplace(a, v1[i], v1[i + 2]) + rw[i] * cubic(a)
         f1[i] = force
         v2[i] = a + (substep * force + step[i])
 
-    @pl.loop(0, 8, unroll=2)
+    @pl.loop(0, 8, unroll=4)
     def _(i):
         a = v2[i + 1]
         force = mob[i] * laplace(a, v2[i], v2[i + 2]) + rea[i] * cubic(a)

time: 106 us -> 106 us (level)
  no operation moved by 1% of the time
where the time goes in v9:
time: 106 us
  starting transfers between devices  56.8 us (54%)
  waiting for transfers between devices  37.9 us (36%)
  Pallas kernels  10.8 us (10%)
    ppermute x10, waiting for transfers between devices, ring(): lax.ppermute(values, axis, [(i, (i + distance) % count) for i in range(co...  30.3 us
    ppermute x10, starting transfers between devices, ring(): lax.ppermute(values, axis, [(i, (i + distance) % count) for i in range(co...  29.2 us
    ppermute x1, starting transfers between devices, body(): b_late = lax.ppermute(sent, 'tm', [(1, 2)])  16.9 us
    pallas_call x7, Pallas kernels, call(): pl.pallas_call(kernel, out_shape=[jax.ShapeDtypeStruct(s, jnp.float32) fo...  6.42 us
    ppermute x3, starting transfers between devices, hop(): lax.ppermute(values, 'tm', [(2 * turn - 2 + core, 2 * turn + core) for co...  6.25 us
    ppermute x3, waiting for transfers between devices, hop(): lax.ppermute(values, 'tm', [(2 * turn - 2 + core, 2 * turn + core) for co...  5.51 us
    ppermute x1, starting transfers between devices, swapped(): return lax.ppermute(values, 'tm', [(i, i ^ 1) for i in range(count)])  2.43 us
    pallas_call x1, Pallas kernels, body(): pl.pallas_call(edge_kernel, out_shape=[jax.ShapeDtypeStruct(s, jnp.float3...  2.24 us
  transfers between devices with their start and end apart: 17, of which 7 were waited for; matrix products, arithmetic and copies ran while one was open for 0% of the time, Pallas kernels for 3%

profile of v9, /device:TPU:33, one launch (start us, length us, event | category | flops | bytes accessed | tf_op | source)
XLA Modules:
  0.0 106.0 jit_solution(10210883263848677718)
XLA Ops:
  0.0 2.2 %shard_map.37 = (f32[2,4,64,128]{3,2,1,0:T(8,128)S(1)}, f32[10,128,128]{2,1,0:T(8,128)S(1)}, f32[10,128,128]{2,1,0:T(8,128)S(1)}) custom-call(f32[3,8,128,128]{3,2,1,0:T(8,128)} %bitcast.5, f32[8,128,128]{2,1,0:T(8,128)} %mob.3, f32[8,128,128]{2,1,0:T(8,128)} %rea.3), custom_call_target="tpu_custom_call" | custom-call | flops 1000000 | bytes 4000000 | tf_op jit(solution)/shard_map/pallas_call | solution.py:422
  2.3 1.4 %collective-permute-start = (f32[10,128,128]{2,1,0:T(8,128)S(1)}, f32[10,128,128]{2,1,0:T(8,128)S(1)}, u32[]{:S(2)}, u32[]{:S(2)}) collective-permute-start(f32[10,128,128]{2,1,0:T(8,128)S(1)} %get-tuple-element.39.to_right), channel_id=1, source_target_pairs={{0,1},{1,2},{2,3},{3,4},{4,5},{5,6},{6,7},{7,8},{8,9},{9,10},{10,1... | collective-permute-start | bytes 1966088 | tf_op jit(solution)/shard_map/ppermute | solution.py:38
  3.6 4.4 %collective-permute-start.1 = (f32[10,128,128]{2,1,0:T(8,128)S(1)}, f32[10,128,128]{2,1,0:T(8,128)S(1)}, u32[]{:S(2)}, u32[]{:S(2)}) collective-permute-start(f32[10,128,128]{2,1,0:T(8,128)S(1)} %get-tuple-element.40.to_left), channel_id=1, source_target_pairs={{0,31},{1,0},{2,1},{3,2},{4,3},{5,4},{6,5},{7,6},{8,7},{9,8},{10,9... | collective-permute-start | bytes 1966088 | tf_op jit(solution)/shard_map/ppermute | solution.py:38
  8.0 1.7 %shard_map.38 = (f32[8,128,128]{2,1,0:T(8,128)S(1)}, f32[8,128,128]{2,1,0:T(8,128)S(1)}, f32[8,128,128]{2,1,0:T(8,128)S(1)}) custom-call(f32[3,8,128,128]{3,2,1,0:T(8,128)S(1)} %bitcast.6, f32[8,128,128]{2,1,0:T(8,128)S(1)} %copy-done.1, f32[8,128,128]{2,1,0:T(8,128)S(1)} %copy-done.2), custom_call_target="tpu_custom_call" | custom-call | flops 10000000 | bytes 4194304 | tf_op jit(solution)/shard_map/pallas_call | solution.py:56
  9.8 12.4 %collective-permute-done.left = f32[10,128,128]{2,1,0:T(8,128)S(1)} collective-permute-done((f32[10,128,128]{2,1,0:T(8,128)S(1)}, f32[10,128,128]{2,1,0:T(8,128)S(1)}, u32[]{:S(2)}, u32[]{:S(2)}) %collective-permute-start) | collective-permute-done | bytes 655392 | tf_op jit(solution)/shard_map/ppermute | solution.py:38
  22.2 2.0 %shard_map.39 = (f32[8,128,128]{2,1,0:T(8,128)S(1)}, f32[8,128,128]{2,1,0:T(8,128)S(1)}, f32[8,64,128]{2,1,0:T(8,128)S(1)}, f32[5,64,128]{2,1,0:T(8,128)S(1)}, f...) custom-call(f32[3,8,128,128]{3,2,1,0:T(8,128)S(1)} %bitcast.7, ...), custom_call_target="tpu_custom_call" | custom-call | flops 20000000 | bytes 9732096 | tf_op jit(solution)/shard_map/pallas_call | solution.py:56
  24.2 5.7 %collective-permute-start.3 = (f32[9,64,128]{2,1,0:T(8,128)S(1)}, f32[9,64,128]{2,1,0:T(8,128)S(1)}, u32[]{:S(2)}, u32[]{:S(2)}) collective-permute-start(f32[9,64,128]{2,1,0:T(8,128)S(1)} %get-tuple-element.51), channel_id=1, source_target_pairs={{0,31},{1,0},{2,1},{3,2},{4,3},{5,4},{6,5},{7,6},{8,7},{9,8},{10,9... | collective-permute-start | bytes 884744 | tf_op jit(solution)/shard_map/ppermute | solution.py:38
  29.9 5.6 %collective-permute-done.2.from_left = f32[9,64,128]{2,1,0:T(8,128)S(1)} collective-permute-done((f32[9,64,128]{2,1,0:T(8,128)S(1)}, f32[9,64,128]{2,1,0:T(8,128)S(1)}, u32[]{:S(2)}, u32[]{:S(2)}) %collective-permute-start.2) | collective-permute-done | bytes 294944 | tf_op jit(solution)/shard_map/ppermute | solution.py:38
  35.6 2.4 %collective-permute-start.4 = (f32[27,64,128]{2,1,0:T(8,128)S(1)}, f32[27,64,128]{2,1,0:T(8,128)S(1)}, u32[]{:S(2)}, u32[]{:S(2)}) collective-permute-start(f32[27,64,128]{2,1,0:T(8,128)S(1)} %shard_map.40.mine), channel_id=1, source_target_pairs={{0,32},{32,0},{64,96},{96,64},{128,160},{160,128},{192,224},{224,1... | collective-permute-start | bytes 2654216 | tf_op jit(solution)/shard_map/ppermute | solution.py:51
  38.0 2.1 %collective-permute-done.4.other = f32[27,64,128]{2,1,0:T(8,128)S(1)} collective-permute-done((f32[27,64,128]{2,1,0:T(8,128)S(1)}, f32[27,64,128]{2,1,0:T(8,128)S(1)}, u32[]{:S(2)}, u32[]{:S(2)}) %collective-permute-start.4) | collective-permute-done | bytes 884768 | tf_op jit(solution)/shard_map/ppermute | solution.py:51
  40.8 4.9 %collective-permute-start.5 = (f32[5,64,128]{2,1,0:T(8,128)S(1)}, f32[5,64,128]{2,1,0:T(8,128)S(1)}, u32[]{:S(2)}, u32[]{:S(2)}) collective-permute-start(f32[5,64,128]{2,1,0:T(8,128)S(1)} %get-tuple-element.55), channel_id=1, source_target_pairs={{0,64},{32,96},{1,65},{33,97},{2,66},{34,98},{3,67},{35,99},{4,68}... | collective-permute-start | bytes 491528 | tf_op jit(solution)/shard_map/ppermute | solution.py:46
  45.8 1.3 %collective-permute-start.8 = (f32[8,128,128]{2,1,0:T(8,128)S(1)}, f32[8,128,128]{2,1,0:T(8,128)S(1)}, u32[]{:S(2)}, u32[]{:S(2)}) collective-permute-start(f32[8,128,128]{2,1,0:T(8,128)S(1)} %get-tuple-element.71.refs_2_), channel_id=1, source_target_pairs={{0,32},{64,96},{128,160},{160,192},{192,224},{1,33},{65,97},{129,1... | collective-permute-start | bytes 1572872 | tf_op jit(solution)/shard_map/ppermute | solution.py:450
  47.1 5.5 %collective-permute-done.5.mid = f32[5,64,128]{2,1,0:T(8,128)S(1)} collective-permute-done((f32[5,64,128]{2,1,0:T(8,128)S(1)}, f32[5,64,128]{2,1,0:T(8,128)S(1)}, u32[]{:S(2)}, u32[]{:S(2)}) %collective-permute-start.5) | collective-permute-done | bytes 163872 | tf_op jit(solution)/shard_map/ppermute | solution.py:46
  52.6 0.7 collective-permute-start.9
  53.4 5.7 %collective-permute-start.7 = (f32[4,64,128]{2,1,0:T(8,128)S(1)}, f32[4,64,128]{2,1,0:T(8,128)S(1)}, u32[]{:S(2)}, u32[]{:S(2)}) collective-permute-start(f32[4,64,128]{2,1,0:T(8,128)S(1)} %get-tuple-element.77), channel_id=1, source_target_pairs={{0,31},{1,0},{2,1},{3,2},{4,3},{5,4},{6,5},{7,6},{8,7},{9,8},{10,9... | collective-permute-start | bytes 393224 | tf_op jit(solution)/shard_map/ppermute | solution.py:38
  59.1 2.3 %collective-permute-done.6.low = f32[4,64,128]{2,1,0:T(8,128)S(1)} collective-permute-done((f32[4,64,128]{2,1,0:T(8,128)S(1)}, f32[4,64,128]{2,1,0:T(8,128)S(1)}, u32[]{:S(2)}, u32[]{:S(2)}) %collective-permute-start.6) | collective-permute-done | bytes 131104 | tf_op jit(solution)/shard_map/ppermute | solution.py:38
  61.5 0.8 shard_map.43
  63.1 5.8 %collective-permute-start.12 = (f32[4,64,128]{2,1,0:T(8,128)S(1)}, f32[4,64,128]{2,1,0:T(8,128)S(1)}, u32[]{:S(2)}, u32[]{:S(2)}) collective-permute-start(f32[4,64,128]{2,1,0:T(8,128)S(1)} %get-tuple-element.75), channel_id=1, source_target_pairs={{0,31},{1,0},{2,1},{3,2},{4,3},{5,4},{6,5},{7,6},{8,7},{9,8},{10,9... | collective-permute-start | bytes 393224 | tf_op jit(solution)/shard_map/ppermute | solution.py:38
  68.9 2.3 %collective-permute-done.11.low = f32[4,64,128]{2,1,0:T(8,128)S(1)} collective-permute-done((f32[4,64,128]{2,1,0:T(8,128)S(1)}, f32[4,64,128]{2,1,0:T(8,128)S(1)}, u32[]{:S(2)}, u32[]{:S(2)}) %collective-permute-start.11) | collective-permute-done | bytes 131104 | tf_op jit(solution)/shard_map/ppermute | solution.py:38
  71.1 1.0 shard_map.44
  72.8 16.9 %collective-permute-start.16 = (f32[8,128,128]{2,1,0:T(8,128)S(1)}, f32[8,128,128]{2,1,0:T(8,128)S(1)}, u32[]{:S(2)}, u32[]{:S(2)}) collective-permute-start(f32[8,128,128]{2,1,0:T(8,128)S(1)} %get-tuple-element.71.refs_2_), channel_id=1, source_target_pairs={{32,64},{33,65},{34,66},{35,67},{36,68},{37,69},{38,70},{39,71},{4... | collective-permute-start | bytes 1572872 | tf_op jit(solution)/shard_map/ppermute | solution.py:467
  89.9 6.0 %collective-permute-start.15 = (f32[4,64,128]{2,1,0:T(8,128)S(1)}, f32[4,64,128]{2,1,0:T(8,128)S(1)}, u32[]{:S(2)}, u32[]{:S(2)}) collective-permute-start(f32[4,64,128]{2,1,0:T(8,128)S(1)} %get-tuple-element.73), channel_id=1, source_target_pairs={{0,31},{1,0},{2,1},{3,2},{4,3},{5,4},{6,5},{7,6},{8,7},{9,8},{10,9... | collective-permute-start | bytes 393224 | tf_op jit(solution)/shard_map/ppermute | solution.py:38
  96.0 7.7 %collective-permute-done.14.low = f32[4,64,128]{2,1,0:T(8,128)S(1)} collective-permute-done((f32[4,64,128]{2,1,0:T(8,128)S(1)}, f32[4,64,128]{2,1,0:T(8,128)S(1)}, u32[]{:S(2)}, u32[]{:S(2)}) %collective-permute-start.14) | collective-permute-done | bytes 131104 | tf_op jit(solution)/shard_map/ppermute | solution.py:38
  103.7 2.1 %shard_map.45 = f32[1,3,8,128,128]{4,3,2,1,0:T(8,128)} custom-call(f32[32,64,128]{2,1,0:T(8,128)S(1)} %get-tuple-element.52.ordered, f32[11,64,128]{2,1,0:T(8,128)S(1)} %get-tuple-element.53.mw, f32[11,64,128]{2,1,0:T(8,128)S(1)} %get-tuple-element.54.rw, f32[5,64,128]{2,1,0:T(8,128)S(1)} %collective-permute-done.13.mid, ...), custom_call_target="tpu_custom_call" | custom-call | flops 10000000 | bytes 8000000 | tf_op jit(solution)/shard_map/pallas_call | solution.py:482
  (30 shorter events, 2.7 us)
Async XLA Ops:
  0.0 8.0 %copy-start = (f32[1,3,8,128,128]{4,3,2,1,0:T(8,128)S(1)}, f32[1,3,8,128,128]{4,3,2,1,0:T(8,128)}, u32[]{:S(2)}) copy-start(f32[1,3,8,128,128]{4,3,2,1,0:T(8,128)} %param.3) | copy-start | bytes 4718596
  0.0 8.0 %copy-start.1 = (f32[8,128,128]{2,1,0:T(8,128)S(1)}, f32[8,128,128]{2,1,0:T(8,128)}, u32[]{:S(2)}) copy-start(f32[8,128,128]{2,1,0:T(8,128)} %mob.3) | copy-start | bytes 1572868
  0.0 8.0 %copy-start.2 = (f32[8,128,128]{2,1,0:T(8,128)S(1)}, f32[8,128,128]{2,1,0:T(8,128)}, u32[]{:S(2)}) copy-start(f32[8,128,128]{2,1,0:T(8,128)} %rea.3) | copy-start | bytes 1572868
  2.3 19.9 %collective-permute-start = (f32[10,128,128]{2,1,0:T(8,128)S(1)}, f32[10,128,128]{2,1,0:T(8,128)S(1)}, u32[]{:S(2)}, u32[]{:S(2)}) collective-permute-start(f32[10,128,128]{2,1,0:T(8,128)S(1)} %get-tuple-element.39.to_right), channel_id=1, source_target_pairs={{0,1},{1,2},{2,3},{3,4},{4,5},{5,6},{6,7},{7,8},{8,9},{9,10},{10,1... | collective-permute-start | bytes 1966088 | tf_op jit(solution)/shard_map/ppermute | solution.py:38
  3.6 18.5 %collective-permute-start.1 = (f32[10,128,128]{2,1,0:T(8,128)S(1)}, f32[10,128,128]{2,1,0:T(8,128)S(1)}, u32[]{:S(2)}, u32[]{:S(2)}) collective-permute-start(f32[10,128,128]{2,1,0:T(8,128)S(1)} %get-tuple-element.40.to_left), channel_id=1, source_target_pairs={{0,31},{1,0},{2,1},{3,2},{4,3},{5,4},{6,5},{7,6},{8,7},{9,8},{10,9... | collective-permute-start | bytes 1966088 | tf_op jit(solution)/shard_map/ppermute | solution.py:38
  24.1 11.4 %collective-permute-start.2 = (f32[9,64,128]{2,1,0:T(8,128)S(1)}, f32[9,64,128]{2,1,0:T(8,128)S(1)}, u32[]{:S(2)}, u32[]{:S(2)}) collective-permute-start(f32[9,64,128]{2,1,0:T(8,128)S(1)} %get-tuple-element.50), channel_id=1, source_target_pairs={{0,1},{1,2},{2,3},{3,4},{4,5},{5,6},{6,7},{7,8},{8,9},{9,10},{10,1... | collective-permute-start | bytes 884744 | tf_op jit(solution)/shard_map/ppermute | solution.py:38
  24.2 11.3 %collective-permute-start.3 = (f32[9,64,128]{2,1,0:T(8,128)S(1)}, f32[9,64,128]{2,1,0:T(8,128)S(1)}, u32[]{:S(2)}, u32[]{:S(2)}) collective-permute-start(f32[9,64,128]{2,1,0:T(8,128)S(1)} %get-tuple-element.51), channel_id=1, source_target_pairs={{0,31},{1,0},{2,1},{3,2},{4,3},{5,4},{6,5},{7,6},{8,7},{9,8},{10,9... | collective-permute-start | bytes 884744 | tf_op jit(solution)/shard_map/ppermute | solution.py:38
  35.6 4.5 %collective-permute-start.4 = (f32[27,64,128]{2,1,0:T(8,128)S(1)}, f32[27,64,128]{2,1,0:T(8,128)S(1)}, u32[]{:S(2)}, u32[]{:S(2)}) collective-permute-start(f32[27,64,128]{2,1,0:T(8,128)S(1)} %shard_map.40.mine), channel_id=1, source_target_pairs={{0,32},{32,0},{64,96},{96,64},{128,160},{160,128},{192,224},{224,1... | collective-permute-start | bytes 2654216 | tf_op jit(solution)/shard_map/ppermute | solution.py:51
  40.8 11.9 %collective-permute-start.5 = (f32[5,64,128]{2,1,0:T(8,128)S(1)}, f32[5,64,128]{2,1,0:T(8,128)S(1)}, u32[]{:S(2)}, u32[]{:S(2)}) collective-permute-start(f32[5,64,128]{2,1,0:T(8,128)S(1)} %get-tuple-element.55), channel_id=1, source_target_pairs={{0,64},{32,96},{1,65},{33,97},{2,66},{34,98},{3,67},{35,99},{4,68}... | collective-permute-start | bytes 491528 | tf_op jit(solution)/shard_map/ppermute | solution.py:46
  45.8 13.3 %collective-permute-start.8 = (f32[8,128,128]{2,1,0:T(8,128)S(1)}, f32[8,128,128]{2,1,0:T(8,128)S(1)}, u32[]{:S(2)}, u32[]{:S(2)}) collective-permute-start(f32[8,128,128]{2,1,0:T(8,128)S(1)} %get-tuple-element.71.refs_2_), channel_id=1, source_target_pairs={{0,32},{64,96},{128,160},{160,192},{192,224},{1,33},{65,97},{129,1... | collective-permute-start | bytes 1572872 | tf_op jit(solution)/shard_map/ppermute | solution.py:450
  52.6 9.7 %collective-permute-start.9 = (f32[8,128,128]{2,1,0:T(8,128)S(1)}, f32[8,128,128]{2,1,0:T(8,128)S(1)}, u32[]{:S(2)}, u32[]{:S(2)}) collective-permute-start(f32[8,128,128]{2,1,0:T(8,128)S(1)} %get-tuple-element.71.refs_2_), channel_id=1, source_target_pairs={{96,128},{97,129},{98,130},{99,131},{100,132},{101,133},{102,134},... | collective-permute-start | bytes 1572872 | tf_op jit(solution)/shard_map/ppermute | solution.py:471
  53.3 8.1 %collective-permute-start.6 = (f32[4,64,128]{2,1,0:T(8,128)S(1)}, f32[4,64,128]{2,1,0:T(8,128)S(1)}, u32[]{:S(2)}, u32[]{:S(2)}) collective-permute-start(f32[4,64,128]{2,1,0:T(8,128)S(1)} %get-tuple-element.78), channel_id=1, source_target_pairs={{0,1},{1,2},{2,3},{3,4},{4,5},{5,6},{6,7},{7,8},{8,9},{9,10},{10,1... | collective-permute-start | bytes 393224 | tf_op jit(solution)/shard_map/ppermute | solution.py:38
  53.4 8.0 %collective-permute-start.7 = (f32[4,64,128]{2,1,0:T(8,128)S(1)}, f32[4,64,128]{2,1,0:T(8,128)S(1)}, u32[]{:S(2)}, u32[]{:S(2)}) collective-permute-start(f32[4,64,128]{2,1,0:T(8,128)S(1)} %get-tuple-element.77), channel_id=1, source_target_pairs={{0,31},{1,0},{2,1},{3,2},{4,3},{5,4},{6,5},{7,6},{8,7},{9,8},{10,9... | collective-permute-start | bytes 393224 | tf_op jit(solution)/shard_map/ppermute | solution.py:38
  62.3 0.7 collective-permute-start.10
  63.0 8.1 %collective-permute-start.11 = (f32[4,64,128]{2,1,0:T(8,128)S(1)}, f32[4,64,128]{2,1,0:T(8,128)S(1)}, u32[]{:S(2)}, u32[]{:S(2)}) collective-permute-start(f32[4,64,128]{2,1,0:T(8,128)S(1)} %get-tuple-element.76), channel_id=1, source_target_pairs={{0,1},{1,2},{2,3},{3,4},{4,5},{5,6},{6,7},{7,8},{8,9},{9,10},{10,1... | collective-permute-start | bytes 393224 | tf_op jit(solution)/shard_map/ppermute | solution.py:38
  63.1 8.0 %collective-permute-start.12 = (f32[4,64,128]{2,1,0:T(8,128)S(1)}, f32[4,64,128]{2,1,0:T(8,128)S(1)}, u32[]{:S(2)}, u32[]{:S(2)}) collective-permute-start(f32[4,64,128]{2,1,0:T(8,128)S(1)} %get-tuple-element.75), channel_id=1, source_target_pairs={{0,31},{1,0},{2,1},{3,2},{4,3},{5,4},{6,5},{7,6},{8,7},{9,8},{10,9... | collective-permute-start | bytes 393224 | tf_op jit(solution)/shard_map/ppermute | solution.py:38
  72.2 17.6 %collective-permute-start.13 = (f32[5,64,128]{2,1,0:T(8,128)S(1)}, f32[5,64,128]{2,1,0:T(8,128)S(1)}, u32[]{:S(2)}, u32[]{:S(2)}) collective-permute-start(f32[5,64,128]{2,1,0:T(8,128)S(1)} %get-tuple-element.67), channel_id=1, source_target_pairs={{128,192},{160,224},{129,193},{161,225},{130,194},{162,226},{131,1... | collective-permute-start | bytes 491528 | tf_op jit(solution)/shard_map/ppermute | solution.py:46
  72.8 30.9 %collective-permute-start.16 = (f32[8,128,128]{2,1,0:T(8,128)S(1)}, f32[8,128,128]{2,1,0:T(8,128)S(1)}, u32[]{:S(2)}, u32[]{:S(2)}) collective-permute-start(f32[8,128,128]{2,1,0:T(8,128)S(1)} %get-tuple-element.71.refs_2_), channel_id=1, source_target_pairs={{32,64},{33,65},{34,66},{35,67},{36,68},{37,69},{38,70},{39,71},{4... | collective-permute-start | bytes 1572872 | tf_op jit(solution)/shard_map/ppermute | solution.py:467
  89.8 13.9 %collective-permute-start.14 = (f32[4,64,128]{2,1,0:T(8,128)S(1)}, f32[4,64,128]{2,1,0:T(8,128)S(1)}, u32[]{:S(2)}, u32[]{:S(2)}) collective-permute-start(f32[4,64,128]{2,1,0:T(8,128)S(1)} %get-tuple-element.74), channel_id=1, source_target_pairs={{0,1},{1,2},{2,3},{3,4},{4,5},{5,6},{6,7},{7,8},{8,9},{9,10},{10,1... | collective-permute-start | bytes 393224 | tf_op jit(solution)/shard_map/ppermute | solution.py:38
  89.9 13.8 %collective-permute-start.15 = (f32[4,64,128]{2,1,0:T(8,128)S(1)}, f32[4,64,128]{2,1,0:T(8,128)S(1)}, u32[]{:S(2)}, u32[]{:S(2)}) collective-permute-start(f32[4,64,128]{2,1,0:T(8,128)S(1)} %get-tuple-element.73), channel_id=1, source_target_pairs={{0,31},{1,0},{2,1},{3,2},{4,3},{5,4},{6,5},{7,6},{8,7},{9,8},{10,9... | collective-permute-start | bytes 393224 | tf_op jit(solution)/shard_map/ppermute | solution.py:38
